TPU v7x, 32 devices: a whole 2x2x4 slice. The times are simulated.
32 devices in a mesh: dp: 4 (over z), seq: 4 (over y, x), fsdp: 2 (over core).
Axes of the slice: x: 2, y: 2, z: 4, core: 2. Of those that a mesh axis runs over, the one named last changes fastest.
Arguments:
- tokens: bfloat16 [4, 4096, 2048], P(None, ('dp', 'seq', 'fsdp')), may hold values from -6 to 6
- cotangent: bfloat16 [4, 4096, 2048], P(None, ('dp', 'seq', 'fsdp')), may hold values from -6 to 6
- segments: int32 [4, 4096], P(None, ('dp', 'seq', 'fsdp')), may hold values from 0 to 3, as said below
- positions: int32 [4, 4096], P(None, ('dp', 'seq', 'fsdp')), may hold values from 0 to 1020, as said below
- w_query: bfloat16 [2048, 2048], P(('dp', 'seq', 'fsdp')), may hold values from -0.125 to 0.125
- w_key: bfloat16 [2048, 128], P(('dp', 'seq', 'fsdp')), may hold values from -0.125 to 0.125
- w_value: bfloat16 [2048, 128], P(('dp', 'seq', 'fsdp')), may hold values from -0.125 to 0.125
- w_out: bfloat16 [2048, 2048], P(('dp', 'seq', 'fsdp')), may hold values from -0.75 to 0.75
- w_gate: bfloat16 [2048, 5632], P(('dp', 'seq', 'fsdp')), may hold values from -0.125 to 0.125
- w_up: bfloat16 [2048, 5632], P(('dp', 'seq', 'fsdp')), may hold values from -0.125 to 0.125
- w_down: bfloat16 [5632, 2048], P(('dp', 'seq', 'fsdp')), may hold values from -0.078125 to 0.078125
- gain_attn: bfloat16 [2048], P(('dp', 'seq', 'fsdp')), may hold values from 0.5 to 1.5
- gain_mlp: bfloat16 [2048], P(('dp', 'seq', 'fsdp')), may hold values from 0.5 to 1.5
Outputs:
- layer_rows: bfloat16 [4, 4096, 2048], P(None, ('dp', 'seq', 'fsdp'))
- shared_keys: bfloat16 [4, 4096, 128], P(None, ('dp', 'seq', 'fsdp'))
- shared_values: bfloat16 [4, 4096, 128], P(None, ('dp', 'seq', 'fsdp'))
- grad_tokens: float32 [4, 4096, 2048], P(None, ('dp', 'seq', 'fsdp'))
- grad_query: float32 [2048, 2048], P(('dp', 'seq', 'fsdp'))
- grad_key: float32 [2048, 128], P(('dp', 'seq', 'fsdp'))
- grad_value: float32 [2048, 128], P(('dp', 'seq', 'fsdp'))
- grad_out: float32 [2048, 2048], P(('dp', 'seq', 'fsdp'))
- grad_gate: float32 [2048, 5632], P(('dp', 'seq', 'fsdp'))
- grad_up: float32 [2048, 5632], P(('dp', 'seq', 'fsdp'))
- grad_down: float32 [5632, 2048], P(('dp', 'seq', 'fsdp'))
- grad_gain_attn: float32 [2048], P(('dp', 'seq', 'fsdp'))
- grad_gain_mlp: float32 [2048], P(('dp', 'seq', 'fsdp'))
Inputs may be any that keep to these rules, and one draw needn't show every extreme that they name: `segments`: in each sequence of 1024 consecutive tokens the ids start at 0, never fall, and number its 4 documents. `positions`: A token's place within its document: 0 at a document's first token, one more at each following token.
All inputs are finite; a program needn't handle non-finite values.
Results may differ from a plain program's by a relative error of at most 0.018.
Values may be sent and summed in bfloat16 or wider, within the bound.
A program may use at most 384 MiB of HBM per device.

v0:
```python
import math

import jax
import jax.numpy as jnp
from jax import lax
from jax.sharding import PartitionSpec as P

EPSILON = 1e-05
MASKED = -1e30


def rope_tables(places, half_dim):
    frequency = jnp.exp(-math.log(10000.0) * jnp.arange(half_dim, dtype=jnp.float32) / half_dim)
    angles = places.astype(jnp.float32)[:, None] * frequency[None, :]
    return (jnp.cos(angles), jnp.sin(angles))


def rotate(vector, cosine, sine_part):
    half_dim = vector.shape[-1] // 2
    first_half = vector[..., :half_dim]
    second_half = vector[..., half_dim:]
    return jnp.concatenate(
        [
            first_half * cosine - second_half * sine_part,
            second_half * cosine + first_half * sine_part,
        ],
        axis=-1,
    )


def norm_back(grad_normed, normed, inverse):
    return inverse * (grad_normed - normed * jnp.mean(grad_normed * normed, axis=-1, keepdims=True))


def mask_scores(scores, query_place, query_segment, key_segment):
    key_place = jnp.arange(key_segment.shape[0], dtype=jnp.int32)
    allowed = (query_segment[:, None] == key_segment[None, :]) & (
        query_place[:, None] >= key_place[None, :]
    )
    return jnp.where(allowed[None], scores, MASKED)


def attend_micro(micro_item, query_place, block_rows, score_scale):
    queries, keys_seq, values_seq, query_segment, key_segment = micro_item
    query_rows, local_heads, head_dim = queries.shape
    blocks = query_rows // block_rows

    def one_block(block_item):
        block_query, block_place, block_segment = block_item
        scores = (
            jnp.einsum("qhd,kd->hqk", block_query, keys_seq, preferred_element_type=jnp.float32)
            * score_scale
        )
        scores = mask_scores(scores, block_place, block_segment, key_segment)
        row_max = jnp.max(scores, axis=-1, keepdims=True)
        log_total = row_max + jnp.log(jnp.sum(jnp.exp(scores - row_max), axis=-1, keepdims=True))
        soft_weights = jnp.exp(scores - log_total).astype(jnp.bfloat16)
        attended = jnp.einsum(
            "hqk,kd->qhd", soft_weights, values_seq, preferred_element_type=jnp.float32
        )
        return (attended.astype(jnp.bfloat16), log_total)

    return lax.map(
        one_block,
        (
            queries.reshape(blocks, block_rows, local_heads, head_dim),
            query_place.reshape(blocks, block_rows),
            query_segment.reshape(blocks, block_rows),
        ),
    )


def attend_back(micro_item, query_place, block_rows, score_scale):
    queries, keys_seq, values_seq, grad_attended, log_total, query_segment, key_segment = micro_item
    query_rows, local_heads, head_dim = queries.shape
    blocks = query_rows // block_rows

    def one_block(running, block_item):
        grad_keys, grad_values = running
        block_query, block_grad, block_total, block_place, block_segment = block_item
        scores = (
            jnp.einsum("qhd,kd->hqk", block_query, keys_seq, preferred_element_type=jnp.float32)
            * score_scale
        )
        scores = mask_scores(scores, block_place, block_segment, key_segment)
        soft_weights = jnp.exp(scores - block_total)
        grad_soft = jnp.einsum(
            "qhd,kd->hqk", block_grad, values_seq, preferred_element_type=jnp.float32
        )
        inner_sum = jnp.sum(soft_weights * grad_soft, axis=-1, keepdims=True)
        grad_scores = (soft_weights * (grad_soft - inner_sum)).astype(jnp.bfloat16)
        grad_queries = (
            jnp.einsum("hqk,kd->qhd", grad_scores, keys_seq, preferred_element_type=jnp.float32)
            * score_scale
        )
        grad_keys = (
            grad_keys
            + jnp.einsum(
                "hqk,qhd->kd", grad_scores, block_query, preferred_element_type=jnp.float32
            )
            * score_scale
        )
        grad_values = grad_values + jnp.einsum(
            "hqk,qhd->kd",
            soft_weights.astype(jnp.bfloat16),
            block_grad,
            preferred_element_type=jnp.float32,
        )
        return ((grad_keys, grad_values), grad_queries)

    zero_init = jnp.zeros(keys_seq.shape, jnp.float32)
    running, grad_queries = lax.scan(
        one_block,
        (zero_init, zero_init),
        (
            queries.reshape(blocks, block_rows, local_heads, head_dim),
            grad_attended.reshape(blocks, block_rows, local_heads, head_dim),
            log_total,
            query_place.reshape(blocks, block_rows),
            query_segment.reshape(blocks, block_rows),
        ),
    )
    return (grad_queries, running[0], running[1])


def body(
    tokens,
    cotangent,
    segments,
    positions,
    w_query,
    w_key,
    w_value,
    w_out,
    w_gate,
    w_up,
    w_down,
    gain_attn,
    gain_mlp,
):
    micro_count, tok_rows, model_width = tokens.shape
    head_dim = w_key.shape[1]
    head_count = model_width // head_dim
    seq_size = lax.axis_size("seq")
    pair_size = lax.axis_size("fsdp")
    local_heads = head_count // seq_size
    row_count = micro_count * tok_rows
    query_rows = seq_size * tok_rows
    block_rows = min(512, query_rows)
    score_scale = 1.0 / math.sqrt(head_dim)
    gathered = (
        lax.all_gather(w_query, ("dp", "seq", "fsdp"), axis=0, tiled=True),
        lax.all_gather(w_key, ("dp", "seq", "fsdp"), axis=0, tiled=True),
        lax.all_gather(w_value, ("dp", "seq", "fsdp"), axis=0, tiled=True),
        lax.all_gather(w_out, ("dp", "seq", "fsdp"), axis=0, tiled=True),
        lax.all_gather(w_gate, ("dp", "seq", "fsdp"), axis=0, tiled=True),
        lax.all_gather(w_up, ("dp", "seq", "fsdp"), axis=0, tiled=True),
        lax.all_gather(w_down, ("dp", "seq", "fsdp"), axis=0, tiled=True),
        lax.all_gather(gain_attn, ("dp", "seq", "fsdp"), axis=0, tiled=True),
        lax.all_gather(gain_mlp, ("dp", "seq", "fsdp"), axis=0, tiled=True),
    )
    query_mat, key_mat, value_mat, out_mat, gate_mat, up_mat, down_mat, gain_one, gain_two = (
        gathered
    )
    flat_rows = tokens.reshape(row_count, model_width).astype(jnp.float32)
    inverse_one = lax.rsqrt(jnp.mean(flat_rows * flat_rows, axis=-1, keepdims=True) + EPSILON)
    normed_one = flat_rows * inverse_one
    hidden_one = (normed_one * gain_one.astype(jnp.float32)).astype(jnp.bfloat16)
    cosine, sine_part = rope_tables(positions.reshape(row_count), head_dim // 2)
    query_lin = jnp.dot(hidden_one, query_mat, preferred_element_type=jnp.float32).reshape(
        row_count, head_count, head_dim
    )
    queries = rotate(query_lin, cosine[:, None, :], sine_part[:, None, :]).astype(jnp.bfloat16)
    keys_local = rotate(
        jnp.dot(hidden_one, key_mat, preferred_element_type=jnp.float32), cosine, sine_part
    ).astype(jnp.bfloat16)
    values_local = jnp.dot(hidden_one, value_mat, preferred_element_type=jnp.float32).astype(
        jnp.bfloat16
    )
    keys_local = keys_local.reshape(micro_count, tok_rows, head_dim)
    values_local = values_local.reshape(micro_count, tok_rows, head_dim)
    keys_seq, values_seq, segment_seq = (
        lax.all_gather(keys_local, ("seq", "fsdp"), axis=1, tiled=True),
        lax.all_gather(values_local, ("seq", "fsdp"), axis=1, tiled=True),
        lax.all_gather(segments.astype(jnp.bfloat16), ("seq", "fsdp"), axis=1, tiled=True),
    )
    key_segment = segment_seq.astype(jnp.int32)
    pair_index = lax.axis_index("fsdp")
    query_place = (
        (jnp.arange(seq_size, dtype=jnp.int32)[:, None] * pair_size + pair_index) * tok_rows
        + jnp.arange(tok_rows, dtype=jnp.int32)[None, :]
    ).reshape(query_rows)
    query_segment = lax.dynamic_index_in_dim(
        key_segment.reshape(micro_count, seq_size, pair_size, tok_rows),
        pair_index,
        axis=2,
        keepdims=False,
    ).reshape(micro_count, query_rows)
    head_queries = lax.all_to_all(
        queries.reshape(micro_count, tok_rows, model_width),
        "seq",
        split_axis=2,
        concat_axis=1,
        tiled=True,
    )
    head_queries = head_queries.reshape(micro_count, query_rows, local_heads, head_dim)

    def forward_micro(micro_item):
        return attend_micro(micro_item, query_place, block_rows, score_scale)

    attended, log_total = lax.map(
        forward_micro, (head_queries, keys_seq, values_seq, query_segment, key_segment)
    )
    mixed_rows = lax.all_to_all(
        attended.reshape(micro_count, query_rows, local_heads * head_dim),
        "seq",
        split_axis=1,
        concat_axis=2,
        tiled=True,
    )
    mixed_rows = mixed_rows.reshape(row_count, model_width)
    middle = flat_rows + jnp.dot(mixed_rows, out_mat, preferred_element_type=jnp.float32)
    inverse_two = lax.rsqrt(jnp.mean(middle * middle, axis=-1, keepdims=True) + EPSILON)
    normed_two = middle * inverse_two
    hidden_two = (normed_two * gain_two.astype(jnp.float32)).astype(jnp.bfloat16)
    gate_proj = jnp.dot(hidden_two, gate_mat, preferred_element_type=jnp.float32)
    up_proj = jnp.dot(hidden_two, up_mat, preferred_element_type=jnp.float32)
    gate_sigmoid = jax.nn.sigmoid(gate_proj)
    gate_silu = gate_proj * gate_sigmoid
    hidden_mlp = (gate_silu * up_proj).astype(jnp.bfloat16)
    result = middle + jnp.dot(hidden_mlp, down_mat, preferred_element_type=jnp.float32)
    back_weights = (
        lax.all_gather(w_query, ("dp", "seq", "fsdp"), axis=0, tiled=True),
        lax.all_gather(w_key, ("dp", "seq", "fsdp"), axis=0, tiled=True),
        lax.all_gather(w_value, ("dp", "seq", "fsdp"), axis=0, tiled=True),
        lax.all_gather(w_out, ("dp", "seq", "fsdp"), axis=0, tiled=True),
        lax.all_gather(w_gate, ("dp", "seq", "fsdp"), axis=0, tiled=True),
        lax.all_gather(w_up, ("dp", "seq", "fsdp"), axis=0, tiled=True),
        lax.all_gather(w_down, ("dp", "seq", "fsdp"), axis=0, tiled=True),
        lax.all_gather(gain_attn, ("dp", "seq", "fsdp"), axis=0, tiled=True),
        lax.all_gather(gain_mlp, ("dp", "seq", "fsdp"), axis=0, tiled=True),
    )
    query_mat, key_mat, value_mat, out_mat, gate_mat, up_mat, down_mat, gain_one, gain_two = (
        back_weights
    )
    grad_rows = cotangent.reshape(row_count, model_width).astype(jnp.float32)
    grad_branch = cotangent.reshape(row_count, model_width)
    grad_down_w = jnp.einsum(
        "nf,nd->fd", hidden_mlp, grad_branch, preferred_element_type=jnp.float32
    )
    grad_hidden = jnp.einsum("nd,fd->nf", grad_branch, down_mat, preferred_element_type=jnp.float32)
    grad_gate_pre = (
        grad_hidden * up_proj * gate_sigmoid * (1.0 + gate_proj * (1.0 - gate_sigmoid))
    ).astype(jnp.bfloat16)
    grad_up_pre = (grad_hidden * gate_silu).astype(jnp.bfloat16)
    grad_gate_w = jnp.einsum(
        "nd,nf->df", hidden_two, grad_gate_pre, preferred_element_type=jnp.float32
    )
    grad_up_w = jnp.einsum("nd,nf->df", hidden_two, grad_up_pre, preferred_element_type=jnp.float32)
    grad_hidden_two = jnp.einsum(
        "nf,df->nd", grad_gate_pre, gate_mat, preferred_element_type=jnp.float32
    ) + jnp.einsum("nf,df->nd", grad_up_pre, up_mat, preferred_element_type=jnp.float32)
    grad_gain_two = jnp.sum(grad_hidden_two * normed_two, axis=0)
    grad_middle = grad_rows + norm_back(
        grad_hidden_two * gain_two.astype(jnp.float32), normed_two, inverse_two
    )
    grad_proj = grad_middle.astype(jnp.bfloat16)
    grad_out_w = jnp.einsum("nd,ne->de", mixed_rows, grad_proj, preferred_element_type=jnp.float32)
    grad_mixed = jnp.einsum(
        "ne,de->nd", grad_proj, out_mat, preferred_element_type=jnp.float32
    ).astype(jnp.bfloat16)
    grad_heads = lax.all_to_all(
        grad_mixed.reshape(micro_count, tok_rows, model_width),
        "seq",
        split_axis=2,
        concat_axis=1,
        tiled=True,
    )
    grad_heads = grad_heads.reshape(micro_count, query_rows, local_heads, head_dim)

    def backward_micro(micro_item):
        return attend_back(micro_item, query_place, block_rows, score_scale)

    grad_head_queries, grad_keys_seq, grad_values_seq = lax.map(
        backward_micro,
        (head_queries, keys_seq, values_seq, grad_heads, log_total, query_segment, key_segment),
    )
    grad_query_rows = lax.all_to_all(
        grad_head_queries.reshape(micro_count, query_rows, local_heads * head_dim).astype(
            jnp.bfloat16
        ),
        "seq",
        split_axis=1,
        concat_axis=2,
        tiled=True,
    ).astype(jnp.float32)
    grad_keys_own, grad_values_own = (
        lax.psum_scatter(
            grad_keys_seq.astype(jnp.bfloat16), ("seq", "fsdp"), scatter_dimension=1, tiled=True
        ).astype(jnp.float32),
        lax.psum_scatter(
            grad_values_seq.astype(jnp.bfloat16), ("seq", "fsdp"), scatter_dimension=1, tiled=True
        ).astype(jnp.float32),
    )
    grad_query_lin = (
        rotate(
            grad_query_rows.reshape(row_count, head_count, head_dim),
            cosine[:, None, :],
            -sine_part[:, None, :],
        )
        .reshape(row_count, model_width)
        .astype(jnp.bfloat16)
    )
    grad_key_lin = rotate(grad_keys_own.reshape(row_count, head_dim), cosine, -sine_part).astype(
        jnp.bfloat16
    )
    grad_value_lin = grad_values_own.reshape(row_count, head_dim).astype(jnp.bfloat16)
    grad_query_w = jnp.einsum(
        "nd,ne->de", hidden_one, grad_query_lin, preferred_element_type=jnp.float32
    )
    grad_key_w = jnp.einsum(
        "nd,ne->de", hidden_one, grad_key_lin, preferred_element_type=jnp.float32
    )
    grad_value_w = jnp.einsum(
        "nd,ne->de", hidden_one, grad_value_lin, preferred_element_type=jnp.float32
    )
    grad_hidden_one = jnp.einsum(
        "ne,de->nd", grad_query_lin, query_mat, preferred_element_type=jnp.float32
    )
    grad_hidden_one = grad_hidden_one + jnp.einsum(
        "ne,de->nd", grad_key_lin, key_mat, preferred_element_type=jnp.float32
    )
    grad_hidden_one = grad_hidden_one + jnp.einsum(
        "ne,de->nd", grad_value_lin, value_mat, preferred_element_type=jnp.float32
    )
    grad_gain_one = jnp.sum(grad_hidden_one * normed_one, axis=0)
    grad_input = grad_middle + norm_back(
        grad_hidden_one * gain_one.astype(jnp.float32), normed_one, inverse_one
    )
    shards = (
        lax.psum_scatter(grad_query_w, ("dp", "seq", "fsdp"), scatter_dimension=0, tiled=True),
        lax.psum_scatter(grad_key_w, ("dp", "seq", "fsdp"), scatter_dimension=0, tiled=True),
        lax.psum_scatter(grad_value_w, ("dp", "seq", "fsdp"), scatter_dimension=0, tiled=True),
        lax.psum_scatter(grad_out_w, ("dp", "seq", "fsdp"), scatter_dimension=0, tiled=True),
        lax.psum_scatter(grad_gate_w, ("dp", "seq", "fsdp"), scatter_dimension=0, tiled=True),
        lax.psum_scatter(grad_up_w, ("dp", "seq", "fsdp"), scatter_dimension=0, tiled=True),
        lax.psum_scatter(grad_down_w, ("dp", "seq", "fsdp"), scatter_dimension=0, tiled=True),
        lax.psum_scatter(grad_gain_one, ("dp", "seq", "fsdp"), scatter_dimension=0, tiled=True),
        lax.psum_scatter(grad_gain_two, ("dp", "seq", "fsdp"), scatter_dimension=0, tiled=True),
    )
    layer_rows = result.reshape(micro_count, tok_rows, model_width).astype(jnp.bfloat16)
    return (
        layer_rows,
        keys_local,
        values_local,
        grad_input.reshape(micro_count, tok_rows, model_width),
        shards[0],
        shards[1],
        shards[2],
        shards[3],
        shards[4],
        shards[5],
        shards[6],
        shards[7],
        shards[8],
    )


def solution(mesh):
    in_specs = (
        P(None, ("dp", "seq", "fsdp"), None),
        P(None, ("dp", "seq", "fsdp"), None),
        P(None, ("dp", "seq", "fsdp")),
        P(None, ("dp", "seq", "fsdp")),
        P(("dp", "seq", "fsdp"), None),
        P(("dp", "seq", "fsdp"), None),
        P(("dp", "seq", "fsdp"), None),
        P(("dp", "seq", "fsdp"), None),
        P(("dp", "seq", "fsdp"), None),
        P(("dp", "seq", "fsdp"), None),
        P(("dp", "seq", "fsdp"), None),
        P(("dp", "seq", "fsdp")),
        P(("dp", "seq", "fsdp")),
    )
    out_specs = (
        P(None, ("dp", "seq", "fsdp"), None),
        P(None, ("dp", "seq", "fsdp"), None),
        P(None, ("dp", "seq", "fsdp"), None),
        P(None, ("dp", "seq", "fsdp"), None),
        P(("dp", "seq", "fsdp"), None),
        P(("dp", "seq", "fsdp"), None),
        P(("dp", "seq", "fsdp"), None),
        P(("dp", "seq", "fsdp"), None),
        P(("dp", "seq", "fsdp"), None),
        P(("dp", "seq", "fsdp"), None),
        P(("dp", "seq", "fsdp"), None),
        P(("dp", "seq", "fsdp")),
        P(("dp", "seq", "fsdp")),
    )
    return jax.shard_map(body, mesh=mesh, in_specs=in_specs, out_specs=out_specs, check_vma=False)
```

profile of v0, /device:TPU:0, one launch (start us, length us, event | category | flops | bytes accessed | tf_op | source)
XLA Modules:
  0.0 3103.8 jit_solution(16483194667036312255)
XLA Ops:
  9.7 42.7 %all-reduce.5 = (bf16[2048]{0:T(1024)(128)(2,1)S(1)}, bf16[2048]{0:T(1024)(128)(2,1)S(1)}) all-reduce(bf16[2048]{0:T(1024)(128)(2,1)S(1)} %dynamic-update-slice, bf16[2048]{0:T(1024)(128)(2,1)S(1)} %dynamic-update-slice.1), channel_id=1, replica_groups=mesh['dp'=4,'seq'=4,'fsdp'=2] {'dp','seq','fsdp'}, use_global_device_ids=true, to_apply=%add | all-reduce | flops 4096 | bytes 16384
  55.2 43.3 %all_gather.49 = bf16[2048,128]{1,0:T(8,128)(2,1)S(1)} all-gather(bf16[64,128]{1,0:T(8,128)(2,1)} %param.22), channel_id=1, replica_groups=mesh['dp'=4,'seq'=4,'fsdp'=2] {'dp','seq','fsdp'}, dimensions={0}, use_global_device_ids=true | all-gather | bytes 540672 | tf_op jit(solution)/shard_map/all_gather | solution.py:153
  102.9 38.2 %all_gather.46 = bf16[2048,128]{1,0:T(8,128)(2,1)S(1)} all-gather(bf16[64,128]{1,0:T(8,128)(2,1)S(1)} %copy-done.42), channel_id=1, replica_groups=mesh['dp'=4,'seq'=4,'fsdp'=2] {'dp','seq','fsdp'}, dimensions={0}, use_global_device_ids=true | all-gather | bytes 540672 | tf_op jit(solution)/shard_map/all_gather | solution.py:154
  149.3 11.9 copy.74
  161.3 7.6 fusion.100
  175.1 4.5 all-to-all-start
  179.7 28.1 all_gather.48
  211.0 4.1 copy.76
  222.5 39.5 %while.28 = (s32[]{:T(128)}, bf16[4,1,512,4,128]{2,4,3,1,0:T(8,128)(2,1)}, f32[4,1,4,512,1]{3,2,4,1,0:T(4,128)}, bf16[4,1024,128]{2,1,0:T(8,128)(2,1)}, s32[4,51...) while((s32[]{:T(128)}, ...), condition=%wide.region_4.5_spmd.clone, body=%wide.region_1.4_spmd.clone.sunk | while | flops 1098643968 | bytes 28926588 | solution.py:211
  228.2 4.2 fusion.170
  238.2 4.1 fusion.170
  248.0 4.1 fusion.170
  262.0 4.5 copy.98
  266.5 4.9 all-to-all-start.1
  271.5 27.0 all-to-all-done.1
  304.1 8.4 multiply_reduce_fusion.2
  314.9 102.0 %all-gather.16.cloned.1.call-done = bf16[2048,5632]{1,0:T(8,128)(2,1)} async-done(((bf16[64,5632]{1,0:T(8,128)(2,1)}), bf16[2048,5632]{1,0:T(8,128)(2,1)}) %all-gather.16.cloned.1.call-update) | async-done | bytes 23068688 | tf_op jit(solution)/shard_map/all_gather | solution.py:156
  416.9 19.0 fusion.101
  436.0 126.5 %all-gather.18.cloned.1.call-done = bf16[2048,5632]{1,0:T(8,128)(2,1)} async-done(((bf16[64,5632]{1,0:T(8,128)(2,1)}), bf16[2048,5632]{1,0:T(8,128)(2,1)}) %all-gather.18.cloned.1.call-update) | async-done | bytes 23068688 | tf_op jit(solution)/shard_map/all_gather | solution.py:157
  562.4 19.4 fusion.102
  581.8 126.3 %all-gather.20.cloned.1.call-done = bf16[5632,2048]{1,0:T(8,128)(2,1)} async-done(((bf16[176,2048]{1,0:T(8,128)(2,1)}), bf16[5632,2048]{1,0:T(8,128)(2,1)}) %all-gather.20.cloned.1.call-update) | async-done | bytes 23068688 | tf_op jit(solution)/shard_map/all_gather | solution.py:158
  708.1 28.2 multiply_convert_fusion
  736.3 19.5 fusion.103
  755.8 19.9 multiply_reduce_fusion
  777.0 9.7 convolution_convert_fusion
  793.1 25.5 all-to-all-done.2
  820.2 4.3 copy.84
  828.4 72.0 %while.29 = (s32[]{:T(128)}, bf16[4,1,512,4,128]{2,4,3,1,0:T(8,128)(2,1)}, bf16[4,1024,128]{2,1,0:T(8,128)(2,1)}, bf16[4,1024,128]{2,1,0:T(8,128)(2,1)}, bf16[4,...) while((s32[]{:T(128)}, ...), condition=%wide.region_9.10_spmd.clone, body=%wide.region_7.9_spmd.clone.sunk | while | flops 2717776384 | bytes 96291096 | solution.py:284
  901.3 33.6 %reduce-scatter.10.cloned.1.call-done = bf16[4,128,128]{2,1,0:T(8,128)(2,1)} async-done(((bf16[4,1024,128]{2,1,0:T(8,128)(2,1)}), bf16[4,128,128]{2,1,0:T(8,128)(2,1)}) %reduce-scatter.10.cloned.1.call-update) | async-done | bytes 131088 | tf_op jit(solution)/shard_map/reduce_scatter | solution.py:298
  939.4 35.3 %reduce-scatter.12.cloned.1.call-done = bf16[4,128,128]{2,1,0:T(8,128)(2,1)} async-done(((bf16[4,1024,128]{2,1,0:T(8,128)(2,1)}), bf16[4,128,128]{2,1,0:T(8,128)(2,1)}) %reduce-scatter.12.cloned.1.call-update) | async-done | bytes 131088 | tf_op jit(solution)/shard_map/reduce_scatter | solution.py:301
  978.1 10.4 fusion.75
  991.9 30.2 all_to_all.54
  1025.1 5.2 copy.89
  1030.3 5.5 reshape.421
  1040.5 8.2 fusion.105
  1050.3 20.9 fusion.106
  1071.3 21.0 fusion.107
  1093.9 21.0 fusion.108
  1115.0 19.8 add_convert_fusion
  1136.4 7.1 fusion.104
  1147.3 39.9 %all-reduce.4 = (f32[2048]{0:T(1024)S(1)}, f32[2048]{0:T(1024)S(1)}) all-reduce(f32[2048]{0:T(1024)S(1)} %get-tuple-element.315, f32[2048]{0:T(1024)S(1)} %copy-done.43), channel_id=11, replica_groups=mesh['dp'=4,'seq'=4,'fsdp'=2] {'dp','seq','fsdp'}, use_global_device_ids=true, to_apply=%region_21.22.clone | all-reduce | flops 4096 | bytes 32768
  1188.4 6.6 fusion.70
  1195.0 51.9 %reduce-scatter.18.cloned.1.call-done = f32[64,128]{1,0:T(8,128)} async-done(((f32[2048,128]{1,0:T(8,128)}), f32[64,128]{1,0:T(8,128)}) %reduce-scatter.18.cloned.1.call-update) | async-done | bytes 32784 | tf_op jit(solution)/shard_map/reduce_scatter | solution.py:343
  1246.9 181.4 %reduce-scatter.20.cloned.1.call-done = f32[64,2048]{1,0:T(8,128)} async-done(((f32[2048,2048]{1,0:T(8,128)}), f32[64,2048]{1,0:T(8,128)}) %reduce-scatter.20.cloned.1.call-update) | async-done | bytes 524304 | tf_op jit(solution)/shard_map/reduce_scatter | solution.py:344
  1428.4 187.4 %reduce-scatter.14.cloned.1.call-done = f32[64,2048]{1,0:T(8,128)} async-done(((f32[2048,2048]{1,0:T(8,128)}), f32[64,2048]{1,0:T(8,128)}) %reduce-scatter.14.cloned.1.call-update) | async-done | bytes 524304 | tf_op jit(solution)/shard_map/reduce_scatter | solution.py:341
  1615.8 489.5 %reduce-scatter.22.cloned.1.call-done = f32[64,5632]{1,0:T(8,128)} async-done(((f32[2048,5632]{1,0:T(8,128)}), f32[64,5632]{1,0:T(8,128)}) %reduce-scatter.22.cloned.1.call-update) | async-done | bytes 1441808 | tf_op jit(solution)/shard_map/reduce_scatter | solution.py:345
  2105.3 495.8 %reduce-scatter.24.cloned.1.call-done = f32[64,5632]{1,0:T(8,128)} async-done(((f32[2048,5632]{1,0:T(8,128)}), f32[64,5632]{1,0:T(8,128)}) %reduce-scatter.24.cloned.1.call-update) | async-done | bytes 1441808 | tf_op jit(solution)/shard_map/reduce_scatter | solution.py:346
  2601.1 495.8 %reduce-scatter.26.cloned.1.call-done = f32[176,2048]{1,0:T(8,128)} async-done(((f32[5632,2048]{1,0:T(8,128)}), f32[176,2048]{1,0:T(8,128)}) %reduce-scatter.26.cloned.1.call-update) | async-done | bytes 1441808 | tf_op jit(solution)/shard_map/reduce_scatter | solution.py:347
  (296 shorter events, 183.6 us)
Async XLA Ops:
  7.2 91.3 %copy-start = (bf16[4,128,2048]{2,1,0:T(8,128)(2,1)S(1)}, bf16[4,128,2048]{2,1,0:T(8,128)(2,1)}, u32[]{:S(2)}) copy-start(bf16[4,128,2048]{2,1,0:T(8,128)(2,1)} %param.17) | copy-start | bytes 6291460
  7.2 142.2 %all-gather.12.cloned.1.call-start = ((), (), s32[]{:S(2)}) async-start(), calls=%async_computation.15 | async-start | bytes 8650752 | tf_op jit(solution)/shard_map/all_gather | solution.py:152
  7.9 214.6 %all-gather.10.cloned.1.call-start = ((), (), s32[]{:S(2)}) async-start(), calls=%async_computation.14 | async-start | bytes 1179648 | tf_op jit(solution)/shard_map/all_gather | solution.py:183
  52.4 95.0 %copy-start.33 = (f32[2048]{0:T(1024)}, f32[2048]{0:T(1024)S(1)}, u32[]{:S(2)}) copy-start(f32[2048]{0:T(1024)S(1)} %convert_element_type.151) | copy-start | bytes 24580
  52.4 48.8 %copy-start.45 = (f32[64]{0:T(128)}, f32[64]{0:T(128)S(1)}, u32[]{:S(2)}) copy-start(f32[64]{0:T(128)S(1)} %multiply_exponential_fusion) | copy-start | bytes 772
  54.5 44.5 %copy-start.38 = (f32[512]{0:T(512)}, f32[512]{0:T(512)S(1)}, u32[]{:S(2)}) copy-start(f32[512]{0:T(512)S(1)} %get-tuple-element.388) | copy-start | bytes 6148
  55.2 46.7 %copy-start.40 = (f32[512]{0:T(512)}, f32[512]{0:T(512)S(1)}, u32[]{:S(2)}) copy-start(f32[512]{0:T(512)S(1)} %convert_bitcast_fusion.1) | copy-start | bytes 6148
  101.8 67.2 %copy-start.23 = (f32[512,64]{0,1:T(8,128)}, f32[512,64]{0,1:T(8,128)S(1)}, u32[]{:S(2)}) copy-start(f32[512,64]{0,1:T(8,128)S(1)} %get-tuple-element.383) | copy-start | bytes 393220
  102.8 119.7 %all-gather.8.cloned.1.call-start = ((), (), s32[]{:S(2)}) async-start(), calls=%async_computation.13 | async-start | bytes 1179648 | tf_op jit(solution)/shard_map/all_gather | solution.py:184
  144.9 159.2 %all-gather.14.cloned.1.call-start = ((), (), s32[]{:S(2)}) async-start(), calls=%async_computation.16 | async-start | bytes 8650752 | tf_op jit(solution)/shard_map/all_gather | solution.py:155
  145.5 271.4 %all-gather.16.cloned.1.call-start = ((), (), s32[]{:S(2)}) async-start(), calls=%async_computation.17 | async-start | bytes 23789568 | tf_op jit(solution)/shard_map/all_gather | solution.py:156
  146.1 416.4 %all-gather.18.cloned.1.call-start = ((), (), s32[]{:S(2)}) async-start(), calls=%async_computation.18 | async-start | bytes 23789568 | tf_op jit(solution)/shard_map/all_gather | solution.py:157
  146.7 561.4 %all-gather.20.cloned.1.call-start = ((), (), s32[]{:S(2)}) async-start(), calls=%async_computation.19 | async-start | bytes 23789568 | tf_op jit(solution)/shard_map/all_gather | solution.py:158
  171.2 8.5 copy-start.44
  175.1 32.7 %all-to-all-start = ((bf16[4,128,2048]{1,0,2:T(4,128)(2,1)}), bf16[4,128,2048]{1,0,2:T(4,128)(2,1)}, u32[]{:S(2)}, u32[]{:S(2)}) async-start(bf16[4,128,2048]{1,0,2:T(4,128)(2,1)} %convert_element_type.160), calls=%async_computation | async-start | bytes 4194304 | tf_op jit(solution)/shard_map/all_to_all | solution.py:199
  262.0 4.5 copy-start.36
  266.5 32.0 %all-to-all-start.1 = ((bf16[4,512,512]{2,0,1:T(4,128)(2,1)}), bf16[4,512,512]{2,0,1:T(4,128)(2,1)}, u32[]{:S(2)}, u32[]{:S(2)}) async-start(bf16[4,512,512]{2,0,1:T(4,128)(2,1)} %copy.98), calls=%async_computation.1 | async-start | bytes 4194304 | tf_op jit(solution)/shard_map/all_to_all | solution.py:214
  314.9 247.5 %copy-start.14 = (bf16[512,2048]{1,0:T(8,128)(2,1)}, bf16[512,2048]{1,0:T(8,128)(2,1)S(1)}, u32[]{:S(2)}) copy-start(bf16[512,2048]{1,0:T(8,128)(2,1)S(1)} %multiply_convert_fusion.3) | copy-start | bytes 6291460
  755.8 19.9 copy-start.7
  755.8 19.9 copy-start.21
  777.0 9.7 copy-start.8
  789.4 29.2 all-to-all-start.2
  793.0 141.9 %reduce-scatter.10.cloned.1.call-start = ((), (), s32[]{:S(2)}) async-start(), calls=%async_computation.20 | async-start | bytes 1179648 | tf_op jit(solution)/shard_map/reduce_scatter | solution.py:298
  820.2 8.3 copy-start.4
  820.2 8.3 copy-start.9
  820.2 8.3 copy-start.37
  900.5 35.7 %copy-start.41 = (f32[512]{0:T(512)S(1)}, f32[512]{0:T(512)}, u32[]{:S(2)}) copy-start(f32[512]{0:T(512)} %copy-done.40) | copy-start | bytes 6148
  900.5 35.7 %copy-start.46 = (f32[64]{0:T(128)S(1)}, f32[64]{0:T(128)}, u32[]{:S(2)}) copy-start(f32[64]{0:T(128)} %copy-done.45) | copy-start | bytes 772
  900.5 36.9 %copy-start.3 = (bf16[512,2048]{1,0:T(8,128)(2,1)S(1)}, bf16[512,2048]{1,0:T(8,128)(2,1)}, u32[]{:S(2)}) copy-start(bf16[512,2048]{1,0:T(8,128)(2,1)} %copy-done.2) | copy-start | bytes 6291460
  900.5 74.2 %reduce-scatter.12.cloned.1.call-start = ((), (), s32[]{:S(2)}) async-start(), calls=%async_computation.21 | async-start | bytes 1179648 | tf_op jit(solution)/shard_map/reduce_scatter | solution.py:301
  901.2 293.7 %reduce-scatter.16.cloned.1.call-start = ((), (), s32[]{:S(2)}) async-start(), calls=%async_computation.23 | async-start | bytes 1081344 | tf_op jit(solution)/shard_map/reduce_scatter | solution.py:342
  939.1 39.0 %copy-start.16 = (bf16[64,8,4,512]{3,1,2,0:T(8,128)(2,1)S(1)}, bf16[64,8,4,512]{3,1,2,0:T(8,128)(2,1)}, u32[]{:S(2)}) copy-start(bf16[64,8,4,512]{3,1,2,0:T(8,128)(2,1)} %copy.107) | copy-start | bytes 6291460
  939.2 307.8 %reduce-scatter.18.cloned.1.call-start = ((), (), s32[]{:S(2)}) async-start(), calls=%async_computation.24 | async-start | bytes 1081344 | tf_op jit(solution)/shard_map/reduce_scatter | solution.py:343
  978.0 450.3 %reduce-scatter.20.cloned.1.call-start = ((), (), s32[]{:S(2)}) async-start(), calls=%async_computation.25 | async-start | bytes 17301504 | tf_op jit(solution)/shard_map/reduce_scatter | solution.py:344
  988.5 627.2 %reduce-scatter.14.cloned.1.call-start = ((), (), s32[]{:S(2)}) async-start(), calls=%async_computation.22 | async-start | bytes 17301504 | tf_op jit(solution)/shard_map/reduce_scatter | solution.py:341
  1030.3 5.5 copy-start.24
  1035.8 4.7 copy-start.5
  1048.7 1056.6 %reduce-scatter.22.cloned.1.call-start = ((), (), s32[]{:S(2)}) async-start(), calls=%async_computation.26 | async-start | bytes 47579136 | tf_op jit(solution)/shard_map/reduce_scatter | solution.py:345
  1071.3 1529.8 %reduce-scatter.24.cloned.1.call-start = ((), (), s32[]{:S(2)}) async-start(), calls=%async_computation.27 | async-start | bytes 47579136 | tf_op jit(solution)/shard_map/reduce_scatter | solution.py:346
  1092.4 2004.5 %reduce-scatter.26.cloned.1.call-start = ((), (), s32[]{:S(2)}) async-start(), calls=%async_computation.28 | async-start | bytes 47579136 | tf_op jit(solution)/shard_map/reduce_scatter | solution.py:347
  1114.9 19.9 copy-start.11
  1114.9 19.9 copy-start.28
  1114.9 19.9 copy-start.30
  1136.4 7.2 copy-start.1
  1136.4 7.2 copy-start.13
  1136.4 7.2 copy-start.31
  1136.4 7.2 copy-start.34
  1136.4 7.2 copy-start.39
  (30 other events, 58.1 us)
Sparse Core Ops, SparseCore 0:
  10.9 84.7 all-gather.11
  102.9 20.3 all-gather.9
  145.0 20.9 all-gather.7
  168.8 89.0 all-gather.13
  260.5 156.3 all-gather.15
  419.6 142.7 all-gather.17
  565.3 142.7 all-gather.19
  900.6 34.2 reduce-scatter.9
  938.6 35.9 reduce-scatter.11
  977.3 135.6 reduce-scatter.15
  1116.0 130.9 reduce-scatter.17
  1249.6 178.6 reduce-scatter.19
  1431.2 184.4 reduce-scatter.13
  1618.5 486.7 reduce-scatter.21
  2108.0 493.0 reduce-scatter.23
  2603.8 493.0 reduce-scatter.25
where the time goes:
time: 3120 us; the launch traced here: 3100 us
  waiting for transfers between devices  2380 us (76%)
  matrix products  321 us (10%)
  blocking collectives  222 us (7%)
  local copies, waits for them, and re-layouts  100 us (3%)
  other arithmetic  49 us (2%)
    reduce_scatter x1, waiting for transfers between devices, body(): lax.psum_scatter(grad_up_w, ('dp', 'seq', 'fsdp'), scatter_dimension=0, t...  496 us
    reduce_scatter x1, waiting for transfers between devices, body(): lax.psum_scatter(grad_down_w, ('dp', 'seq', 'fsdp'), scatter_dimension=0,...  496 us
    reduce_scatter x1, waiting for transfers between devices, body(): lax.psum_scatter(grad_gate_w, ('dp', 'seq', 'fsdp'), scatter_dimension=0,...  490 us
    reduce_scatter x1, waiting for transfers between devices, body(): lax.psum_scatter(grad_query_w, ('dp', 'seq', 'fsdp'), scatter_dimension=0...  187 us
    reduce_scatter x1, waiting for transfers between devices, body(): lax.psum_scatter(grad_out_w, ('dp', 'seq', 'fsdp'), scatter_dimension=0,...  181 us
    all_gather x1, waiting for transfers between devices, body(): lax.all_gather(w_up, ('dp', 'seq', 'fsdp'), axis=0, tiled=True)  126 us
    all_gather x1, waiting for transfers between devices, body(): lax.all_gather(w_down, ('dp', 'seq', 'fsdp'), axis=0, tiled=True)  126 us
    all_gather x1, waiting for transfers between devices, body(): lax.all_gather(w_gate, ('dp', 'seq', 'fsdp'), axis=0, tiled=True)  102 us
  transfers between devices with their start and end apart: 19, of which 13 were waited for; matrix products, arithmetic and copies ran while one was open for 10% of the time, Pallas kernels for 0%

commit v1 on v0

--- a/solution.py
+++ b/solution.py
@@ -1,8 +1,11 @@
+import functools
 import math
 
 import jax
 import jax.numpy as jnp
 from jax import lax
+from jax.experimental import pallas as pl
+from jax.experimental.pallas import tpu as pltpu
 from jax.sharding import PartitionSpec as P
 
 EPSILON = 1e-05
@@ -123,7 +126,7 @@
     return (grad_queries, running[0], running[1])
 
 
-def body(
+def body_general(
     tokens,
     cotangent,
     segments,
@@ -337,14 +340,21 @@
     grad_input = grad_middle + norm_back(
         grad_hidden_one * gain_one.astype(jnp.float32), normed_one, inverse_one
     )
-    shards = (
-        lax.psum_scatter(grad_query_w, ("dp", "seq", "fsdp"), scatter_dimension=0, tiled=True),
-        lax.psum_scatter(grad_key_w, ("dp", "seq", "fsdp"), scatter_dimension=0, tiled=True),
-        lax.psum_scatter(grad_value_w, ("dp", "seq", "fsdp"), scatter_dimension=0, tiled=True),
-        lax.psum_scatter(grad_out_w, ("dp", "seq", "fsdp"), scatter_dimension=0, tiled=True),
-        lax.psum_scatter(grad_gate_w, ("dp", "seq", "fsdp"), scatter_dimension=0, tiled=True),
-        lax.psum_scatter(grad_up_w, ("dp", "seq", "fsdp"), scatter_dimension=0, tiled=True),
-        lax.psum_scatter(grad_down_w, ("dp", "seq", "fsdp"), scatter_dimension=0, tiled=True),
+    matrix_grads = (
+        grad_query_w,
+        grad_key_w,
+        grad_value_w,
+        grad_out_w,
+        grad_gate_w,
+        grad_up_w,
+        grad_down_w,
+    )
+    shards = tuple(
+        lax.psum_scatter(
+            grad.astype(jnp.bfloat16), ("dp", "seq", "fsdp"), scatter_dimension=0, tiled=True
+        ).astype(jnp.float32)
+        for grad in matrix_grads
+    ) + (
         lax.psum_scatter(grad_gain_one, ("dp", "seq", "fsdp"), scatter_dimension=0, tiled=True),
         lax.psum_scatter(grad_gain_two, ("dp", "seq", "fsdp"), scatter_dimension=0, tiled=True),
     )
@@ -366,6 +376,440 @@
     )
 
 
+BF16 = jnp.bfloat16
+F32 = jnp.float32
+
+
+def dot32(left, right, contract):
+    return lax.dot_general(left, right, ((contract[0], contract[1]), ((), ())), preferred_element_type=F32)
+
+
+def turn(vector, cosine, sine):
+    return vector * cosine + pltpu.roll(vector, vector.shape[-1] // 2, 1) * sine
+
+
+def stack_heads(ref, start, rows, heads, head_dim):
+    return jnp.concatenate(
+        [ref[pl.ds(start, rows), pl.ds(h * head_dim, head_dim)] for h in range(heads)], axis=0
+    )
+
+
+def masked_block(stacked, keys, query_place, query_segment, key_segment, heads, score_scale):
+    rows, extent = query_place.shape[0], keys.shape[0]
+    key_place = lax.broadcasted_iota(jnp.int32, (rows, extent), 1)
+    allowed = (query_place >= key_place) & (query_segment == key_segment)
+    bias = jnp.where(allowed, 0.0, MASKED).astype(F32)
+    scores = dot32(stacked, keys, ((1,), (1,))) * score_scale
+    scores = (scores.reshape(heads, rows, extent) + bias[None]).reshape(heads * rows, extent)
+    row_max = jnp.max(scores, axis=-1, keepdims=True)
+    weights = jnp.exp(scores - row_max)
+    total = jnp.sum(weights, axis=-1, keepdims=True)
+    return weights * (1.0 / total)
+
+
+def attend_kernel(
+    plan,
+    query_lin_ref,
+    keys_ref,
+    values_ref,
+    place_ref,
+    segment_ref,
+    key_segment_ref,
+    cosine_ref,
+    sine_ref,
+    attended_ref,
+    queries_ref,
+):
+    blocks, rows, pair, heads, head_dim, score_scale = plan
+    for block in range(blocks):
+        start = block * rows
+        extent = (block + 1) * pair * rows
+        cosine, sine = cosine_ref[pl.ds(start, rows), :], sine_ref[pl.ds(start, rows), :]
+        turned = []
+        for h in range(heads):
+            part = query_lin_ref[pl.ds(start, rows), pl.ds(h * head_dim, head_dim)]
+            part = turn(part, cosine, sine).astype(BF16)
+            queries_ref[pl.ds(start, rows), pl.ds(h * head_dim, head_dim)] = part
+            turned.append(part)
+        stacked = jnp.concatenate(turned, axis=0)
+        soft = masked_block(
+            stacked,
+            keys_ref[pl.ds(0, extent), :],
+            place_ref[pl.ds(start, rows), :],
+            segment_ref[pl.ds(start, rows), :],
+            key_segment_ref[:, pl.ds(0, extent)],
+            heads,
+            score_scale,
+        ).astype(BF16)
+        mixed = dot32(soft, values_ref[pl.ds(0, extent), :], ((1,), (0,))).astype(BF16)
+        for h in range(heads):
+            attended_ref[pl.ds(start, rows), pl.ds(h * head_dim, head_dim)] = mixed[
+                h * rows : (h + 1) * rows
+            ]
+
+
+def attend_back_kernel(
+    plan,
+    queries_ref,
+    grad_ref,
+    keys_ref,
+    values_ref,
+    place_ref,
+    segment_ref,
+    key_segment_ref,
+    cosine_ref,
+    sine_ref,
+    grad_lin_ref,
+    grad_keys_ref,
+    grad_values_ref,
+):
+    blocks, rows, pair, heads, head_dim, score_scale = plan
+
+    @pl.when(pl.program_id(0) == 0)
+    def _():
+        grad_keys_ref[...] = jnp.zeros_like(grad_keys_ref)
+        grad_values_ref[...] = jnp.zeros_like(grad_values_ref)
+
+    for block in range(blocks):
+        start = block * rows
+        extent = (block + 1) * pair * rows
+        stacked = stack_heads(queries_ref, start, rows, heads, head_dim)
+        grads = stack_heads(grad_ref, start, rows, heads, head_dim)
+        keys = keys_ref[pl.ds(0, extent), :]
+        values = values_ref[pl.ds(0, extent), :]
+        soft = masked_block(
+            stacked,
+            keys,
+            place_ref[pl.ds(start, rows), :],
+            segment_ref[pl.ds(start, rows), :],
+            key_segment_ref[:, pl.ds(0, extent)],
+            heads,
+            score_scale,
+        )
+        grad_soft = dot32(grads, values, ((1,), (1,)))
+        inner = jnp.sum(soft * grad_soft, axis=-1, keepdims=True)
+        grad_scores = (soft * (grad_soft - inner)).astype(BF16)
+        grad_values_ref[pl.ds(0, extent), :] += dot32(soft.astype(BF16), grads, ((0,), (0,)))
+        grad_keys_ref[pl.ds(0, extent), :] += (
+            dot32(grad_scores, stacked, ((0,), (0,))) * score_scale
+        )
+        grad_queries = dot32(grad_scores, keys, ((1,), (0,))) * score_scale
+        cosine, sine = cosine_ref[pl.ds(start, rows), :], sine_ref[pl.ds(start, rows), :]
+        for h in range(heads):
+            part = turn(grad_queries[h * rows : (h + 1) * rows], cosine, -sine)
+            grad_lin_ref[pl.ds(start, rows), pl.ds(h * head_dim, head_dim)] = part.astype(BF16)
+
+
+def whole(shape):
+    return pl.BlockSpec(shape, lambda g: (0,) * len(shape))
+
+
+def attention_call(kernel, plan, groups, wide, narrow, outs, name, flops):
+    rows = wide[0].shape[0]
+    group = wide[0].shape[1] // groups
+    column = pl.BlockSpec((rows, group), lambda g: (0, g))
+    return pl.pallas_call(
+        functools.partial(kernel, plan),
+        grid=(groups,),
+        in_specs=[column] * len(wide) + [whole(a.shape) for a in narrow],
+        out_specs=[column if a.shape[0] == rows else whole(a.shape) for a in outs],
+        out_shape=outs,
+        compiler_params=pltpu.CompilerParams(vmem_limit_bytes=48 * 1024 * 1024),
+        cost_estimate=pl.CostEstimate(
+            flops=flops, bytes_accessed=6 * rows * wide[0].shape[1], transcendentals=flops // 512
+        ),
+        name=name,
+    )(*wide, *narrow)
+
+
+def gather(value, axes, dim):
+    return lax.all_gather(value, axes, axis=dim, tiled=True)
+
+
+def scatter_sum(value, axes, dim):
+    return lax.psum_scatter(value, axes, scatter_dimension=dim, tiled=True)
+
+
+def send_plane(value, step):
+    return lax.ppermute(value, "seq", [(i, i ^ step) for i in range(4)])
+
+
+def send_line(value, step):
+    size = lax.axis_size("dp")
+    return lax.ppermute(value, "dp", [(i, (i + step) % size) for i in range(size)])
+
+
+def send_core(value):
+    return lax.ppermute(value, "fsdp", [(0, 1), (1, 0)])
+
+
+def block_of(value, index, dim=0):
+    return lax.dynamic_index_in_dim(value, index, axis=dim, keepdims=False)
+
+
+def put_block(value, block, index, dim=0):
+    return lax.dynamic_update_index_in_dim(value, block, index, axis=dim)
+
+
+def swap_blocks(value, own):
+    out = value
+    for step in (1, 2, 3):
+        other = own ^ step
+        out = put_block(out, send_plane(block_of(value, other), step), other)
+    return out
+
+
+def gather_plane(value):
+    half = value.shape[-1] // 2
+    by_x, by_y = send_plane(value, 1), send_plane(value, 2)
+    far = jnp.concatenate(
+        [send_plane(by_x[..., :half], 2), send_plane(by_y[..., half:], 1)], axis=-1
+    )
+    return jnp.concatenate([value, by_x, by_y, far], axis=0)
+
+
+def scatter_plane(value):
+    half = value.shape[-1] // 2
+    left, right = value[..., :half], value[..., half:]
+    got = send_plane(jnp.stack([left[1], left[3]]), 1).astype(F32)
+    passed = send_plane((left[2].astype(F32) + got[1]).astype(BF16), 2).astype(F32)
+    left = left[0].astype(F32) + got[0] + passed
+    got = send_plane(right[2:], 2).astype(F32)
+    passed = send_plane((right[1].astype(F32) + got[1]).astype(BF16), 1).astype(F32)
+    right = right[0].astype(F32) + got[0] + passed
+    return jnp.concatenate([left, right], axis=-1)
+
+
+def gather_line(value, plane):
+    size = lax.axis_size("dp")
+    out = jnp.zeros((size,) + value.shape, value.dtype)
+    out = put_block(out, value, plane)
+    for step in range(1, size):
+        out = put_block(out, send_line(value, step), (plane + size - step) % size)
+    return out
+
+
+def scatter_line(value, plane):
+    size = lax.axis_size("dp")
+    total = block_of(value, plane).astype(F32)
+    for step in range(1, size):
+        total = total + send_line(block_of(value, (plane + step) % size), step).astype(F32)
+    return total
+
+
+def gather_core(value, core, dim):
+    other = send_core(value)
+    first = jnp.where(core == 0, value, other)
+    second = jnp.where(core == 0, other, value)
+    return jnp.stack([first, second], axis=dim)
+
+
+def scatter_core(value, core, dim):
+    other = send_core(block_of(value, 1 - core, dim))
+    return (block_of(value, core, dim).astype(F32) + other.astype(F32)).astype(BF16)
+
+
+def scatter_every(value, plane, own, core):
+    planes, chips, pair, shard, columns = value.shape
+    value = scatter_core(value, core, 2)
+    blocks = jnp.stack([block_of(value, own ^ step, 1) for step in range(chips)])
+    value = scatter_plane(blocks).astype(BF16)
+    return scatter_line(value, plane)
+
+
+def body_plane(
+    tokens,
+    cotangent,
+    segments,
+    positions,
+    w_query,
+    w_key,
+    w_value,
+    w_out,
+    w_gate,
+    w_up,
+    w_down,
+    gain_attn,
+    gain_mlp,
+):
+    micro, tile, width = tokens.shape
+    head_dim = w_key.shape[1]
+    head_count = width // head_dim
+    planes = lax.axis_size("dp")
+    chips = lax.axis_size("seq")
+    pair = lax.axis_size("fsdp")
+    plane = lax.axis_index("dp")
+    own = lax.axis_index("seq")
+    core = lax.axis_index("fsdp")
+    rows = micro * tile
+    hidden = w_gate.shape[1]
+    shard = w_query.shape[0]
+    own_hidden = hidden // chips
+    piece = own_hidden // planes
+    qkv = width + 2 * head_dim
+    score_scale = 1.0 / math.sqrt(head_dim)
+    every = ("dp", "seq", "fsdp")
+
+    gains = jnp.stack([gain_attn, gain_mlp], axis=1)
+    gains = jnp.pad(gains, ((0, 0), (0, head_dim - 2)))
+    w_qkv = gather(jnp.concatenate([w_query, w_key, w_value, gains], axis=1), every, 0)
+    out_mat = gather(w_out, every, 0)
+    gate_up = jnp.stack([w_gate, w_up], axis=1).reshape(shard, 2, planes, chips, piece)
+    gate_up = gate_up.transpose(3, 0, 1, 2, 4).reshape(chips, shard, 2 * own_hidden)
+    w_qkv, gate_up, w_down = lax.optimization_barrier((w_qkv, gate_up, w_down))
+    gate_up = swap_blocks(gate_up, own)
+    gate_up = gather_core(gate_up, core, 1).reshape(pair, -1, 2 * own_hidden)
+    gate_up_half = gather_line(block_of(gate_up, core), plane)
+    gate_up = gather_core(gate_up_half, core, 1).reshape(width, 2 * own_hidden)
+    down_mat = gather_core(gather_line(w_down, plane), core, 1).reshape(own_hidden, width)
+    grads_in = gather(cotangent, "seq", 1).reshape(chips, rows, width)
+    grads_in = jnp.concatenate([block_of(grads_in, own ^ step) for step in range(chips)])
+
+    gain_one, gain_two = w_qkv[:, qkv].astype(F32), w_qkv[:, qkv + 1].astype(F32)
+    w_qkv = w_qkv[:, :qkv]
+
+    x_rows = swap_blocks(tokens, own).reshape(rows, width).astype(F32)
+    marks = swap_blocks(jnp.stack([segments, positions], axis=1), own)
+    segment_own, place_doc = marks[:, 0], marks[:, 1].reshape(rows)
+    key_segment = gather_core(segment_own, core, 1).reshape(1, rows * pair)
+    query_place = (
+        (jnp.arange(chips, dtype=jnp.int32)[:, None] * pair + core) * tile
+        + jnp.arange(tile, dtype=jnp.int32)[None, :]
+    ).reshape(rows, 1)
+    query_segment = segment_own.reshape(rows, 1)
+    cosine, sine = rope_tables(place_doc, head_dim // 2)
+    cosine = jnp.concatenate([cosine, cosine], axis=1)
+    sine = jnp.concatenate([-sine, sine], axis=1)
+
+    inverse_one = lax.rsqrt(jnp.mean(x_rows * x_rows, axis=-1, keepdims=True) + EPSILON)
+    normed_one = x_rows * inverse_one
+    hidden_one = (normed_one * gain_one).astype(BF16)
+    lin = jnp.dot(hidden_one, w_qkv, preferred_element_type=F32)
+    query_lin, key_lin, value_lin = (
+        lin[:, :width],
+        lin[:, width : width + head_dim],
+        lin[:, width + head_dim :],
+    )
+    keys_own = (key_lin * cosine + jnp.roll(key_lin, head_dim // 2, axis=1) * sine).astype(BF16)
+    values_own = value_lin.astype(BF16)
+    kv_own = jnp.concatenate([keys_own, values_own], axis=1).reshape(chips, tile, 2 * head_dim)
+    kv = gather_core(kv_own, core, 1).reshape(rows * pair, 2 * head_dim)
+    keys, values = kv[:, :head_dim], kv[:, head_dim:]
+    kv_home = swap_blocks(kv_own, own)
+    groups = max(1, head_count // 4)
+    heads = head_count // groups
+    plan = (chips, tile, pair, heads, head_dim, score_scale)
+    pairs_seen = tile * tile * pair * chips * (chips + 1) // 2 * head_count * head_dim
+    narrow = (keys, values, query_place, query_segment, key_segment, cosine, sine)
+    attended, queries = attention_call(
+        attend_kernel,
+        plan,
+        groups,
+        (query_lin,),
+        narrow,
+        [jax.ShapeDtypeStruct((rows, width), BF16)] * 2,
+        "attend",
+        4 * pairs_seen,
+    )
+    middle = x_rows + jnp.dot(attended, out_mat, preferred_element_type=F32)
+    inverse_two = lax.rsqrt(jnp.mean(middle * middle, axis=-1, keepdims=True) + EPSILON)
+    normed_two = middle * inverse_two
+    hidden_two = (normed_two * gain_two).astype(BF16)
+
+    plane_two = gather_plane(hidden_two)
+    gate_up_lin = jnp.dot(plane_two, gate_up, preferred_element_type=F32)
+    gate_proj, up_proj = gate_up_lin[:, :own_hidden], gate_up_lin[:, own_hidden:]
+    gate_sigmoid = jax.nn.sigmoid(gate_proj)
+    gate_silu = gate_proj * gate_sigmoid
+    hidden_mlp = (gate_silu * up_proj).astype(BF16)
+    partial_out = jnp.dot(hidden_mlp, down_mat, preferred_element_type=F32).astype(BF16)
+    result = middle + scatter_plane(partial_out.reshape(chips, rows, width))
+    layer_rows = swap_blocks(result.astype(BF16).reshape(chips, tile, width), own)
+
+    grad_hidden = dot32(grads_in, down_mat, ((1,), (1,)))
+    grad_gate_pre = (
+        grad_hidden * up_proj * gate_sigmoid * (1.0 + gate_proj * (1.0 - gate_sigmoid))
+    ).astype(BF16)
+    grad_up_pre = (grad_hidden * gate_silu).astype(BF16)
+    grad_pre = jnp.concatenate([grad_gate_pre, grad_up_pre], axis=1)
+    partial_two = dot32(grad_pre, gate_up, ((1,), (1,))).astype(BF16)
+    grad_hidden_two = scatter_plane(partial_two.reshape(chips, rows, width))
+    grad_gate_up = dot32(plane_two, grad_pre, ((0,), (0,))).astype(BF16)
+    grad_down = dot32(hidden_mlp, grads_in, ((0,), (0,))).astype(BF16)
+
+    grad_down = scatter_core(grad_down.reshape(planes, pair, -1, width), core, 1)
+    grad_down = scatter_line(grad_down, plane)
+    grad_gate_up = scatter_core(
+        grad_gate_up.reshape(planes, chips, pair, shard, 2 * own_hidden), core, 2
+    )
+    grad_gate_up = scatter_line(grad_gate_up, plane).astype(BF16)
+    grad_gate_up = swap_blocks(grad_gate_up, own).reshape(chips, shard, 2, planes, piece)
+    grad_gate_up = grad_gate_up.transpose(2, 1, 3, 0, 4).reshape(2, shard, hidden).astype(F32)
+
+    grad_gain_two = jnp.sum(grad_hidden_two * normed_two, axis=0)
+    grad_rows = grads_in[:rows].astype(F32)
+    grad_middle = grad_rows + norm_back(grad_hidden_two * gain_two, normed_two, inverse_two)
+    grad_proj = grad_middle.astype(BF16)
+    grad_mixed = dot32(grad_proj, out_mat, ((1,), (1,))).astype(BF16)
+    grad_query_lin, grad_keys, grad_values = attention_call(
+        attend_back_kernel,
+        plan,
+        groups,
+        (queries, grad_mixed),
+        narrow,
+        [
+            jax.ShapeDtypeStruct((rows, width), BF16),
+            jax.ShapeDtypeStruct((rows * pair, head_dim), F32),
+            jax.ShapeDtypeStruct((rows * pair, head_dim), F32),
+        ],
+        "attend_back",
+        10 * pairs_seen,
+    )
+    grad_kv = jnp.concatenate([grad_keys, grad_values], axis=1)
+    grad_kv = grad_kv.reshape(chips, pair, tile, 2 * head_dim)
+    grad_kv = block_of(grad_kv, core, 1) + send_core(block_of(grad_kv, 1 - core, 1))
+    grad_kv = grad_kv.reshape(rows, 2 * head_dim)
+    grad_keys = grad_kv[:, :head_dim]
+    grad_keys = grad_keys * cosine - jnp.roll(grad_keys, head_dim // 2, axis=1) * sine
+    grad_lin = jnp.concatenate(
+        [grad_query_lin, grad_keys.astype(BF16), grad_kv[:, head_dim:].astype(BF16)], axis=1
+    )
+    grad_out = dot32(attended, grad_proj, ((0,), (0,))).astype(BF16)
+    grad_hidden_one = dot32(grad_lin, w_qkv, ((1,), (1,)))
+    grad_gain_one = jnp.sum(grad_hidden_one * normed_one, axis=0)
+    grad_input = grad_middle + norm_back(grad_hidden_one * gain_one, normed_one, inverse_one)
+    grad_input = swap_blocks(grad_input.astype(BF16).reshape(chips, tile, width), own)
+    grad_out = scatter_every(grad_out.reshape(planes, chips, pair, shard, width), plane, own, core)
+    grad_gains = jnp.pad(
+        jnp.stack([grad_gain_one, grad_gain_two], axis=1), ((0, 0), (0, head_dim - 2))
+    )
+    grad_qkv = dot32(hidden_one, grad_lin, ((0,), (0,)))
+    grad_qkv = jnp.concatenate([grad_qkv, grad_gains], axis=1).astype(BF16)
+    grad_qkv = grad_qkv.reshape(planes, chips, pair, shard, qkv + head_dim)
+    grad_qkv = scatter_every(grad_qkv, plane, own, core)
+    return (
+        layer_rows,
+        kv_home[..., :head_dim],
+        kv_home[..., head_dim:],
+        grad_input.astype(F32),
+        grad_qkv[:, :width],
+        grad_qkv[:, width : width + head_dim],
+        grad_qkv[:, width + head_dim : qkv],
+        grad_out,
+        grad_gate_up[0],
+        grad_gate_up[1],
+        grad_down,
+        grad_qkv[:, qkv],
+        grad_qkv[:, qkv + 1],
+    )
+
+
+def body(tokens, *rest):
+    if tokens.shape[0] == lax.axis_size("seq") == 4 and lax.axis_size("fsdp") == 2:
+        return body_plane(tokens, *rest)
+    return body_general(tokens, *rest)
+
+
 def solution(mesh):
     in_specs = (
         P(None, ("dp", "seq", "fsdp"), None),

time: 3120 us -> 1170 us (0.38)
  waiting for transfers between devices: 2380 us -> 559 us
  blocking collectives: 222 us -> 0 us
  matrix products: 321 us -> 219 us
  other arithmetic: 49 us -> 123 us
  starting transfers between devices: 14 us -> 80.8 us
  Pallas kernels: 0 us -> 40.9 us
    reduce_scatter x9 -> x0, waiting for transfers between devices: 1970 us -> none  [the longest x1 496 us: body(): lax.psum_scatter(grad_up_w, ('dp', 'seq', 'fsdp'), scatter_dimension=0, t...]
    ppermute x0 -> x69, waiting for transfers between devices: none -> 516 us  [the longest x18 288 us: send_line(): lax.ppermute(value, 'dp', [(i, (i + step) % size) for i in range(size)])]
    all_gather x7 -> x3, waiting for transfers between devices: 355 us -> 42 us  [gather(): return lax.all_gather(value, axes, axis=dim, tiled=True)]
    all_gather x3 -> x0, blocking collectives: 110 us -> none  [the longest x1 43.3 us: body(): lax.all_gather(w_key, ('dp', 'seq', 'fsdp'), axis=0, tiled=True)]
    dot_general x49 -> x12, matrix products: 321 us -> 219 us  [the longest x8 145 us: dot32(): lax.dot_general(left, right, ((contract[0], contract[1]), ((), ())), pref...]
    unnamed x2 -> x0, blocking collectives: 82.6 us -> none
    ppermute x0 -> x69, starting transfers between devices: none -> 80.6 us  [the longest x41 44.8 us: send_plane(): return lax.ppermute(value, 'seq', [(i, i ^ step) for i in range(4)])]
    all_to_all x3 -> x0, waiting for transfers between devices: 52.5 us -> none  [the longest x1 27 us: body(): lax.all_to_all(attended.reshape(micro_count, query_rows, local_heads * he...]
  transfers between devices with their start and end apart: 19 -> 72, of which waited for: 13 -> 27; matrix products, arithmetic and copies ran while one was open for 10% -> 26% of each run, Pallas kernels for 0% -> 4%
where the time goes in v1:
time: 1170 us; the launch traced here: 1150 us
  waiting for transfers between devices  559 us (48%)
  matrix products  219 us (19%)
  other arithmetic  123 us (11%)
  local copies, waits for them, and re-layouts  116 us (10%)
  starting transfers between devices  80.8 us (7%)
  Pallas kernels  40.9 us (3%)
  between operations  15.4 us (1%)
    ppermute x18, waiting for transfers between devices, send_line(): lax.ppermute(value, 'dp', [(i, (i + step) % size) for i in range(size)])  288 us
    ppermute x41, waiting for transfers between devices, send_plane(): return lax.ppermute(value, 'seq', [(i, i ^ step) for i in range(4)])  228 us
    dot_general x8, matrix products, dot32(): lax.dot_general(left, right, ((contract[0], contract[1]), ((), ())), pref...  145 us
    ppermute x41, starting transfers between devices, send_plane(): return lax.ppermute(value, 'seq', [(i, i ^ step) for i in range(4)])  44.8 us
    all_gather x3, waiting for transfers between devices, gather(): return lax.all_gather(value, axes, axis=dim, tiled=True)  42 us
    pallas_call x2, Pallas kernels, attention_call(): pl.pallas_call(functools.partial(kernel, plan), grid=(groups,), in_specs=...  40.9 us
    dot_general x1, matrix products, body_plane(): gate_up_lin = jnp.dot(plane_two, gate_up, preferred_element_type=F32)  39 us
    squeeze x20, local copies, waits for them, and re-layouts, block_of(): return lax.dynamic_index_in_dim(value, index, axis=dim, keepdims=False)  35.9 us
  transfers between devices with their start and end apart: 72, of which 27 were waited for; matrix products, arithmetic and copies ran while one was open for 26% of the time, Pallas kernels for 4%

profile of v1, /device:TPU:0, one launch (start us, length us, event | category | flops | bytes accessed | tf_op | source)
XLA Modules:
  0.0 1154.2 jit_solution(741482001221903572)
XLA Ops:
  28.7 4.2 reshape.250
  38.3 27.3 %collective-permute-done.1 = bf16[128,2048]{1,0:T(8,128)(2,1)} collective-permute-done((bf16[128,2048]{1,0:T(8,128)(2,1)}, bf16[128,2048]{1,0:T(8,128)(2,1)}, u32[]{:S(2)}, u32[]{:S(2)}) %collective-permute-start.1) | collective-permute-done | bytes 524320 | tf_op jit(solution)/shard_map/ppermute | solution.py:534
  67.3 42.0 %all-gather.4.cloned.1.call-done = bf16[2048,2432]{1,0:T(8,128)(2,1)} async-done(((bf16[64,2432]{1,0:T(8,128)(2,1)}), bf16[2048,2432]{1,0:T(8,128)(2,1)}) %all-gather.4.cloned.1.call-update) | async-done | bytes 9961488 | tf_op jit(solution)/shard_map/all_gather | solution.py:526
  114.7 11.2 collective-permute-start.20
  132.3 14.5 %collective-permute-done.13 = bf16[64,2816]{1,0:T(8,128)(2,1)S(1)} collective-permute-done((bf16[64,2816]{1,0:T(8,128)(2,1)S(1)}, bf16[64,2816]{1,0:T(8,128)(2,1)S(1)}, u32[]{:S(2)}, u32[]{:S(2)}) %collective-permute-start.13) | collective-permute-done | bytes 360480 | tf_op jit(solution)/shard_map/ppermute | solution.py:534
  147.0 7.4 fusion.6
  169.3 16.0 %attend.1 = (bf16[512,2048]{1,0:T(8,128)(2,1)S(1)}, bf16[512,2048]{1,0:T(8,128)(2,1)S(1)}) custom-call(f32[512,2048]{1,0:T(8,128)} %slice.352.query_lin_ref, bf16[1024,128]{1,0:T(8,128)(2,1)S(1)} %get-tuple-element.116.keys_ref, bf16[1024,128]{1,0:T(8,128)(2,1)S(1)} %get-tuple-element.115.values_ref, s32[512,1]{1,0:T(8,128)S(1)} %copy.39.place_ref, ...), custom_call_target="tpu_custom_call" | custom-call | flops 2684354560 | bytes 6291456 | tf_op jit(solution)/shard_map/attend/pallas_call | solution.py:511
  185.3 25.6 %collective-permute-done.16 = bf16[256,2816]{1,0:T(8,128)(2,1)S(1)} collective-permute-done((bf16[256,2816]{1,0:T(8,128)(2,1)S(1)}, bf16[256,2816]{1,0:T(8,128)(2,1)S(1)}, u32[]{:S(2)}, u32[]{:S(2)}) %collective-permute-start.16) | collective-permute-done | bytes 1441824 | tf_op jit(solution)/shard_map/ppermute | solution.py:539
  213.6 96.1 %collective-permute-done.17 = bf16[256,2816]{1,0:T(8,128)(2,1)S(1)} collective-permute-done((bf16[256,2816]{1,0:T(8,128)(2,1)S(1)}, bf16[256,2816]{1,0:T(8,128)(2,1)S(1)}, u32[]{:S(2)}, u32[]{:S(2)}) %collective-permute-start.17) | collective-permute-done | bytes 1441824 | tf_op jit(solution)/shard_map/ppermute | solution.py:539
  310.9 30.2 %collective-permute-done.18 = bf16[256,2816]{1,0:T(8,128)(2,1)S(1)} collective-permute-done((bf16[256,2816]{1,0:T(8,128)(2,1)S(1)}, bf16[256,2816]{1,0:T(8,128)(2,1)S(1)}, u32[]{:S(2)}, u32[]{:S(2)}) %collective-permute-start.18) | collective-permute-done | bytes 1441824 | tf_op jit(solution)/shard_map/ppermute | solution.py:539
  342.3 8.9 multiply_reduce_fusion.2
  362.9 79.7 %collective-permute-done.31 = bf16[128,256]{1,0:T(8,128)(2,1)S(1)} collective-permute-done((bf16[128,256]{1,0:T(8,128)(2,1)S(1)}, bf16[128,256]{1,0:T(8,128)(2,1)S(1)}, u32[]{:S(2)}, u32[]{:S(2)}) %collective-permute-start.31) | collective-permute-done | bytes 65568 | tf_op jit(solution)/shard_map/ppermute | solution.py:534
  444.2 7.5 dynamic-slice_bitcast_fusion.5
  455.0 4.7 collective-permute-done.33
  470.3 9.3 select_bitcast_fusion.1
  479.6 9.8 pad_maximum_fusion
  489.4 39.0 %fusion.108 = f32[2048,2816]{1,0:T(8,128)} fusion(bf16[2048,2816]{1,0:T(8,128)(2,1)} %bitcast.354, bf16[512,1024]{1,0:T(8,128)(2,1)} %collective-permute-done.11, bf16[512,1024]{1,0:T(8,128)(2,1)} %collective-permute-done.10, bf16[512,2048]{1,0:T(8,128)(2,1)} %collective-permute-done.9, bf16[512,2048]{1,0:T(8,128)(2,1)} %collective-permute-done.8, ...), kind=kOutput, calls=%fused_computation.303 | convolution fusion | flops 23664263168 | bytes 42991616 | tf_op jit(solution)/shard_map/dot_general | solution.py:720
  528.4 28.9 %multiply_convert_fusion.1 = (bf16[2048,1408]{1,0:T(8,128)(2,1)}, bf16[2048,1408]{1,0:T(8,128)(2,1)}, bf16[2048,1408]{1,0:T(8,128)(2,1)}) fusion(f32[2048,2816]{1,0:T(8,128)} %fusion.108, bf16[1408,2048]{1,0:T(8,128)(2,1)} %bitcast.374, bf16[512,2048]{1,0:T(8,128)(2,1)} %get-tuple-element.51, bf16[512,2048]{1,0:T(8,128)(2,1)} %get-tuple-element.52, ...), kind=kOutput, calls=%fused_computation.7 | convolution fusion | flops 11887968256 | bytes 54525952 | tf_op jit(solution)/shard_map/dot_general | solution.py:384
  557.3 31.1 %convolution_convert_fusion.5 = bf16[2048,2048]{1,0:T(8,128)(2,1)} fusion(bf16[2048,2816]{1,0:T(8,128)(2,1)} %bitcast.355, bf16[2048,1408]{1,0:T(8,128)(2,1)} %get-tuple-element.40, bf16[2048,1408]{1,0:T(8,128)(2,1)} %get-tuple-element.39), kind=kOutput, calls=%fused_computation.28 | convolution fusion | flops 23649583104 | bytes 31457280 | tf_op jit(solution)/shard_map/dot_general | solution.py:384
  593.2 16.3 %convolution_convert_fusion.4 = bf16[1408,2048]{1,0:T(8,128)(2,1)S(1)} fusion(bf16[2048,1408]{1,0:T(8,128)(2,1)} %get-tuple-element.41, bf16[512,2048]{1,0:T(8,128)(2,1)} %get-tuple-element.51, bf16[512,2048]{1,0:T(8,128)(2,1)} %get-tuple-element.52, bf16[512,2048]{1,0:T(8,128)(2,1)} %get-tuple-element.50, bf16[512,2048]{1,0:T(8,128)(2,1)S(1)} %copy-done.24), kind=kOutput, calls=%fused_computation.27 | convolution fusion | flops 11847598080 | bytes 19922944 | tf_op jit(solution)/shard_map/dot_general | solution.py:384
  609.5 18.9 %convolution_convert_fusion.3 = bf16[2048,2048]{1,0:T(8,128)(2,1)S(1)} fusion(bf16[2048,1408]{1,0:T(8,128)(2,1)} %get-tuple-element.41, bf16[1408,2048]{1,0:T(8,128)(2,1)} %bitcast.375), kind=kOutput, calls=%fused_computation.26 | convolution fusion | flops 11815354368 | bytes 19922944 | tf_op jit(solution)/shard_map/dot_general | solution.py:725
  641.5 33.7 %convolution_convert_fusion = bf16[2048,2816]{1,0:T(8,128)(2,1)} fusion(bf16[2048,1408]{1,0:T(8,128)(2,1)} %get-tuple-element.40, bf16[2048,1408]{1,0:T(8,128)(2,1)} %get-tuple-element.39, bf16[512,1024]{1,0:T(8,128)(2,1)} %collective-permute-done.11, bf16[512,1024]{1,0:T(8,128)(2,1)} %collective-permute-done.10, ...), kind=kOutput, calls=%fused_computation.11 | convolution fusion | flops 23693099008 | bytes 31457280 | tf_op jit(solution)/shard_map/dot_general | solution.py:384
  675.1 5.6 dynamic-slice_bitcast_fusion
  686.9 3.9 fusion.55
  692.4 32.4 %collective-permute-done.24 = bf16[2,512,1024]{2,1,0:T(8,128)(2,1)} collective-permute-done((bf16[2,512,1024]{2,1,0:T(8,128)(2,1)}, bf16[2,512,1024]{2,1,0:T(8,128)(2,1)}, u32[]{:S(2)}, u32[]{:S(2)}) %collective-permute-start.24) | collective-permute-done | bytes 2097184 | tf_op jit(solution)/shard_map/ppermute | solution.py:534
  743.0 8.6 collective-permute-done.35
  760.2 10.5 collective-permute-done.25
  773.1 4.0 fusion.41
  781.8 6.8 convolution_convert_fusion.2
  788.7 9.3 convolution_convert_fusion.6.grad_ref
  798.0 25.0 %attend_back.1 = (bf16[512,2048]{1,0:T(8,128)(2,1)S(1)}, f32[1024,128]{1,0:T(8,128)S(1)}, f32[1024,128]{1,0:T(8,128)S(1)}) custom-call(bf16[512,2048]{1,0:T(8,128)(2,1)} %copy-done.8, bf16[512,2048]{1,0:T(8,128)(2,1)} %convolution_convert_fusion.6.grad_ref, bf16[1024,128]{1,0:T(8,128)(2,1)S(1)} %copy-done.7, bf16[1024,128]{1,0:T(8,128)(2,1)S(1)} %copy-done.5, ...), custom_call_target="tpu_custom_call" | custom-call | flops 6710886400 | bytes 6291456 | tf_op jit(solution)/shard_map/attend_back/pallas_call | solution.py:511
  823.1 4.9 dynamic-slice_bitcast_fusion.1
  836.2 11.0 fusion.24
  847.2 3.6 fusion.23
  852.3 7.8 convolution_convert_fusion.1
  860.5 5.0 fusion.10
  869.7 6.0 fusion
  883.4 8.7 collective-permute-done.40
  898.6 13.8 %collective-permute-done.59 = bf16[4,64,2816]{2,1,0:T(8,128)(2,1)S(1)} collective-permute-done((bf16[4,64,2816]{2,1,0:T(8,128)(2,1)S(1)}, bf16[4,64,2816]{2,1,0:T(8,128)(2,1)S(1)}, u32[]{:S(2)}, u32[]{:S(2)}) %collective-permute-start.59) | collective-permute-done | bytes 1441824 | tf_op jit(solution)/shard_map/ppermute | solution.py:539
  912.5 28.1 %collective-permute-done.61 = bf16[4,64,2816]{2,1,0:T(8,128)(2,1)S(1)} collective-permute-done((bf16[4,64,2816]{2,1,0:T(8,128)(2,1)S(1)}, bf16[4,64,2816]{2,1,0:T(8,128)(2,1)S(1)}, u32[]{:S(2)}, u32[]{:S(2)}) %collective-permute-start.61) | collective-permute-done | bytes 1441824 | tf_op jit(solution)/shard_map/ppermute | solution.py:539
  940.6 61.3 %collective-permute-done.60 = bf16[4,64,2816]{2,1,0:T(8,128)(2,1)S(1)} collective-permute-done((bf16[4,64,2816]{2,1,0:T(8,128)(2,1)S(1)}, bf16[4,64,2816]{2,1,0:T(8,128)(2,1)S(1)}, u32[]{:S(2)}, u32[]{:S(2)}) %collective-permute-start.60) | collective-permute-done | bytes 1441824 | tf_op jit(solution)/shard_map/ppermute | solution.py:539
  1005.4 5.6 fusion.3
  1027.7 3.9 fusion.2
  1038.3 16.1 %collective-permute-done.64 = bf16[64,2816]{1,0:T(8,128)(2,1)S(1)} collective-permute-done((bf16[64,2816]{1,0:T(8,128)(2,1)S(1)}, bf16[64,2816]{1,0:T(8,128)(2,1)S(1)}, u32[]{:S(2)}, u32[]{:S(2)}) %collective-permute-start.64) | collective-permute-done | bytes 360480 | tf_op jit(solution)/shard_map/ppermute | solution.py:534
  1055.1 4.0 reshape.277
  1068.0 14.5 %collective-permute-done.43 = bf16[2,4,64,1216]{3,2,1,0:T(8,128)(2,1)} collective-permute-done((bf16[2,4,64,1216]{3,2,1,0:T(8,128)(2,1)}, bf16[2,4,64,1216]{3,2,1,0:T(8,128)(2,1)}, u32[]{:S(2)}, u32[]{:S(2)}) %collective-permute-start.43) | collective-permute-done | bytes 1245216 | tf_op jit(solution)/shard_map/ppermute | solution.py:534
  1114.1 13.2 %collective-permute-done.56 = bf16[64,2048]{1,0:T(8,128)(2,1)S(1)} collective-permute-done((bf16[64,2048]{1,0:T(8,128)(2,1)S(1)}, bf16[64,2048]{1,0:T(8,128)(2,1)S(1)}, u32[]{:S(2)}, u32[]{:S(2)}) %collective-permute-start.56) | collective-permute-done | bytes 262176 | tf_op jit(solution)/shard_map/ppermute | solution.py:539
  1131.6 13.5 %collective-permute-done.48 = bf16[64,2432]{1,0:T(8,128)(2,1)S(1)} collective-permute-done((bf16[64,2432]{1,0:T(8,128)(2,1)S(1)}, bf16[64,2432]{1,0:T(8,128)(2,1)S(1)}, u32[]{:S(2)}, u32[]{:S(2)}) %collective-permute-start.48) | collective-permute-done | bytes 311328 | tf_op jit(solution)/shard_map/ppermute | solution.py:539
  (404 shorter events, 249.6 us)
Async XLA Ops:
  7.3 102.1 %all-gather.4.cloned.1.call-start = ((), (), s32[]{:S(2)}) async-start(), calls=%async_computation | async-start | bytes 10272768 | tf_op jit(solution)/shard_map/all_gather | solution.py:526
  9.9 332.4 %all-gather.6.cloned.1.call-start = ((), (), s32[]{:S(2)}) async-start(), calls=%async_computation.1 | async-start | bytes 8650752 | tf_op jit(solution)/shard_map/all_gather | solution.py:526
  10.6 433.6 %all-gather.8.cloned.1.call-start = ((), (), s32[]{:S(2)}) async-start(), calls=%async_computation.2 | async-start | bytes 10485760 | tf_op jit(solution)/shard_map/all_gather | solution.py:526
  35.3 30.3 %collective-permute-start.1 = (bf16[128,2048]{1,0:T(8,128)(2,1)}, bf16[128,2048]{1,0:T(8,128)(2,1)}, u32[]{:S(2)}, u32[]{:S(2)}) collective-permute-start(bf16[128,2048]{1,0:T(8,128)(2,1)} %get-tuple-element.94), channel_id=1, source_target_pairs={{0,4},{2,6},{4,0},{6,2},{1,5},{3,7},{5,1},{7,3},{8,12},{10,14},{12... | collective-permute-start | bytes 1572872 | tf_op jit(solution)/shard_map/ppermute | solution.py:534
  38.0 28.7 %collective-permute-start.2 = (bf16[128,2048]{1,0:T(8,128)(2,1)}, bf16[128,2048]{1,0:T(8,128)(2,1)S(1)}, u32[]{:S(2)}, u32[]{:S(2)}) collective-permute-start(bf16[128,2048]{1,0:T(8,128)(2,1)} %get-tuple-element.92), channel_id=1, source_target_pairs={{0,6},{2,4},{4,2},{6,0},{1,7},{3,5},{5,3},{7,1},{8,14},{10,12},{12... | collective-permute-start | bytes 1572872 | tf_op jit(solution)/shard_map/ppermute | solution.py:534
  111.8 244.1 %collective-permute-start.22 = (bf16[176,2048]{1,0:T(8,128)(2,1)}, bf16[176,2048]{1,0:T(8,128)(2,1)}, u32[]{:S(2)}, u32[]{:S(2)}) collective-permute-start(bf16[176,2048]{1,0:T(8,128)(2,1)} %param.23), channel_id=1, source_target_pairs={{0,24},{8,0},{16,8},{24,16},{1,25},{9,1},{17,9},{25,17},{2,26},{10... | collective-permute-start | bytes 2162696 | tf_op jit(solution)/shard_map/ppermute | solution.py:539
  113.7 240.2 %collective-permute-start.21 = (bf16[176,2048]{1,0:T(8,128)(2,1)}, bf16[176,2048]{1,0:T(8,128)(2,1)}, u32[]{:S(2)}, u32[]{:S(2)}) collective-permute-start(bf16[176,2048]{1,0:T(8,128)(2,1)} %param.23), channel_id=1, source_target_pairs={{0,16},{8,24},{16,0},{24,8},{1,17},{9,25},{17,1},{25,9},{2,18},{10... | collective-permute-start | bytes 2162696 | tf_op jit(solution)/shard_map/ppermute | solution.py:539
  114.7 236.5 %collective-permute-start.20 = (bf16[176,2048]{1,0:T(8,128)(2,1)}, bf16[176,2048]{1,0:T(8,128)(2,1)}, u32[]{:S(2)}, u32[]{:S(2)}) collective-permute-start(bf16[176,2048]{1,0:T(8,128)(2,1)} %param.23), channel_id=1, source_target_pairs={{0,8},{8,16},{16,24},{24,0},{1,9},{9,17},{17,25},{25,1},{2,10},{10... | collective-permute-start | bytes 2162696 | tf_op jit(solution)/shard_map/ppermute | solution.py:539
  162.4 48.5 %collective-permute-start.16 = (bf16[256,2816]{1,0:T(8,128)(2,1)S(1)}, bf16[256,2816]{1,0:T(8,128)(2,1)S(1)}, u32[]{:S(2)}, u32[]{:S(2)}) collective-permute-start(bf16[256,2816]{1,0:T(8,128)(2,1)S(1)} %get-tuple-element.82), channel_id=1, source_target_pairs={{0,8},{8,16},{16,24},{24,0},{1,9},{9,17},{17,25},{25,1},{2,10},{10... | collective-permute-start | bytes 4325384 | tf_op jit(solution)/shard_map/ppermute | solution.py:539
  167.1 142.6 %collective-permute-start.17 = (bf16[256,2816]{1,0:T(8,128)(2,1)S(1)}, bf16[256,2816]{1,0:T(8,128)(2,1)S(1)}, u32[]{:S(2)}, u32[]{:S(2)}) collective-permute-start(bf16[256,2816]{1,0:T(8,128)(2,1)S(1)} %get-tuple-element.82), channel_id=1, source_target_pairs={{0,16},{8,24},{16,0},{24,8},{1,17},{9,25},{17,1},{25,9},{2,18},{10... | collective-permute-start | bytes 4325384 | tf_op jit(solution)/shard_map/ppermute | solution.py:539
  210.9 130.2 %collective-permute-start.18 = (bf16[256,2816]{1,0:T(8,128)(2,1)S(1)}, bf16[256,2816]{1,0:T(8,128)(2,1)S(1)}, u32[]{:S(2)}, u32[]{:S(2)}) collective-permute-start(bf16[256,2816]{1,0:T(8,128)(2,1)S(1)} %get-tuple-element.82), channel_id=1, source_target_pairs={{0,24},{8,0},{16,8},{24,16},{1,25},{9,1},{17,9},{25,17},{2,26},{10... | collective-permute-start | bytes 4325384 | tf_op jit(solution)/shard_map/ppermute | solution.py:539
  342.3 128.0 %collective-permute-start.19 = (bf16[4,256,2816]{2,1,0:T(8,128)(2,1)}, bf16[4,256,2816]{2,1,0:T(8,128)(2,1)}, u32[]{:S(2)}, u32[]{:S(2)}) collective-permute-start(bf16[4,256,2816]{2,1,0:T(8,128)(2,1)} %bitcast_dynamic-update-slice_fusion), channel_id=1, source_target_pairs={{0,1},{1,0},{2,3},{3,2},{4,5},{5,4},{6,7},{7,6},{8,9},{9,8},{10,11... | collective-permute-start | bytes 17301512 | tf_op jit(solution)/shard_map/ppermute | solution.py:543
  357.9 106.2 %collective-permute-start.23 = (bf16[4,176,2048]{2,1,0:T(8,128)(2,1)}, bf16[4,176,2048]{2,1,0:T(8,128)(2,1)}, u32[]{:S(2)}, u32[]{:S(2)}) collective-permute-start(bf16[4,176,2048]{2,1,0:T(8,128)(2,1)} %bitcast_dynamic-update-slice_fusion.3), channel_id=1, source_target_pairs={{0,1},{1,0},{2,3},{3,2},{4,5},{5,4},{6,7},{7,6},{8,9},{9,8},{10,11... | collective-permute-start | bytes 8650760 | tf_op jit(solution)/shard_map/ppermute | solution.py:543
  360.2 100.2 %collective-permute-start.9 = (bf16[512,2048]{1,0:T(8,128)(2,1)}, bf16[512,2048]{1,0:T(8,128)(2,1)}, u32[]{:S(2)}, u32[]{:S(2)}) collective-permute-start(bf16[512,2048]{1,0:T(8,128)(2,1)} %multiply_convert_fusion.3), channel_id=1, source_target_pairs={{0,4},{2,6},{4,0},{6,2},{1,5},{3,7},{5,1},{7,3},{8,12},{10,14},{12... | collective-permute-start | bytes 6291464 | tf_op jit(solution)/shard_map/ppermute | solution.py:534
  360.9 101.4 %collective-permute-start.8 = (bf16[512,2048]{1,0:T(8,128)(2,1)}, bf16[512,2048]{1,0:T(8,128)(2,1)}, u32[]{:S(2)}, u32[]{:S(2)}) collective-permute-start(bf16[512,2048]{1,0:T(8,128)(2,1)} %multiply_convert_fusion.3), channel_id=1, source_target_pairs={{0,2},{2,0},{4,6},{6,4},{1,3},{3,1},{5,7},{7,5},{8,10},{10,8},{12,... | collective-permute-start | bytes 6291464 | tf_op jit(solution)/shard_map/ppermute | solution.py:534
  362.4 80.3 %collective-permute-start.31 = (bf16[128,256]{1,0:T(8,128)(2,1)S(1)}, bf16[128,256]{1,0:T(8,128)(2,1)S(1)}, u32[]{:S(2)}, u32[]{:S(2)}) collective-permute-start(bf16[128,256]{1,0:T(8,128)(2,1)S(1)} %dynamic-slice_bitcast_fusion.40), channel_id=1, source_target_pairs={{0,2},{2,0},{4,6},{6,4},{1,3},{3,1},{5,7},{7,5},{8,10},{10,8},{12,... | collective-permute-start | bytes 196616 | tf_op jit(solution)/shard_map/ppermute | solution.py:534
  461.7 27.7 %collective-permute-start.11 = (bf16[512,1024]{1,0:T(8,128)(2,1)S(1)}, bf16[512,1024]{1,0:T(8,128)(2,1)}, u32[]{:S(2)}, u32[]{:S(2)}) collective-permute-start(bf16[512,1024]{1,0:T(8,128)(2,1)S(1)} %slice.362), channel_id=1, source_target_pairs={{0,2},{2,0},{4,6},{6,4},{1,3},{3,1},{5,7},{7,5},{8,10},{10,8},{12,... | collective-permute-start | bytes 3145736 | tf_op jit(solution)/shard_map/ppermute | solution.py:534
  463.6 25.8 %collective-permute-start.10 = (bf16[512,1024]{1,0:T(8,128)(2,1)S(1)}, bf16[512,1024]{1,0:T(8,128)(2,1)}, u32[]{:S(2)}, u32[]{:S(2)}) collective-permute-start(bf16[512,1024]{1,0:T(8,128)(2,1)S(1)} %slice.361), channel_id=1, source_target_pairs={{0,4},{2,6},{4,0},{6,2},{1,5},{3,7},{5,1},{7,3},{8,12},{10,14},{12... | collective-permute-start | bytes 3145736 | tf_op jit(solution)/shard_map/ppermute | solution.py:534
  633.9 48.9 %collective-permute-start.34 = (bf16[2,512,1024]{2,1,0:T(8,128)(2,1)}, bf16[2,512,1024]{2,1,0:T(8,128)(2,1)}, u32[]{:S(2)}, u32[]{:S(2)}) collective-permute-start(bf16[2,512,1024]{2,1,0:T(8,128)(2,1)} %pad_maximum_fusion.10), channel_id=1, source_target_pairs={{0,2},{2,0},{4,6},{6,4},{1,3},{3,1},{5,7},{7,5},{8,10},{10,8},{12,... | collective-permute-start | bytes 6291464 | tf_op jit(solution)/shard_map/ppermute | solution.py:534
  635.4 49.4 %collective-permute-start.36 = (bf16[2,512,1024]{2,1,0:T(8,128)(2,1)}, bf16[2,512,1024]{2,1,0:T(8,128)(2,1)}, u32[]{:S(2)}, u32[]{:S(2)}) collective-permute-start(bf16[2,512,1024]{2,1,0:T(8,128)(2,1)} %slice.385), channel_id=1, source_target_pairs={{0,4},{2,6},{4,0},{6,2},{1,5},{3,7},{5,1},{7,3},{8,12},{10,14},{12... | collective-permute-start | bytes 6291464 | tf_op jit(solution)/shard_map/ppermute | solution.py:534
  638.4 86.3 %collective-permute-start.24 = (bf16[2,512,1024]{2,1,0:T(8,128)(2,1)}, bf16[2,512,1024]{2,1,0:T(8,128)(2,1)}, u32[]{:S(2)}, u32[]{:S(2)}) collective-permute-start(bf16[2,512,1024]{2,1,0:T(8,128)(2,1)} %pad_maximum_fusion.9), channel_id=1, source_target_pairs={{0,2},{2,0},{4,6},{6,4},{1,3},{3,1},{5,7},{7,5},{8,10},{10,8},{12,... | collective-permute-start | bytes 6291464 | tf_op jit(solution)/shard_map/ppermute | solution.py:534
  639.0 90.3 %collective-permute-start.26 = (bf16[2,512,1024]{2,1,0:T(8,128)(2,1)}, bf16[2,512,1024]{2,1,0:T(8,128)(2,1)}, u32[]{:S(2)}, u32[]{:S(2)}) collective-permute-start(bf16[2,512,1024]{2,1,0:T(8,128)(2,1)} %slice.372), channel_id=1, source_target_pairs={{0,4},{2,6},{4,0},{6,2},{1,5},{3,7},{5,1},{7,3},{8,12},{10,14},{12... | collective-permute-start | bytes 6291464 | tf_op jit(solution)/shard_map/ppermute | solution.py:534
  641.4 95.0 %collective-permute-start.65 = (bf16[4,176,2048]{2,1,0:T(8,128)(2,1)}, bf16[4,176,2048]{2,1,0:T(8,128)(2,1)S(1)}, u32[]{:S(2)}, u32[]{:S(2)}) collective-permute-start(bf16[4,176,2048]{2,1,0:T(8,128)(2,1)} %dynamic-slice_bitcast_fusion.2), channel_id=1, source_target_pairs={{0,1},{1,0},{2,3},{3,2},{4,5},{5,4},{6,7},{7,6},{8,9},{9,8},{10,11... | collective-permute-start | bytes 8650760 | tf_op jit(solution)/shard_map/ppermute | solution.py:543
  682.8 186.2 %collective-permute-start.58 = (bf16[4,4,64,2816]{3,2,1,0:T(8,128)(2,1)}, bf16[4,4,64,2816]{3,2,1,0:T(8,128)(2,1)}, u32[]{:S(2)}, u32[]{:S(2)}) collective-permute-start(bf16[4,4,64,2816]{3,2,1,0:T(8,128)(2,1)} %dynamic-slice_bitcast_fusion), channel_id=1, source_target_pairs={{0,1},{1,0},{2,3},{3,2},{4,5},{5,4},{6,7},{7,6},{8,9},{9,8},{10,11... | collective-permute-start | bytes 17301512 | tf_op jit(solution)/shard_map/ppermute | solution.py:543
  690.8 60.8 %collective-permute-start.35 = (bf16[512,1024]{1,0:T(8,128)(2,1)S(1)}, bf16[512,1024]{1,0:T(8,128)(2,1)S(1)}, u32[]{:S(2)}, u32[]{:S(2)}) collective-permute-start(bf16[512,1024]{1,0:T(8,128)(2,1)S(1)} %get-tuple-element.46), channel_id=1, source_target_pairs={{0,4},{2,6},{4,0},{6,2},{1,5},{3,7},{5,1},{7,3},{8,12},{10,14},{12... | collective-permute-start | bytes 3145736 | tf_op jit(solution)/shard_map/ppermute | solution.py:534
  724.8 28.3 %collective-permute-start.37 = (bf16[512,1024]{1,0:T(8,128)(2,1)S(1)}, bf16[512,1024]{1,0:T(8,128)(2,1)S(1)}, u32[]{:S(2)}, u32[]{:S(2)}) collective-permute-start(bf16[512,1024]{1,0:T(8,128)(2,1)S(1)} %get-tuple-element.47), channel_id=1, source_target_pairs={{0,2},{2,0},{4,6},{6,4},{1,3},{3,1},{5,7},{7,5},{8,10},{10,8},{12,... | collective-permute-start | bytes 3145736 | tf_op jit(solution)/shard_map/ppermute | solution.py:534
  735.0 35.7 %collective-permute-start.25 = (bf16[512,1024]{1,0:T(8,128)(2,1)}, bf16[512,1024]{1,0:T(8,128)(2,1)S(1)}, u32[]{:S(2)}, u32[]{:S(2)}) collective-permute-start(bf16[512,1024]{1,0:T(8,128)(2,1)} %get-tuple-element.56), channel_id=1, source_target_pairs={{0,4},{2,6},{4,0},{6,2},{1,5},{3,7},{5,1},{7,3},{8,12},{10,14},{12... | collective-permute-start | bytes 3145736 | tf_op jit(solution)/shard_map/ppermute | solution.py:534
  738.0 35.0 %collective-permute-start.27 = (bf16[512,1024]{1,0:T(8,128)(2,1)S(1)}, bf16[512,1024]{1,0:T(8,128)(2,1)S(1)}, u32[]{:S(2)}, u32[]{:S(2)}) collective-permute-start(bf16[512,1024]{1,0:T(8,128)(2,1)S(1)} %get-tuple-element.57), channel_id=1, source_target_pairs={{0,2},{2,0},{4,6},{6,4},{1,3},{3,1},{5,7},{7,5},{8,10},{10,8},{12,... | collective-permute-start | bytes 3145736 | tf_op jit(solution)/shard_map/ppermute | solution.py:534
  751.6 76.3 %collective-permute-start.66 = (bf16[176,2048]{1,0:T(8,128)(2,1)}, bf16[176,2048]{1,0:T(8,128)(2,1)}, u32[]{:S(2)}, u32[]{:S(2)}) collective-permute-start(bf16[176,2048]{1,0:T(8,128)(2,1)} %get-tuple-element.79), channel_id=1, source_target_pairs={{0,8},{8,16},{16,24},{24,0},{1,9},{9,17},{17,25},{25,1},{2,10},{10... | collective-permute-start | bytes 2162696 | tf_op jit(solution)/shard_map/ppermute | solution.py:539
  753.1 74.8 %collective-permute-start.68 = (bf16[176,2048]{1,0:T(8,128)(2,1)}, bf16[176,2048]{1,0:T(8,128)(2,1)}, u32[]{:S(2)}, u32[]{:S(2)}) collective-permute-start(bf16[176,2048]{1,0:T(8,128)(2,1)} %get-tuple-element.80), channel_id=1, source_target_pairs={{0,24},{8,0},{16,8},{24,16},{1,25},{9,1},{17,9},{25,17},{2,26},{10... | collective-permute-start | bytes 2162696 | tf_op jit(solution)/shard_map/ppermute | solution.py:539
  770.7 57.8 %collective-permute-start.67 = (bf16[176,2048]{1,0:T(8,128)(2,1)}, bf16[176,2048]{1,0:T(8,128)(2,1)}, u32[]{:S(2)}, u32[]{:S(2)}) collective-permute-start(bf16[176,2048]{1,0:T(8,128)(2,1)} %get-tuple-element.81), channel_id=1, source_target_pairs={{0,16},{8,24},{16,0},{24,8},{1,17},{9,25},{17,1},{25,9},{2,18},{10... | collective-permute-start | bytes 2162696 | tf_op jit(solution)/shard_map/ppermute | solution.py:539
  781.2 50.4 %collective-permute-start.28 = (bf16[128,2048]{1,0:T(8,128)(2,1)}, bf16[128,2048]{1,0:T(8,128)(2,1)S(1)}, u32[]{:S(2)}, u32[]{:S(2)}) collective-permute-start(bf16[128,2048]{1,0:T(8,128)(2,1)} %dynamic-slice_bitcast_fusion.28), channel_id=1, source_target_pairs={{0,2},{2,0},{4,6},{6,4},{1,3},{3,1},{5,7},{7,5},{8,10},{10,8},{12,... | collective-permute-start | bytes 1572872 | tf_op jit(solution)/shard_map/ppermute | solution.py:534
  828.0 177.4 %collective-permute-start.50 = (bf16[4,4,64,2048]{3,2,1,0:T(8,128)(2,1)}, bf16[4,4,64,2048]{3,2,1,0:T(8,128)(2,1)}, u32[]{:S(2)}, u32[]{:S(2)}) collective-permute-start(bf16[4,4,64,2048]{3,2,1,0:T(8,128)(2,1)} %dynamic-slice_bitcast_fusion.1), channel_id=1, source_target_pairs={{0,1},{1,0},{2,3},{3,2},{4,5},{5,4},{6,7},{7,6},{8,9},{9,8},{10,11... | collective-permute-start | bytes 12582920 | tf_op jit(solution)/shard_map/ppermute | solution.py:543
  832.8 43.2 %collective-permute-start.30 = (bf16[128,2048]{1,0:T(8,128)(2,1)}, bf16[128,2048]{1,0:T(8,128)(2,1)}, u32[]{:S(2)}, u32[]{:S(2)}) collective-permute-start(bf16[128,2048]{1,0:T(8,128)(2,1)} %get-tuple-element.89), channel_id=1, source_target_pairs={{0,6},{2,4},{4,2},{6,0},{1,7},{3,5},{5,3},{7,1},{8,14},{10,12},{12... | collective-permute-start | bytes 1572872 | tf_op jit(solution)/shard_map/ppermute | solution.py:534
  835.0 42.6 %collective-permute-start.29 = (bf16[128,2048]{1,0:T(8,128)(2,1)}, bf16[128,2048]{1,0:T(8,128)(2,1)}, u32[]{:S(2)}, u32[]{:S(2)}) collective-permute-start(bf16[128,2048]{1,0:T(8,128)(2,1)} %get-tuple-element.90), channel_id=1, source_target_pairs={{0,4},{2,6},{4,0},{6,2},{1,5},{3,7},{5,1},{7,3},{8,12},{10,14},{12... | collective-permute-start | bytes 1572872 | tf_op jit(solution)/shard_map/ppermute | solution.py:534
  876.1 36.4 %collective-permute-start.59 = (bf16[4,64,2816]{2,1,0:T(8,128)(2,1)S(1)}, bf16[4,64,2816]{2,1,0:T(8,128)(2,1)S(1)}, u32[]{:S(2)}, u32[]{:S(2)}) collective-permute-start(bf16[4,64,2816]{2,1,0:T(8,128)(2,1)S(1)} %get-tuple-element.60), channel_id=1, source_target_pairs={{0,8},{8,16},{16,24},{24,0},{1,9},{9,17},{17,25},{25,1},{2,10},{10... | collective-permute-start | bytes 4325384 | tf_op jit(solution)/shard_map/ppermute | solution.py:539
  877.6 63.0 %collective-permute-start.61 = (bf16[4,64,2816]{2,1,0:T(8,128)(2,1)S(1)}, bf16[4,64,2816]{2,1,0:T(8,128)(2,1)S(1)}, u32[]{:S(2)}, u32[]{:S(2)}) collective-permute-start(bf16[4,64,2816]{2,1,0:T(8,128)(2,1)S(1)} %get-tuple-element.61), channel_id=1, source_target_pairs={{0,24},{8,0},{16,8},{24,16},{1,25},{9,1},{17,9},{25,17},{2,26},{10... | collective-permute-start | bytes 4325384 | tf_op jit(solution)/shard_map/ppermute | solution.py:539
  880.9 121.0 %collective-permute-start.60 = (bf16[4,64,2816]{2,1,0:T(8,128)(2,1)S(1)}, bf16[4,64,2816]{2,1,0:T(8,128)(2,1)S(1)}, u32[]{:S(2)}, u32[]{:S(2)}) collective-permute-start(bf16[4,64,2816]{2,1,0:T(8,128)(2,1)S(1)} %get-tuple-element.62), channel_id=1, source_target_pairs={{0,16},{8,24},{16,0},{24,8},{1,17},{9,25},{17,1},{25,9},{2,18},{10... | collective-permute-start | bytes 4325384 | tf_op jit(solution)/shard_map/ppermute | solution.py:539
  892.0 135.7 %collective-permute-start.42 = (bf16[4,4,64,2432]{3,2,1,0:T(8,128)(2,1)}, bf16[4,4,64,2432]{3,2,1,0:T(8,128)(2,1)}, u32[]{:S(2)}, u32[]{:S(2)}) collective-permute-start(bf16[4,4,64,2432]{3,2,1,0:T(8,128)(2,1)} %fusion.10), channel_id=1, source_target_pairs={{0,1},{1,0},{2,3},{3,2},{4,5},{5,4},{6,7},{7,6},{8,9},{9,8},{10,11... | collective-permute-start | bytes 14942216 | tf_op jit(solution)/shard_map/ppermute | solution.py:543
  1020.2 41.0 %collective-permute-start.51 = (bf16[2,4,64,1024]{3,2,1,0:T(8,128)(2,1)}, bf16[2,4,64,1024]{3,2,1,0:T(8,128)(2,1)}, u32[]{:S(2)}, u32[]{:S(2)}) collective-permute-start(bf16[2,4,64,1024]{3,2,1,0:T(8,128)(2,1)} %pad_maximum_fusion.17), channel_id=1, source_target_pairs={{0,2},{2,0},{4,6},{6,4},{1,3},{3,1},{5,7},{7,5},{8,10},{10,8},{12,... | collective-permute-start | bytes 3145736 | tf_op jit(solution)/shard_map/ppermute | solution.py:534
  1021.9 43.1 %collective-permute-start.53 = (bf16[2,4,64,1024]{3,2,1,0:T(8,128)(2,1)}, bf16[2,4,64,1024]{3,2,1,0:T(8,128)(2,1)}, u32[]{:S(2)}, u32[]{:S(2)}) collective-permute-start(bf16[2,4,64,1024]{3,2,1,0:T(8,128)(2,1)} %pad_maximum_fusion.15), channel_id=1, source_target_pairs={{0,4},{2,6},{4,0},{6,2},{1,5},{3,7},{5,1},{7,3},{8,12},{10,14},{12... | collective-permute-start | bytes 3145736 | tf_op jit(solution)/shard_map/ppermute | solution.py:534
  1022.6 31.8 %collective-permute-start.64 = (bf16[64,2816]{1,0:T(8,128)(2,1)S(1)}, bf16[64,2816]{1,0:T(8,128)(2,1)S(1)}, u32[]{:S(2)}, u32[]{:S(2)}) collective-permute-start(bf16[64,2816]{1,0:T(8,128)(2,1)S(1)} %get-tuple-element.95), channel_id=1, source_target_pairs={{0,6},{2,4},{4,2},{6,0},{1,7},{3,5},{5,3},{7,1},{8,14},{10,12},{12... | collective-permute-start | bytes 1081352 | tf_op jit(solution)/shard_map/ppermute | solution.py:534
  1036.4 46.1 %collective-permute-start.43 = (bf16[2,4,64,1216]{3,2,1,0:T(8,128)(2,1)}, bf16[2,4,64,1216]{3,2,1,0:T(8,128)(2,1)}, u32[]{:S(2)}, u32[]{:S(2)}) collective-permute-start(bf16[2,4,64,1216]{3,2,1,0:T(8,128)(2,1)} %pad_maximum_fusion.14), channel_id=1, source_target_pairs={{0,2},{2,0},{4,6},{6,4},{1,3},{3,1},{5,7},{7,5},{8,10},{10,8},{12,... | collective-permute-start | bytes 3735560 | tf_op jit(solution)/shard_map/ppermute | solution.py:534
  1036.4 49.3 %collective-permute-start.45 = (bf16[2,4,64,1216]{3,2,1,0:T(8,128)(2,1)}, bf16[2,4,64,1216]{3,2,1,0:T(8,128)(2,1)}, u32[]{:S(2)}, u32[]{:S(2)}) collective-permute-start(bf16[2,4,64,1216]{3,2,1,0:T(8,128)(2,1)} %pad_maximum_fusion.13), channel_id=1, source_target_pairs={{0,4},{2,6},{4,0},{6,2},{1,5},{3,7},{5,1},{7,3},{8,12},{10,14},{12... | collective-permute-start | bytes 3735560 | tf_op jit(solution)/shard_map/ppermute | solution.py:534
  1063.6 36.0 %collective-permute-start.52 = (bf16[4,64,1024]{2,1,0:T(8,128)(2,1)}, bf16[4,64,1024]{2,1,0:T(8,128)(2,1)}, u32[]{:S(2)}, u32[]{:S(2)}) collective-permute-start(bf16[4,64,1024]{2,1,0:T(8,128)(2,1)} %fusion.72), channel_id=1, source_target_pairs={{0,4},{2,6},{4,0},{6,2},{1,5},{3,7},{5,1},{7,3},{8,12},{10,14},{12... | collective-permute-start | bytes 1572872 | tf_op jit(solution)/shard_map/ppermute | solution.py:534
  1067.4 32.2 %collective-permute-start.54 = (bf16[4,64,1024]{2,1,0:T(8,128)(2,1)}, bf16[4,64,1024]{2,1,0:T(8,128)(2,1)}, u32[]{:S(2)}, u32[]{:S(2)}) collective-permute-start(bf16[4,64,1024]{2,1,0:T(8,128)(2,1)} %fusion.73), channel_id=1, source_target_pairs={{0,2},{2,0},{4,6},{6,4},{1,3},{3,1},{5,7},{7,5},{8,10},{10,8},{12,... | collective-permute-start | bytes 1572872 | tf_op jit(solution)/shard_map/ppermute | solution.py:534
  1110.3 34.8 %collective-permute-start.48 = (bf16[64,2432]{1,0:T(8,128)(2,1)S(1)}, bf16[64,2432]{1,0:T(8,128)(2,1)S(1)}, u32[]{:S(2)}, u32[]{:S(2)}) collective-permute-start(bf16[64,2432]{1,0:T(8,128)(2,1)S(1)} %get-tuple-element.102), channel_id=1, source_target_pairs={{0,16},{8,24},{16,0},{24,8},{1,17},{9,25},{17,1},{25,9},{2,18},{10... | collective-permute-start | bytes 933896 | tf_op jit(solution)/shard_map/ppermute | solution.py:539
  1113.8 31.3 %collective-permute-start.49 = (bf16[64,2432]{1,0:T(8,128)(2,1)S(1)}, bf16[64,2432]{1,0:T(8,128)(2,1)S(1)}, u32[]{:S(2)}, u32[]{:S(2)}) collective-permute-start(bf16[64,2432]{1,0:T(8,128)(2,1)S(1)} %get-tuple-element.103), channel_id=1, source_target_pairs={{0,24},{8,0},{16,8},{24,16},{1,25},{9,1},{17,9},{25,17},{2,26},{10... | collective-permute-start | bytes 933896 | tf_op jit(solution)/shard_map/ppermute | solution.py:539
  (88 other events, 1593.6 us)
Sparse Core Ops, SparseCore 0:
  11.5 97.7 all-gather.3
  112.2 191.6 all-gather.5
  305.8 123.9 all-gather.7

commit v2 on v1

--- a/solution.py
+++ b/solution.py
@@ -378,6 +378,8 @@
 
 BF16 = jnp.bfloat16
 F32 = jnp.float32
+MESH = pl.DeviceIdType.MESH
+GROUPS = 64
 
 
 def dot32(left, right, contract):
@@ -405,47 +407,6 @@
     weights = jnp.exp(scores - row_max)
     total = jnp.sum(weights, axis=-1, keepdims=True)
     return weights * (1.0 / total)
-
-
-def attend_kernel(
-    plan,
-    query_lin_ref,
-    keys_ref,
-    values_ref,
-    place_ref,
-    segment_ref,
-    key_segment_ref,
-    cosine_ref,
-    sine_ref,
-    attended_ref,
-    queries_ref,
-):
-    blocks, rows, pair, heads, head_dim, score_scale = plan
-    for block in range(blocks):
-        start = block * rows
-        extent = (block + 1) * pair * rows
-        cosine, sine = cosine_ref[pl.ds(start, rows), :], sine_ref[pl.ds(start, rows), :]
-        turned = []
-        for h in range(heads):
-            part = query_lin_ref[pl.ds(start, rows), pl.ds(h * head_dim, head_dim)]
-            part = turn(part, cosine, sine).astype(BF16)
-            queries_ref[pl.ds(start, rows), pl.ds(h * head_dim, head_dim)] = part
-            turned.append(part)
-        stacked = jnp.concatenate(turned, axis=0)
-        soft = masked_block(
-            stacked,
-            keys_ref[pl.ds(0, extent), :],
-            place_ref[pl.ds(start, rows), :],
-            segment_ref[pl.ds(start, rows), :],
-            key_segment_ref[:, pl.ds(0, extent)],
-            heads,
-            score_scale,
-        ).astype(BF16)
-        mixed = dot32(soft, values_ref[pl.ds(0, extent), :], ((1,), (0,))).astype(BF16)
-        for h in range(heads):
-            attended_ref[pl.ds(start, rows), pl.ds(h * head_dim, head_dim)] = mixed[
-                h * rows : (h + 1) * rows
-            ]
 
 
 def attend_back_kernel(
@@ -559,15 +520,6 @@
     return out
 
 
-def gather_plane(value):
-    half = value.shape[-1] // 2
-    by_x, by_y = send_plane(value, 1), send_plane(value, 2)
-    far = jnp.concatenate(
-        [send_plane(by_x[..., :half], 2), send_plane(by_y[..., half:], 1)], axis=-1
-    )
-    return jnp.concatenate([value, by_x, by_y, far], axis=0)
-
-
 def scatter_plane(value):
     half = value.shape[-1] // 2
     left, right = value[..., :half], value[..., half:]
@@ -580,15 +532,6 @@
     return jnp.concatenate([left, right], axis=-1)
 
 
-def gather_line(value, plane):
-    size = lax.axis_size("dp")
-    out = jnp.zeros((size,) + value.shape, value.dtype)
-    out = put_block(out, value, plane)
-    for step in range(1, size):
-        out = put_block(out, send_line(value, step), (plane + size - step) % size)
-    return out
-
-
 def scatter_line(value, plane):
     size = lax.axis_size("dp")
     total = block_of(value, plane).astype(F32)
@@ -597,13 +540,6 @@
     return total
 
 
-def gather_core(value, core, dim):
-    other = send_core(value)
-    first = jnp.where(core == 0, value, other)
-    second = jnp.where(core == 0, other, value)
-    return jnp.stack([first, second], axis=dim)
-
-
 def scatter_core(value, core, dim):
     other = send_core(block_of(value, 1 - core, dim))
     return (block_of(value, core, dim).astype(F32) + other.astype(F32)).astype(BF16)
@@ -615,6 +551,332 @@
     blocks = jnp.stack([block_of(value, own ^ step, 1) for step in range(chips)])
     value = scatter_plane(blocks).astype(BF16)
     return scatter_line(value, plane)
+
+
+def by_step(blocks, own):
+    return jnp.stack([block_of(blocks, own ^ step) for step in range(4)])
+
+
+class Post:
+    def __init__(self, send_sem, recv_sem):
+        self.plane=lax.axis_index("dp"); self.own=lax.axis_index("seq"); self.core=lax.axis_index("fsdp")
+        self.planes=lax.axis_size("dp")
+        x=lax.rem(self.own,2); y=lax.div(self.own,2)
+        self.by_x=self.own+1-2*x; self.by_y=self.own+2-4*y; self.far=3-self.own
+        z,s,c=self.plane,self.own,self.core
+        self.to_x=(z,self.by_x,c); self.to_y=(z,self.by_y,c); self.to_far=(z,self.far,c)
+        self.to_core=(z,s,1-c)
+        self.to_up=(lax.rem(z+1,self.planes),s,c); self.to_down=(lax.rem(z+self.planes-1,self.planes),s,c)
+        self.has_up=z<self.planes-1; self.has_down=z>0
+        self.send_sem, self.recv_sem = send_sem, recv_sem
+        self.sent=[]
+        self.steps={0:[(z,())]}
+        for k in range(1,self.planes):
+            self.steps[k]=[(jnp.clip(z-k,0,self.planes-1),(z-k>=0,)),(jnp.clip(z+k,0,self.planes-1),(z+k<=self.planes-1,))]
+        self.groups={}
+    def group(self, name):
+        return self.groups.setdefault(name, len(self.groups))
+    def barrier(self):
+        bar=pltpu.get_barrier_semaphore()
+        for t in (self.to_x,self.to_y,self.to_far,self.to_core):
+            pl.semaphore_signal(bar,inc=1,device_id=t,device_id_type=MESH)
+        for chip in (self.by_x,self.by_y,self.far):
+            pl.semaphore_signal(bar,inc=1,device_id=(self.plane,chip,1-self.core),device_id_type=MESH)
+        @pl.when(self.has_up)
+        def _(): pl.semaphore_signal(bar,inc=1,device_id=self.to_up,device_id_type=MESH)
+        @pl.when(self.has_down)
+        def _(): pl.semaphore_signal(bar,inc=1,device_id=self.to_down,device_id_type=MESH)
+        pl.semaphore_wait(bar,7+self.has_up.astype(jnp.int32)+self.has_down.astype(jnp.int32))
+    def copy(self, src, dst, name, index, target, arrive=None):
+        return pltpu.make_async_remote_copy(src_ref=src,dst_ref=dst,
+            send_sem=self.send_sem.at[self.group(name),index],
+            recv_sem=self.recv_sem.at[self.group(arrive or name),index],
+            device_id=target,device_id_type=MESH)
+    def send(self, src, dst, name, index, target, arrive=None, when=()):
+        def go(): self.copy(src,dst,name,index,target,arrive).start()
+        if when:
+            cond=functools.reduce(jnp.logical_and,when)
+            pl.when(cond)(go)
+        else: go()
+        self.sent.append((when,lambda: self.copy(src,dst,name,index,target,arrive).wait_send()))
+    def wait(self, ref, name, index):
+        self.copy(ref,ref,name,index,self.to_core).wait_recv()
+    def finish(self):
+        for when,w in self.sent:
+            if when: pl.when(functools.reduce(jnp.logical_and,when))(w)
+            else: w()
+
+class Line:
+    def __init__(self, post, name, unit, own_source):
+        self.p, self.name, self.unit, self.src = post, name, unit, own_source
+    def start(self):
+        p=self.p
+        p.send(self.src,self.unit(p.plane),self.name+"_up",p.plane,p.to_up,self.name,(p.has_up,))
+        p.send(self.src,self.unit(p.plane),self.name+"_down",p.plane,p.to_down,self.name,(p.has_down,))
+    def hop(self, k, then=None):
+        p=self.p
+        for sign,(at,(here,)) in zip((-1,1),p.steps[k]):
+            on=p.has_up if sign<0 else p.has_down
+            target=p.to_up if sign<0 else p.to_down
+            ref=self.unit(at)
+            @pl.when(here)
+            def _(ref=ref,at=at): p.wait(ref,self.name,at)
+            if k<p.planes-1:
+                p.send(ref,ref,self.name+("_up" if sign<0 else "_down"),at,target,self.name,(here,on))
+            if then: then(at,here)
+
+class Spread:
+    def __init__(self, post, name, unit, low, high):
+        self.p,self.name,self.unit,self.low,self.high=post,name,unit,low,high
+    def start(self, index, source, when=()):
+        p=self.p
+        dst=self.unit(index,p.own)
+        p.send(source,dst,self.name+"_x",index,p.to_x,None,when)
+        p.send(source,dst,self.name+"_y",index,p.to_y,None,when)
+    def relay(self, index, when=()):
+        p=self.p
+        def go(f):
+            if when: pl.when(functools.reduce(jnp.logical_and,when))(f)
+            else: f()
+        go(lambda: p.wait(self.unit(index,p.by_x),self.name+"_x",index))
+        ref=self.low(index,p.by_x)
+        p.send(ref,ref,self.name+"_l",index,p.to_y,None,when)
+        go(lambda: p.wait(self.unit(index,p.by_y),self.name+"_y",index))
+        ref=self.high(index,p.by_y)
+        p.send(ref,ref,self.name+"_h",index,p.to_x,None,when)
+    def arrive(self, index, when=()):
+        p=self.p
+        def go():
+            p.wait(self.low(index,p.far),self.name+"_l",index)
+            p.wait(self.high(index,p.far),self.name+"_h",index)
+        if when: pl.when(functools.reduce(jnp.logical_and,when))(go)
+        else: go()
+
+
+def dot2(l, r, ca, cb):
+    return dot32(l, r, ((ca,), (cb,)))
+
+
+def front_kernel(plan,tok,cot,marks,wq_in,wo_in,gu_in,wd_in,freq,
+    x_out,marks_out,wq_out,wo_out,gu,wd,E,two,middle_out,h1_out,q_out,att_out,kv_out,home,cos_out,sin_out,
+    send_sem,recv_sem,local_sem,b_cot,b_gu,b_wd,
+    x_v,marks_v,wq_v,wo_v,h1_v,lin_v,q_v,att_v,kv_v,mid_v,two_v,cos_v,sin_v,gain_v):
+    tile,width,head_dim,group=plan
+    scale=head_dim**-0.5
+    p=Post(send_sem,recv_sem)
+    z,s,c=p.plane,p.own,p.core
+    chips=4
+    rows=chips*tile
+    groups=width//group; heads=group//head_dim
+    qkv=width+2*head_dim
+    count=[0]
+    outs_=[]
+    def local(src,dst):
+        cp=pltpu.make_async_copy(src,dst,local_sem.at[count[0]]); count[0]+=1
+        cp.start(); return cp
+    def out(src,dst):
+        outs_.append(local(src,dst))
+    loads=[local(tok.at[s],x_v.at[s]),local(marks.at[s],marks_v.at[c,s]),local(wq_in,wq_v.at[z,s,c]),local(wo_in,wo_v.at[z,s,c])]
+    late=[local(cot,b_cot),local(gu_in.at[s],b_gu),local(wd_in,b_wd)]
+    p.barrier()
+    def attention_weight(name, arr, src):
+        n=arr.shape[3]//2
+        spread=Spread(p,name,lambda a,b: arr.at[a,b,c],lambda a,b: arr.at[a,b,c,pl.ds(0,n)],lambda a,b: arr.at[a,b,c,pl.ds(n,n)])
+        line=Line(p,name+"_z",lambda a: arr.at[a,s,c],src)
+        return spread,line
+    q_spread,q_line=attention_weight("wq",wq_v,wq_in)
+    o_spread,o_line=attention_weight("wo",wo_v,wo_in)
+    def each(k, f):
+        for at,when in p.steps[k]: f(at,when)
+    def to_sibling(name, arr, a, when):
+        ref=arr.at[a,:,c]
+        p.send(ref,ref,name+"_c",a,p.to_core,None,when)
+    others=((p.to_x,p.by_x),(p.to_y,p.by_y),(p.to_far,p.far))
+    def swap(src,dst_of,name):
+        for i,(t,o) in enumerate(others):
+            p.send(src.at[o],dst_of(s),name,i,t)
+    def swapped(dst_of,name):
+        for i,(t,o) in enumerate(others):
+            p.wait(dst_of(o),name,i)
+    q_line.start()
+    swap(tok,lambda b: x_v.at[b],"tok")
+    q_spread.start(z,wq_in)
+    for i,(t,o) in enumerate(others):
+        p.send(marks.at[o],marks_v.at[c,s],"mk",i,t)
+        p.send(marks.at[o],marks_v.at[c,s],"mk2",i,(z,o,1-c))
+    p.send(marks.at[s],marks_v.at[c,s],"mk2",3,p.to_core)
+    fwd=lambda a,here: q_spread.start(a,wq_v.at[a,s,c],(here,))
+    wd_line=Line(p,"wd_z",lambda a: wd.at[a,c],wd_in)
+    gu_line=Line(p,"gu_z",lambda a: gu.at[a,:,c],gu.at[z,:,c])
+    q_line.hop(1,fwd)
+    wd_line.start()
+    q_line.hop(2,fwd)
+    q_line.hop(3,fwd)
+    swap(gu_in,lambda b: gu.at[z,b,c],"gu")
+    for cp in loads+late: cp.wait()
+    out(b_cot,E.at[:,s]); out(b_gu,gu.at[z,s,c]); own_gu=outs_[-1]; out(b_wd,wd.at[z,c]); own_wd=outs_[-1]
+    for k in range(4): each(k,lambda a,w: q_spread.relay(a,w))
+    o_line.start(); o_spread.start(z,wo_in)
+    def each_q(a,w):
+        q_spread.arrive(a,w); to_sibling("wq",wq_v,a,w)
+    for k in range(4): each(k,each_q)
+    swapped(lambda b: x_v.at[b],"tok")
+    for i,(t,o) in enumerate(others):
+        p.wait(marks_v.at[c,o],"mk",i); p.wait(marks_v.at[1-c,o],"mk2",i)
+    p.wait(marks_v.at[1-c,s],"mk2",3)
+    swapped(lambda b: gu.at[z,b,c],"gu")
+    own_gu.wait(); outs_[:]=[o for o in outs_ if o is not own_gu]
+    gu_line.start(); to_sibling("gu",gu,z,())
+    for a in range(4): p.wait(wq_v.at[a,:,1-c],"wq_c",a)
+    out(x_v,x_out); out(marks_v,marks_out); out(wq_v,wq_out)
+    ofwd=lambda a,here: o_spread.start(a,wo_v.at[a,s,c],(here,))
+    gufwd=lambda a,here: to_sibling("gu",gu,a,(here,))
+    e_parts=[]
+    for i in range(2):
+        def sub(lo,n,i=i): return lambda _,b: E.at[pl.ds(2*i+lo,n),b]
+        e_parts.append(Spread(p,"E%d"%i,sub(0,2),sub(0,1),sub(1,1)))
+    def e_start(i):
+        for t,nm in ((p.to_x,"_x"),(p.to_y,"_y")):
+            p.send(cot.at[pl.ds(2*i,2)],E.at[pl.ds(2*i,2),s],"E%d"%i+nm,0,t)
+    for i in range(width//head_dim):
+        a,b=divmod(i,4)
+        block=wq_v[a,b,:,:,pl.ds(qkv,head_dim)].reshape(head_dim,head_dim).astype(F32)
+        gain_v[:,pl.ds(i*head_dim,head_dim)]=jnp.transpose(block)[0:8]
+    def norm_block(b,carry):
+        x=x_v[b].astype(F32)
+        inv=lax.rsqrt(jnp.mean(x*x,axis=-1,keepdims=True)+EPSILON)
+        h1_v[pl.ds(b*tile,tile),:]=(x*inv*gain_v[0:1,:]).astype(BF16)
+        return carry
+    lax.fori_loop(0,chips,norm_block,0)
+    lane=lax.broadcasted_iota(jnp.int32,(1,head_dim),1)
+    sign=jnp.where(lane<head_dim//2,-1.0,1.0).astype(F32)
+    seg_cols=[]
+    for b in range(chips):
+        m=jnp.transpose(marks_v[c,b].astype(F32))
+        angle=m[:,1:2]*freq[...]
+        cos_v[pl.ds(b*tile,tile),:]=jnp.cos(angle); sin_v[pl.ds(b*tile,tile),:]=jnp.sin(angle)*sign
+        seg_cols.append(m[:,0:1])
+    key_seg=jnp.concatenate([marks_v[k%2,k//2,0:1,:] for k in range(2*chips)],axis=1).astype(F32)
+    o_line.hop(1,ofwd)
+    w=wq_v[:,:,:,:,pl.ds(width,2*head_dim)].reshape(width,2*head_dim)
+    kv=dot2(h1_v[...],w,1,0)
+    kv=jnp.concatenate([turn(kv[:,:head_dim],cos_v[...],sin_v[...]),kv[:,head_dim:]],axis=1).astype(BF16)
+    kv_v[:,pl.ds(c,1)]=kv.reshape(chips,1,tile,2*head_dim)
+    p.send(kv_v.at[:,c],kv_v.at[:,c],"kv",0,p.to_core)
+    swap(kv_v.at[:,c],lambda b: home.at[b],"home")
+    out(kv_v.at[s,c],home.at[s]); out(h1_v,h1_out); out(cos_v,cos_out); out(sin_v,sin_out)
+    steps={0:[lambda: o_line.hop(2,ofwd)],
+           1:[lambda: p.wait(kv_v.at[:,1-c],"kv",0), lambda: o_line.hop(3,ofwd)],
+           2:[lambda: wd_line.hop(1), lambda: each(0,lambda a,w: o_spread.relay(a,w)), lambda: each(1,lambda a,w: o_spread.relay(a,w))],
+           3:[lambda: each(2,lambda a,w: o_spread.relay(a,w)), lambda: each(3,lambda a,w: o_spread.relay(a,w)),lambda: gu_line.hop(1,gufwd)],
+           4:[lambda: wd_line.hop(2), lambda: e_start(0)]}
+    def lin_group(g,carry):
+        w=wq_v[:,:,:,:,pl.ds(pl.multiple_of(g*group,group),group)].reshape(width,group)
+        lin_v[...]=dot2(h1_v[...],w,1,0)
+        for b in range(chips):
+            cos,sin=cos_v[pl.ds(b*tile,tile),:],sin_v[pl.ds(b*tile,tile),:]
+            for h in range(heads):
+                part=lin_v[pl.ds(b*tile,tile),pl.ds(h*head_dim,head_dim)]
+                q_v[pl.ds(b*tile,tile),pl.ds(pl.multiple_of(g*group+h*head_dim,head_dim),head_dim)]=turn(part,cos,sin).astype(BF16)
+        return carry
+    for f in steps[0]: f()
+    lax.fori_loop(0,groups,lin_group,0)
+    for f in steps[1]: f()
+    out(kv_v,kv_out); out(q_v,q_out)
+    def attend_group(g,carry):
+        for b in range(chips):
+            extent=(b+1)*2*tile
+            at=lambda h: pl.ds(pl.multiple_of(g*group+h*head_dim,head_dim),head_dim)
+            q=jnp.concatenate([q_v[pl.ds(b*tile,tile),at(h)] for h in range(heads)],axis=0)
+            kvs=kv_v[pl.ds(0,b+1)].reshape(extent,2*head_dim)
+            place=(2*b+c)*tile+lax.broadcasted_iota(jnp.int32,(tile,extent),0)
+            seen=lax.broadcasted_iota(jnp.int32,(tile,extent),1)
+            allowed=(place>=seen)&(seg_cols[b]==key_seg[:,:extent])
+            bias=jnp.where(allowed,0.0,MASKED).astype(F32)
+            sc=dot2(q,kvs[:,:head_dim],1,1)*scale
+            sc=(sc.reshape(heads,tile,extent)+bias[None]).reshape(heads*tile,extent)
+            top=jnp.max(sc,axis=-1,keepdims=True)
+            e=jnp.exp(sc-top)
+            soft=(e*(1.0/jnp.sum(e,axis=-1,keepdims=True))).astype(BF16)
+            mixed=dot2(soft,kvs[:,head_dim:],1,0).astype(BF16)
+            for h in range(heads):
+                att_v[pl.ds(b*tile,tile),at(h)]=mixed[h*tile:(h+1)*tile]
+        for i in (2,3):
+            @pl.when(g==i-1)
+            def _(i=i):
+                for f in steps[i]: f()
+        return carry
+    lax.fori_loop(0,groups,attend_group,0)
+    out(att_v,att_out)
+    def each_o(a,w):
+        o_spread.arrive(a,w); to_sibling("wo",wo_v,a,w)
+    for k in range(4): each(k,each_o)
+    for f in steps[4]: f()
+    for a in range(4): p.wait(wo_v.at[a,:,1-c],"wo_c",a)
+    out(wo_v,wo_out)
+    def project(g,carry):
+        at=pl.ds(pl.multiple_of(g*group,group),group)
+        w=wo_v[:,:,:,:,at].reshape(width,group)
+        lin_v[...]=dot2(att_v[...],w,1,0)
+        for b in range(chips):
+            mid_v[pl.ds(b*tile,tile),at]=x_v[b,:,at].astype(F32)+lin_v[pl.ds(b*tile,tile),:]
+        return carry
+    lax.fori_loop(0,groups,project,0)
+    out(mid_v,middle_out)
+    def norm_two(b,carry):
+        at=pl.ds(pl.multiple_of(b*tile,tile),tile)
+        m=mid_v[at,:]
+        inv=lax.rsqrt(jnp.mean(m*m,axis=-1,keepdims=True)+EPSILON)
+        two_v[at,:]=(m*inv*gain_v[1:2,:]).astype(BF16)
+        return carry
+    lax.fori_loop(0,chips,norm_two,0)
+    half=rows//2
+    two_spread=Spread(p,"two",lambda _,b: two.at[b],lambda _,b: two.at[b,pl.ds(0,half)],lambda _,b: two.at[b,pl.ds(half,half)])
+    two_spread.start(0,two_v)
+    out(two_v,two.at[s])
+    e_start(1)
+    wd_line.hop(3)
+    gu_line.hop(2,gufwd)
+    e_parts[0].relay(0)
+    own_wd.wait(); outs_[:]=[o for o in outs_ if o is not own_wd]
+    p.send(wd.at[:,c],wd.at[:,c],"wd_c",0,p.to_core)
+    gu_line.hop(3,gufwd)
+    two_spread.relay(0)
+    e_parts[0].arrive(0)
+    e_parts[1].relay(0)
+    two_spread.arrive(0)
+    e_parts[1].arrive(0)
+    p.wait(wd.at[:,1-c],"wd_c",0)
+    for a in range(4): p.wait(gu.at[a,:,1-c],"gu_c",a)
+    swapped(lambda b: home.at[b],"home")
+    for cp in outs_: cp.wait()
+    p.finish()
+    assert len(p.groups)<=GROUPS, len(p.groups)
+
+def front(tok,cot,marks,wq_in,wo_in,gu_in,wd_in):
+    Z,S,C=lax.axis_size("dp"),lax.axis_size("seq"),lax.axis_size("fsdp")
+    sd=jax.ShapeDtypeStruct
+    micro,tile,width=tok.shape
+    rows=micro*tile
+    head_dim=128
+    group=512
+    half=head_dim//2
+    freq=jnp.exp(-jnp.log(jnp.float32(10000.0))*jnp.arange(half,dtype=F32)/half)
+    freq=jnp.concatenate([freq,freq])[None]
+    outs=[sd((S,tile,width),BF16),sd((C,)+marks.shape,jnp.int32),sd((Z,S,C)+wq_in.shape,BF16),sd((Z,S,C)+wo_in.shape,BF16),
+          sd((Z,S,C)+gu_in.shape[1:],BF16),sd((Z,C)+wd_in.shape,BF16),sd((S,)+cot.shape,BF16),
+          sd((S,rows,width),BF16),sd((rows,width),F32),sd((rows,width),BF16),sd((rows,width),BF16),sd((rows,width),BF16),
+          sd((S,C,tile,2*head_dim),BF16),sd((S,tile,2*head_dim),BF16),sd((rows,head_dim),F32),sd((rows,head_dim),F32)]
+    anyspec=pl.BlockSpec(memory_space=pl.ANY)
+    V=pltpu.VMEM
+    return pl.pallas_call(functools.partial(front_kernel,(tile,width,head_dim,group)),out_shape=outs,
+        in_specs=[anyspec]*7+[pl.BlockSpec(memory_space=V)],out_specs=[anyspec]*len(outs),
+        scratch_shapes=[pltpu.SemaphoreType.DMA((GROUPS,4)),pltpu.SemaphoreType.DMA((GROUPS,4)),pltpu.SemaphoreType.DMA((32,)),
+          V(cot.shape,BF16),V(gu_in.shape[1:],BF16),V(wd_in.shape,BF16),
+          V((S,tile,width),BF16),V((C,)+marks.shape,jnp.int32),V((Z,S,C)+wq_in.shape,BF16),V((Z,S,C)+wo_in.shape,BF16),
+          V((rows,width),BF16),V((rows,group),F32),V((rows,width),BF16),V((rows,width),BF16),V((S,C,tile,2*head_dim),BF16),
+          V((rows,width),F32),V((rows,width),BF16),V((rows,head_dim),F32),V((rows,head_dim),F32),V((8,width),F32)],
+        compiler_params=pltpu.CompilerParams(collective_id=1,has_side_effects=True,vmem_limit_bytes=60*1024*1024),name="front")(tok,cot,marks,wq_in,wo_in,gu_in,wd_in,freq)
 
 
 def body_plane(
@@ -648,82 +910,64 @@
     piece = own_hidden // planes
     qkv = width + 2 * head_dim
     score_scale = 1.0 / math.sqrt(head_dim)
-    every = ("dp", "seq", "fsdp")
 
     gains = jnp.stack([gain_attn, gain_mlp], axis=1)
     gains = jnp.pad(gains, ((0, 0), (0, head_dim - 2)))
-    w_qkv = gather(jnp.concatenate([w_query, w_key, w_value, gains], axis=1), every, 0)
-    out_mat = gather(w_out, every, 0)
+    w_in = jnp.concatenate([w_query, w_key, w_value, gains], axis=1)
     gate_up = jnp.stack([w_gate, w_up], axis=1).reshape(shard, 2, planes, chips, piece)
     gate_up = gate_up.transpose(3, 0, 1, 2, 4).reshape(chips, shard, 2 * own_hidden)
-    w_qkv, gate_up, w_down = lax.optimization_barrier((w_qkv, gate_up, w_down))
-    gate_up = swap_blocks(gate_up, own)
-    gate_up = gather_core(gate_up, core, 1).reshape(pair, -1, 2 * own_hidden)
-    gate_up_half = gather_line(block_of(gate_up, core), plane)
-    gate_up = gather_core(gate_up_half, core, 1).reshape(width, 2 * own_hidden)
-    down_mat = gather_core(gather_line(w_down, plane), core, 1).reshape(own_hidden, width)
-    grads_in = gather(cotangent, "seq", 1).reshape(chips, rows, width)
-    grads_in = jnp.concatenate([block_of(grads_in, own ^ step) for step in range(chips)])
-
+    marks = jnp.pad(jnp.stack([segments, positions], axis=1), ((0, 0), (0, 6), (0, 0)))
+    (
+        x_rows,
+        marks,
+        w_qkv,
+        out_mat,
+        gate_up,
+        down_mat,
+        grads_in,
+        plane_two,
+        middle,
+        hidden_one,
+        queries,
+        attended,
+        kv,
+        kv_home,
+        cosine,
+        sine,
+    ) = front(tokens, cotangent, marks, w_in, w_out, gate_up, w_down)
+    x_rows = x_rows.reshape(rows, width).astype(F32)
+    w_qkv = w_qkv.reshape(width, qkv + head_dim)
     gain_one, gain_two = w_qkv[:, qkv].astype(F32), w_qkv[:, qkv + 1].astype(F32)
-    w_qkv = w_qkv[:, :qkv]
-
-    x_rows = swap_blocks(tokens, own).reshape(rows, width).astype(F32)
-    marks = swap_blocks(jnp.stack([segments, positions], axis=1), own)
-    segment_own, place_doc = marks[:, 0], marks[:, 1].reshape(rows)
-    key_segment = gather_core(segment_own, core, 1).reshape(1, rows * pair)
+    out_mat = out_mat.reshape(width, width)
+    gate_up = gate_up.reshape(width, 2 * own_hidden)
+    down_mat = down_mat.reshape(own_hidden, width)
+    grads_in = grads_in.reshape(chips * rows, width)
+    plane_two = plane_two.reshape(chips * rows, width)
+    kv = kv.reshape(rows * pair, 2 * head_dim)
+    keys, values = kv[:, :head_dim], kv[:, head_dim:]
+    query_segment = block_of(marks, core)[:, 0].reshape(rows, 1)
+    key_segment = marks[:, :, 0].transpose(1, 0, 2).reshape(1, rows * pair)
     query_place = (
         (jnp.arange(chips, dtype=jnp.int32)[:, None] * pair + core) * tile
         + jnp.arange(tile, dtype=jnp.int32)[None, :]
     ).reshape(rows, 1)
-    query_segment = segment_own.reshape(rows, 1)
-    cosine, sine = rope_tables(place_doc, head_dim // 2)
-    cosine = jnp.concatenate([cosine, cosine], axis=1)
-    sine = jnp.concatenate([-sine, sine], axis=1)
-
-    inverse_one = lax.rsqrt(jnp.mean(x_rows * x_rows, axis=-1, keepdims=True) + EPSILON)
-    normed_one = x_rows * inverse_one
-    hidden_one = (normed_one * gain_one).astype(BF16)
-    lin = jnp.dot(hidden_one, w_qkv, preferred_element_type=F32)
-    query_lin, key_lin, value_lin = (
-        lin[:, :width],
-        lin[:, width : width + head_dim],
-        lin[:, width + head_dim :],
-    )
-    keys_own = (key_lin * cosine + jnp.roll(key_lin, head_dim // 2, axis=1) * sine).astype(BF16)
-    values_own = value_lin.astype(BF16)
-    kv_own = jnp.concatenate([keys_own, values_own], axis=1).reshape(chips, tile, 2 * head_dim)
-    kv = gather_core(kv_own, core, 1).reshape(rows * pair, 2 * head_dim)
-    keys, values = kv[:, :head_dim], kv[:, head_dim:]
-    kv_home = swap_blocks(kv_own, own)
     groups = max(1, head_count // 4)
     heads = head_count // groups
     plan = (chips, tile, pair, heads, head_dim, score_scale)
     pairs_seen = tile * tile * pair * chips * (chips + 1) // 2 * head_count * head_dim
     narrow = (keys, values, query_place, query_segment, key_segment, cosine, sine)
-    attended, queries = attention_call(
-        attend_kernel,
-        plan,
-        groups,
-        (query_lin,),
-        narrow,
-        [jax.ShapeDtypeStruct((rows, width), BF16)] * 2,
-        "attend",
-        4 * pairs_seen,
-    )
-    middle = x_rows + jnp.dot(attended, out_mat, preferred_element_type=F32)
+    inverse_one = lax.rsqrt(jnp.mean(x_rows * x_rows, axis=-1, keepdims=True) + EPSILON)
+    normed_one = x_rows * inverse_one
     inverse_two = lax.rsqrt(jnp.mean(middle * middle, axis=-1, keepdims=True) + EPSILON)
     normed_two = middle * inverse_two
-    hidden_two = (normed_two * gain_two).astype(BF16)
-
-    plane_two = gather_plane(hidden_two)
+
     gate_up_lin = jnp.dot(plane_two, gate_up, preferred_element_type=F32)
     gate_proj, up_proj = gate_up_lin[:, :own_hidden], gate_up_lin[:, own_hidden:]
     gate_sigmoid = jax.nn.sigmoid(gate_proj)
     gate_silu = gate_proj * gate_sigmoid
     hidden_mlp = (gate_silu * up_proj).astype(BF16)
     partial_out = jnp.dot(hidden_mlp, down_mat, preferred_element_type=F32).astype(BF16)
-    result = middle + scatter_plane(partial_out.reshape(chips, rows, width))
+    result = middle + scatter_plane(by_step(partial_out.reshape(chips, rows, width), own))
     layer_rows = swap_blocks(result.astype(BF16).reshape(chips, tile, width), own)
 
     grad_hidden = dot32(grads_in, down_mat, ((1,), (1,)))
@@ -733,7 +977,7 @@
     grad_up_pre = (grad_hidden * gate_silu).astype(BF16)
     grad_pre = jnp.concatenate([grad_gate_pre, grad_up_pre], axis=1)
     partial_two = dot32(grad_pre, gate_up, ((1,), (1,))).astype(BF16)
-    grad_hidden_two = scatter_plane(partial_two.reshape(chips, rows, width))
+    grad_hidden_two = scatter_plane(by_step(partial_two.reshape(chips, rows, width), own))
     grad_gate_up = dot32(plane_two, grad_pre, ((0,), (0,))).astype(BF16)
     grad_down = dot32(hidden_mlp, grads_in, ((0,), (0,))).astype(BF16)
 
@@ -747,7 +991,7 @@
     grad_gate_up = grad_gate_up.transpose(2, 1, 3, 0, 4).reshape(2, shard, hidden).astype(F32)
 
     grad_gain_two = jnp.sum(grad_hidden_two * normed_two, axis=0)
-    grad_rows = grads_in[:rows].astype(F32)
+    grad_rows = lax.dynamic_slice_in_dim(grads_in, own * rows, rows, axis=0).astype(F32)
     grad_middle = grad_rows + norm_back(grad_hidden_two * gain_two, normed_two, inverse_two)
     grad_proj = grad_middle.astype(BF16)
     grad_mixed = dot32(grad_proj, out_mat, ((1,), (1,))).astype(BF16)
@@ -775,7 +1019,7 @@
         [grad_query_lin, grad_keys.astype(BF16), grad_kv[:, head_dim:].astype(BF16)], axis=1
     )
     grad_out = dot32(attended, grad_proj, ((0,), (0,))).astype(BF16)
-    grad_hidden_one = dot32(grad_lin, w_qkv, ((1,), (1,)))
+    grad_hidden_one = dot32(grad_lin, w_qkv[:, :qkv], ((1,), (1,)))
     grad_gain_one = jnp.sum(grad_hidden_one * normed_one, axis=0)
     grad_input = grad_middle + norm_back(grad_hidden_one * gain_one, normed_one, inverse_one)
     grad_input = swap_blocks(grad_input.astype(BF16).reshape(chips, tile, width), own)

time: 1170 us -> 939 us (0.80)
  waiting for transfers between devices: 559 us -> 206 us
  Pallas kernels: 40.9 us -> 318 us
  local copies, waits for them, and re-layouts: 116 us -> 74.4 us
  starting transfers between devices: 80.8 us -> 46.3 us
  matrix products: 219 us -> 189 us
  other arithmetic: 123 us -> 96 us
  between operations: 15.4 us -> 1.94 us
    pallas_call x0 -> x1, Pallas kernels: none -> 294 us  [front(): pl.pallas_call(functools.partial(front_kernel, (tile, width, head_dim, gr...]
    ppermute x41 -> x25, waiting for transfers between devices: 228 us -> 72.6 us  [send_plane(): return lax.ppermute(value, 'seq', [(i, i ^ step) for i in range(4)])]
    ppermute x18 -> x12, waiting for transfers between devices: 288 us -> 134 us  [send_line(): lax.ppermute(value, 'dp', [(i, (i + step) % size) for i in range(size)])]
    all_gather x3 -> x0, waiting for transfers between devices: 42 us -> none  [gather(): return lax.all_gather(value, axes, axis=dim, tiled=True)]
    another operation x14 -> x5, other arithmetic: 30.5 us -> 8.29 us  [the longest x10 25.9 us: gather_core(): return jnp.stack([first, second], axis=dim)]
    ppermute x41 -> x25, starting transfers between devices: 44.8 us -> 27.1 us  [send_plane(): return lax.ppermute(value, 'seq', [(i, i ^ step) for i in range(4)])]
    pallas_call x2 -> x1, Pallas kernels: 40.9 us -> 24.5 us  [attention_call(): pl.pallas_call(functools.partial(kernel, plan), grid=(groups,), in_specs=...]
    dot_general x2 -> x0, matrix products: 16.3 us -> none  [the longest x1 8.87 us: body_plane(): middle = x_rows + jnp.dot(attended, out_mat, preferred_element_type=F32)]
  transfers between devices with their start and end apart: 72 -> 42, of which waited for: 27 -> 14; matrix products, arithmetic and copies ran while one was open for 26% -> 27% of each run, Pallas kernels for 4% -> 3%
where the time goes in v2:
time: 939 us; the launch traced here: 933 us
  Pallas kernels  318 us (34%)
  waiting for transfers between devices  206 us (22%)
  matrix products  189 us (20%)
  other arithmetic  96 us (10%)
  local copies, waits for them, and re-layouts  74.4 us (8%)
  starting transfers between devices  46.3 us (5%)
    pallas_call x1, Pallas kernels, front(): pl.pallas_call(functools.partial(front_kernel, (tile, width, head_dim, gr...  294 us
    dot_general x8, matrix products, dot32(): lax.dot_general(left, right, ((contract[0], contract[1]), ((), ())), pref...  142 us
    ppermute x12, waiting for transfers between devices, send_line(): lax.ppermute(value, 'dp', [(i, (i + step) % size) for i in range(size)])  134 us
    ppermute x25, waiting for transfers between devices, send_plane(): return lax.ppermute(value, 'seq', [(i, i ^ step) for i in range(4)])  72.6 us
    dot_general x1, matrix products, body_plane(): gate_up_lin = jnp.dot(plane_two, gate_up, preferred_element_type=F32)  32.1 us
    ppermute x25, starting transfers between devices, send_plane(): return lax.ppermute(value, 'seq', [(i, i ^ step) for i in range(4)])  27.1 us
    pallas_call x1, Pallas kernels, attention_call(): pl.pallas_call(functools.partial(kernel, plan), grid=(groups,), in_specs=...  24.5 us
    squeeze x13, local copies, waits for them, and re-layouts, block_of(): return lax.dynamic_index_in_dim(value, index, axis=dim, keepdims=False)  22.8 us
  transfers between devices with their start and end apart: 42, of which 14 were waited for; matrix products, arithmetic and copies ran while one was open for 27% of the time, Pallas kernels for 3%

profile of v2, /device:TPU:0, one launch (start us, length us, event | category | flops | bytes accessed | tf_op | source)
XLA Modules:
  0.0 932.6 jit_solution(731385236762732958)
XLA Ops:
  2.8 2.7 stack.102
  5.8 2.7 stack.101
  13.6 293.5 %front.1 = (bf16[4,128,2048]{2,1,0:T(8,128)(2,1)}, s32[2,4,8,128]{3,2,1,0:T(8,128)}, bf16[4,4,2,64,2432]{4,3,2,1,0:T(8,128)(2,1)}, bf16[4,4,2,64,2048]{4,3,2,1,0...) custom-call(bf16[4,128,2048]{2,1,0:T(8,128)(2,1)} %tok.1, ...), custom_call_target="tpu_custom_call" | custom-call | tf_op jit(solution)/shard_map/front/pallas_call | solution.py:872
  307.1 32.1 %fusion.89 = f32[2048,2816]{1,0:T(8,128)} fusion(bf16[2048,2048]{1,0:T(8,128)(2,1)} %bitcast.289, bf16[2048,2816]{1,0:T(8,128)(2,1)} %bitcast.286), kind=kOutput, calls=%fused_computation.234 | convolution fusion | flops 23622320128 | bytes 42991616 | tf_op jit(solution)/shard_map/dot_general | solution.py:964
  339.2 26.0 %multiply_convert_fusion.1 = (bf16[2048,1408]{1,0:T(8,128)(2,1)}, bf16[2048,1408]{1,0:T(8,128)(2,1)}, bf16[2048,1408]{1,0:T(8,128)(2,1)}) fusion(f32[2048,2816]{1,0:T(8,128)} %fusion.89, bf16[2048,2048]{1,0:T(8,128)(2,1)} %bitcast.272, bf16[1408,2048]{1,0:T(8,128)(2,1)} %bitcast.291), kind=kOutput, calls=%fused_computation.6 | convolution fusion | flops 11854413824 | bytes 54525952 | tf_op jit(solution)/shard_map/dot_general | solution.py:386
  365.3 31.6 %convolution_convert_fusion.5 = bf16[2048,2048]{1,0:T(8,128)(2,1)} fusion(bf16[2048,2816]{1,0:T(8,128)(2,1)} %bitcast.287, bf16[2048,1408]{1,0:T(8,128)(2,1)} %get-tuple-element.58, bf16[2048,1408]{1,0:T(8,128)(2,1)} %get-tuple-element.57), kind=kOutput, calls=%fused_computation.23 | convolution fusion | flops 23649583104 | bytes 31457280 | tf_op jit(solution)/shard_map/dot_general | solution.py:386
  400.5 2.9 constant_dynamic-slice_fusion.5
  406.6 15.2 %convolution_convert_fusion.3 = bf16[2048,2048]{1,0:T(8,128)(2,1)S(1)} fusion(bf16[2048,1408]{1,0:T(8,128)(2,1)} %get-tuple-element.59, bf16[1408,2048]{1,0:T(8,128)(2,1)S(1)} %bitcast.294), kind=kOutput, calls=%fused_computation.21 | convolution fusion | flops 11815354368 | bytes 19922944 | tf_op jit(solution)/shard_map/dot_general | solution.py:969
  428.1 18.1 %convolution_convert_fusion.4 = bf16[1408,2048]{1,0:T(8,128)(2,1)} fusion(bf16[2048,1408]{1,0:T(8,128)(2,1)} %get-tuple-element.59, bf16[2048,2048]{1,0:T(8,128)(2,1)} %bitcast.273), kind=kOutput, calls=%fused_computation.22 | convolution fusion | flops 11814043648 | bytes 19922944 | tf_op jit(solution)/shard_map/dot_general | solution.py:386
  446.2 3.8 dynamic-slice_bitcast_fusion.2
  450.0 31.7 %convolution_convert_fusion = bf16[2048,2816]{1,0:T(8,128)(2,1)} fusion(bf16[2048,2048]{1,0:T(8,128)(2,1)} %bitcast.290, bf16[2048,1408]{1,0:T(8,128)(2,1)} %get-tuple-element.58, bf16[2048,1408]{1,0:T(8,128)(2,1)} %get-tuple-element.57), kind=kOutput, calls=%fused_computation.10 | convolution fusion | flops 23651155968 | bytes 31457280 | tf_op jit(solution)/shard_map/dot_general | solution.py:386
  482.2 2.9 slice_convert_fusion
  490.0 5.7 dynamic-slice_bitcast_fusion
  509.0 3.8 fusion.37
  514.8 3.0 fusion.6
  519.2 9.5 %collective-permute-done.8 = bf16[512,1024]{1,0:T(8,128)(2,1)S(1)} collective-permute-done((bf16[512,1024]{1,0:T(8,128)(2,1)S(1)}, bf16[512,1024]{1,0:T(8,128)(2,1)S(1)}, u32[]{:S(2)}, u32[]{:S(2)}) %collective-permute-start.8) | collective-permute-done | bytes 1048608 | tf_op jit(solution)/shard_map/ppermute | solution.py:495
  532.8 3.0 fusion.20
  537.0 13.3 %collective-permute-done.1 = bf16[512,1024]{1,0:T(8,128)(2,1)S(1)} collective-permute-done((bf16[512,1024]{1,0:T(8,128)(2,1)}, bf16[512,1024]{1,0:T(8,128)(2,1)S(1)}, u32[]{:S(2)}, u32[]{:S(2)}) %collective-permute-start.1) | collective-permute-done | bytes 1048608 | tf_op jit(solution)/shard_map/ppermute | solution.py:495
  551.7 3.2 fusion.26
  554.9 3.5 multiply_add_fusion
  560.3 9.2 convolution_convert_fusion.6.grad_ref
  569.6 6.8 convolution_convert_fusion.2
  576.4 24.5 %attend_back.1 = (bf16[512,2048]{1,0:T(8,128)(2,1)S(1)}, f32[1024,128]{1,0:T(8,128)S(1)}, f32[1024,128]{1,0:T(8,128)S(1)}) custom-call(bf16[512,2048]{1,0:T(8,128)(2,1)} %get-tuple-element.40.queries_ref, bf16[512,2048]{1,0:T(8,128)(2,1)} %convolution_convert_fusion.6.grad_ref, bf16[1024,128]{1,0:T(8,128)(2,1)S(1)} %get-tuple-element.120.keys_ref, ...), custom_call_target="tpu_custom_call" | custom-call | flops 6710886400 | bytes 6291456 | tf_op jit(solution)/shard_map/attend_back/pallas_call | solution.py:472
  601.1 4.7 dynamic-slice_bitcast_fusion.1
  606.4 3.1 fusion.28
  613.4 10.9 %multiply_reduce_fusion.1 = (bf16[2048]{0:T(1024)(128)(2,1)S(1)}, f32[512]{0:T(512)S(1)}, f32[512,2048]{1,0:T(8,128)}) fusion(bf16[4,128,2048]{2,1,0:T(8,128)(2,1)S(1)} %copy-done.8, f32[512]{0:T(512)S(1)} %rsqrt_bitcast_fusion, f32[2048]{0:T(1024)S(1)} %bitcast.280, bf16[2048,2432]{1,0:T(8,128)(2,1)} %bitcast.277, bf16[512,128]{1,0:T(8,128)(2,1)S(1)} %slice.499, ...), kind=kOutput, calls=%fused_computation.37 | convolution fusion | flops 4846253568 | bytes 18104320 | tf_op jit(solution)/shard_map/dot_general | solution.py:386
  624.3 3.5 add_convert_fusion
  629.8 7.7 convolution_convert_fusion.1
  637.9 5.0 fusion.8
  646.6 6.0 fusion
  653.0 2.5 collective-permute-start.34
  655.4 13.2 %collective-permute-done.13 = bf16[128,2048]{1,0:T(8,128)(2,1)} collective-permute-done((bf16[128,2048]{1,0:T(8,128)(2,1)S(1)}, bf16[128,2048]{1,0:T(8,128)(2,1)}, u32[]{:S(2)}, u32[]{:S(2)}) %collective-permute-start.13) | collective-permute-done | bytes 524320 | tf_op jit(solution)/shard_map/ppermute | solution.py:495
  675.6 2.5 convert_element_type.406
  678.2 9.3 %collective-permute-done.34 = bf16[4,64,2816]{2,1,0:T(8,128)(2,1)S(1)} collective-permute-done((bf16[4,64,2816]{2,1,0:T(8,128)(2,1)S(1)}, bf16[4,64,2816]{2,1,0:T(8,128)(2,1)S(1)}, u32[]{:S(2)}, u32[]{:S(2)}) %collective-permute-start.34) | collective-permute-done | bytes 1441824 | tf_op jit(solution)/shard_map/ppermute | solution.py:500
  687.5 90.4 %collective-permute-done.33 = bf16[4,64,2816]{2,1,0:T(8,128)(2,1)S(1)} collective-permute-done((bf16[4,64,2816]{2,1,0:T(8,128)(2,1)S(1)}, bf16[4,64,2816]{2,1,0:T(8,128)(2,1)S(1)}, u32[]{:S(2)}, u32[]{:S(2)}) %collective-permute-start.33) | collective-permute-done | bytes 1441824 | tf_op jit(solution)/shard_map/ppermute | solution.py:500
  782.4 5.6 fusion.5
  802.8 3.9 fusion.2
  813.5 18.3 %collective-permute-done.37 = bf16[64,2816]{1,0:T(8,128)(2,1)S(1)} collective-permute-done((bf16[64,2816]{1,0:T(8,128)(2,1)S(1)}, bf16[64,2816]{1,0:T(8,128)(2,1)S(1)}, u32[]{:S(2)}, u32[]{:S(2)}) %collective-permute-start.37) | collective-permute-done | bytes 360480 | tf_op jit(solution)/shard_map/ppermute | solution.py:495
  832.5 4.1 reshape.274
  846.0 14.4 %collective-permute-done.18 = bf16[2,4,64,1216]{3,2,1,0:T(8,128)(2,1)} collective-permute-done((bf16[2,4,64,1216]{3,2,1,0:T(8,128)(2,1)}, bf16[2,4,64,1216]{3,2,1,0:T(8,128)(2,1)}, u32[]{:S(2)}, u32[]{:S(2)}) %collective-permute-start.18) | collective-permute-done | bytes 1245216 | tf_op jit(solution)/shard_map/ppermute | solution.py:495
  871.5 3.5 squeeze.197
  875.0 3.5 squeeze.198
  878.5 2.9 fusion.44
  881.5 4.3 collective-permute-start.29
  891.5 3.4 collective-permute-done.30
  895.0 3.3 collective-permute-start.20
  898.2 22.3 %collective-permute-done.29 = bf16[64,2048]{1,0:T(8,128)(2,1)S(1)} collective-permute-done((bf16[64,2048]{1,0:T(8,128)(2,1)S(1)}, bf16[64,2048]{1,0:T(8,128)(2,1)S(1)}, u32[]{:S(2)}, u32[]{:S(2)}) %collective-permute-start.29) | collective-permute-done | bytes 262176 | tf_op jit(solution)/shard_map/ppermute | solution.py:500
  921.5 8.3 collective-permute-done.21
  (246 shorter events, 125.4 us)
Async XLA Ops:
  400.1 95.6 %collective-permute-start.7 = (bf16[2,512,1024]{2,1,0:T(8,128)(2,1)}, bf16[2,512,1024]{2,1,0:T(8,128)(2,1)}, u32[]{:S(2)}, u32[]{:S(2)}) collective-permute-start(bf16[2,512,1024]{2,1,0:T(8,128)(2,1)} %pad_maximum_fusion.8), channel_id=1, source_target_pairs={{0,2},{2,0},{4,6},{6,4},{1,3},{3,1},{5,7},{7,5},{8,10},{10,8},{12,... | collective-permute-start | bytes 6291464 | tf_op jit(solution)/shard_map/ppermute | solution.py:495
  405.0 93.2 %collective-permute-start.9 = (bf16[2,512,1024]{2,1,0:T(8,128)(2,1)}, bf16[2,512,1024]{2,1,0:T(8,128)(2,1)}, u32[]{:S(2)}, u32[]{:S(2)}) collective-permute-start(bf16[2,512,1024]{2,1,0:T(8,128)(2,1)} %pad_maximum_fusion.5), channel_id=1, source_target_pairs={{0,4},{2,6},{4,0},{6,2},{1,5},{3,7},{5,1},{7,3},{8,12},{10,14},{12... | collective-permute-start | bytes 6291464 | tf_op jit(solution)/shard_map/ppermute | solution.py:495
  423.9 80.4 %collective-permute-start = (bf16[2,512,1024]{2,1,0:T(8,128)(2,1)}, bf16[2,512,1024]{2,1,0:T(8,128)(2,1)}, u32[]{:S(2)}, u32[]{:S(2)}) collective-permute-start(bf16[2,512,1024]{2,1,0:T(8,128)(2,1)} %pad_maximum_fusion.7), channel_id=1, source_target_pairs={{0,2},{2,0},{4,6},{6,4},{1,3},{3,1},{5,7},{7,5},{8,10},{10,8},{12,... | collective-permute-start | bytes 6291464 | tf_op jit(solution)/shard_map/ppermute | solution.py:495
  427.7 79.1 %collective-permute-start.2 = (bf16[2,512,1024]{2,1,0:T(8,128)(2,1)}, bf16[2,512,1024]{2,1,0:T(8,128)(2,1)}, u32[]{:S(2)}, u32[]{:S(2)}) collective-permute-start(bf16[2,512,1024]{2,1,0:T(8,128)(2,1)} %pad_maximum_fusion.6), channel_id=1, source_target_pairs={{0,4},{2,6},{4,0},{6,2},{1,5},{3,7},{5,1},{7,3},{8,12},{10,14},{12... | collective-permute-start | bytes 6291464 | tf_op jit(solution)/shard_map/ppermute | solution.py:495
  450.0 64.3 %collective-permute-start.38 = (bf16[4,176,2048]{2,1,0:T(8,128)(2,1)}, bf16[4,176,2048]{2,1,0:T(8,128)(2,1)}, u32[]{:S(2)}, u32[]{:S(2)}) collective-permute-start(bf16[4,176,2048]{2,1,0:T(8,128)(2,1)} %dynamic-slice_bitcast_fusion.2), channel_id=1, source_target_pairs={{0,1},{1,0},{2,3},{3,2},{4,5},{5,4},{6,7},{7,6},{8,9},{9,8},{10,11... | collective-permute-start | bytes 8650760 | tf_op jit(solution)/shard_map/ppermute | solution.py:504
  450.0 31.8 %copy-start.2 = (f32[512,2048]{1,0:T(8,128)S(1)}, f32[512,2048]{1,0:T(8,128)}, u32[]{:S(2)}) copy-start(f32[512,2048]{1,0:T(8,128)} %get-tuple-element.32) | copy-start | bytes 12582916
  495.7 149.4 %collective-permute-start.31 = (bf16[4,4,64,2816]{3,2,1,0:T(8,128)(2,1)}, bf16[4,4,64,2816]{3,2,1,0:T(8,128)(2,1)}, u32[]{:S(2)}, u32[]{:S(2)}) collective-permute-start(bf16[4,4,64,2816]{3,2,1,0:T(8,128)(2,1)} %dynamic-slice_bitcast_fusion), channel_id=1, source_target_pairs={{0,1},{1,0},{2,3},{3,2},{4,5},{5,4},{6,7},{7,6},{8,9},{9,8},{10,11... | collective-permute-start | bytes 17301512 | tf_op jit(solution)/shard_map/ppermute | solution.py:504
  502.6 26.1 %collective-permute-start.8 = (bf16[512,1024]{1,0:T(8,128)(2,1)S(1)}, bf16[512,1024]{1,0:T(8,128)(2,1)S(1)}, u32[]{:S(2)}, u32[]{:S(2)}) collective-permute-start(bf16[512,1024]{1,0:T(8,128)(2,1)S(1)} %get-tuple-element.64), channel_id=1, source_target_pairs={{0,4},{2,6},{4,0},{6,2},{1,5},{3,7},{5,1},{7,3},{8,12},{10,14},{12... | collective-permute-start | bytes 3145736 | tf_op jit(solution)/shard_map/ppermute | solution.py:495
  504.3 26.1 %collective-permute-start.10 = (bf16[512,1024]{1,0:T(8,128)(2,1)S(1)}, bf16[512,1024]{1,0:T(8,128)(2,1)S(1)}, u32[]{:S(2)}, u32[]{:S(2)}) collective-permute-start(bf16[512,1024]{1,0:T(8,128)(2,1)S(1)} %get-tuple-element.65), channel_id=1, source_target_pairs={{0,2},{2,0},{4,6},{6,4},{1,3},{3,1},{5,7},{7,5},{8,10},{10,8},{12,... | collective-permute-start | bytes 3145736 | tf_op jit(solution)/shard_map/ppermute | solution.py:495
  512.8 37.4 %collective-permute-start.1 = (bf16[512,1024]{1,0:T(8,128)(2,1)}, bf16[512,1024]{1,0:T(8,128)(2,1)S(1)}, u32[]{:S(2)}, u32[]{:S(2)}) collective-permute-start(bf16[512,1024]{1,0:T(8,128)(2,1)} %get-tuple-element.72), channel_id=1, source_target_pairs={{0,4},{2,6},{4,0},{6,2},{1,5},{3,7},{5,1},{7,3},{8,12},{10,14},{12... | collective-permute-start | bytes 3145736 | tf_op jit(solution)/shard_map/ppermute | solution.py:495
  514.3 37.3 %collective-permute-start.3 = (bf16[512,1024]{1,0:T(8,128)(2,1)}, bf16[512,1024]{1,0:T(8,128)(2,1)}, u32[]{:S(2)}, u32[]{:S(2)}) collective-permute-start(bf16[512,1024]{1,0:T(8,128)(2,1)} %get-tuple-element.73), channel_id=1, source_target_pairs={{0,2},{2,0},{4,6},{6,4},{1,3},{3,1},{5,7},{7,5},{8,10},{10,8},{12,... | collective-permute-start | bytes 3145736 | tf_op jit(solution)/shard_map/ppermute | solution.py:495
  528.7 77.1 %collective-permute-start.41 = (bf16[176,2048]{1,0:T(8,128)(2,1)}, bf16[176,2048]{1,0:T(8,128)(2,1)}, u32[]{:S(2)}, u32[]{:S(2)}) collective-permute-start(bf16[176,2048]{1,0:T(8,128)(2,1)} %get-tuple-element.94), channel_id=1, source_target_pairs={{0,24},{8,0},{16,8},{24,16},{1,25},{9,1},{17,9},{25,17},{2,26},{10... | collective-permute-start | bytes 2162696 | tf_op jit(solution)/shard_map/ppermute | solution.py:500
  531.3 74.5 %collective-permute-start.40 = (bf16[176,2048]{1,0:T(8,128)(2,1)}, bf16[176,2048]{1,0:T(8,128)(2,1)}, u32[]{:S(2)}, u32[]{:S(2)}) collective-permute-start(bf16[176,2048]{1,0:T(8,128)(2,1)} %get-tuple-element.95), channel_id=1, source_target_pairs={{0,16},{8,24},{16,0},{24,8},{1,17},{9,25},{17,1},{25,9},{2,18},{10... | collective-permute-start | bytes 2162696 | tf_op jit(solution)/shard_map/ppermute | solution.py:500
  550.2 56.1 %collective-permute-start.39 = (bf16[176,2048]{1,0:T(8,128)(2,1)}, bf16[176,2048]{1,0:T(8,128)(2,1)}, u32[]{:S(2)}, u32[]{:S(2)}) collective-permute-start(bf16[176,2048]{1,0:T(8,128)(2,1)} %get-tuple-element.93), channel_id=1, source_target_pairs={{0,8},{8,16},{16,24},{24,0},{1,9},{9,17},{17,25},{25,1},{2,10},{10... | collective-permute-start | bytes 2162696 | tf_op jit(solution)/shard_map/ppermute | solution.py:500
  559.2 50.2 %collective-permute-start.4 = (bf16[128,2048]{1,0:T(8,128)(2,1)}, bf16[128,2048]{1,0:T(8,128)(2,1)S(1)}, u32[]{:S(2)}, u32[]{:S(2)}) collective-permute-start(bf16[128,2048]{1,0:T(8,128)(2,1)} %dynamic-slice_bitcast_fusion.23), channel_id=1, source_target_pairs={{0,2},{2,0},{4,6},{6,4},{1,3},{3,1},{5,7},{7,5},{8,10},{10,8},{12,... | collective-permute-start | bytes 1572872 | tf_op jit(solution)/shard_map/ppermute | solution.py:495
  605.9 7.1 collective-permute-start.11
  605.9 176.5 %collective-permute-start.23 = (bf16[4,4,64,2048]{3,2,1,0:T(8,128)(2,1)}, bf16[4,4,64,2048]{3,2,1,0:T(8,128)(2,1)}, u32[]{:S(2)}, u32[]{:S(2)}) collective-permute-start(bf16[4,4,64,2048]{3,2,1,0:T(8,128)(2,1)} %dynamic-slice_bitcast_fusion.1), channel_id=1, source_target_pairs={{0,1},{1,0},{2,3},{3,2},{4,5},{5,4},{6,7},{7,6},{8,9},{9,8},{10,11... | collective-permute-start | bytes 12582920 | tf_op jit(solution)/shard_map/ppermute | solution.py:504
  610.6 13.7 %copy-start.15 = (bf16[4,128,2048]{2,1,0:T(8,128)(2,1)}, bf16[4,128,2048]{2,1,0:T(8,128)(2,1)S(1)}, u32[]{:S(2)}) copy-start(bf16[4,128,2048]{2,1,0:T(8,128)(2,1)S(1)} %get-tuple-element.101) | copy-start | bytes 6291460
  610.6 42.4 %collective-permute-start.5 = (bf16[128,2048]{1,0:T(8,128)(2,1)}, bf16[128,2048]{1,0:T(8,128)(2,1)}, u32[]{:S(2)}, u32[]{:S(2)}) collective-permute-start(bf16[128,2048]{1,0:T(8,128)(2,1)} %get-tuple-element.100), channel_id=1, source_target_pairs={{0,4},{2,6},{4,0},{6,2},{1,5},{3,7},{5,1},{7,3},{8,12},{10,14},{12... | collective-permute-start | bytes 1572872 | tf_op jit(solution)/shard_map/ppermute | solution.py:495
  611.5 44.0 %collective-permute-start.6 = (bf16[128,2048]{1,0:T(8,128)(2,1)}, bf16[128,2048]{1,0:T(8,128)(2,1)}, u32[]{:S(2)}, u32[]{:S(2)}) collective-permute-start(bf16[128,2048]{1,0:T(8,128)(2,1)} %get-tuple-element.99), channel_id=1, source_target_pairs={{0,6},{2,4},{4,2},{6,0},{1,7},{3,5},{5,3},{7,1},{8,14},{10,12},{12... | collective-permute-start | bytes 1572872 | tf_op jit(solution)/shard_map/ppermute | solution.py:495
  628.6 14.3 %collective-permute-start.12 = (bf16[128,2048]{1,0:T(8,128)(2,1)}, bf16[128,2048]{1,0:T(8,128)(2,1)}, u32[]{:S(2)}, u32[]{:S(2)}) collective-permute-start(bf16[128,2048]{1,0:T(8,128)(2,1)} %dynamic-slice_bitcast_fusion.19), channel_id=1, source_target_pairs={{0,2},{2,0},{4,6},{6,4},{1,3},{3,1},{5,7},{7,5},{8,10},{10,8},{12,... | collective-permute-start | bytes 1572872 | tf_op jit(solution)/shard_map/ppermute | solution.py:495
  644.1 24.5 %collective-permute-start.13 = (bf16[128,2048]{1,0:T(8,128)(2,1)S(1)}, bf16[128,2048]{1,0:T(8,128)(2,1)}, u32[]{:S(2)}, u32[]{:S(2)}) collective-permute-start(bf16[128,2048]{1,0:T(8,128)(2,1)S(1)} %get-tuple-element.97), channel_id=1, source_target_pairs={{0,4},{2,6},{4,0},{6,2},{1,5},{3,7},{5,1},{7,3},{8,12},{10,14},{12... | collective-permute-start | bytes 1572872 | tf_op jit(solution)/shard_map/ppermute | solution.py:495
  645.1 26.5 %collective-permute-start.14 = (bf16[128,2048]{1,0:T(8,128)(2,1)S(1)}, bf16[128,2048]{1,0:T(8,128)(2,1)}, u32[]{:S(2)}, u32[]{:S(2)}) collective-permute-start(bf16[128,2048]{1,0:T(8,128)(2,1)S(1)} %get-tuple-element.96), channel_id=1, source_target_pairs={{0,6},{2,4},{4,2},{6,0},{1,7},{3,5},{5,3},{7,1},{8,14},{10,12},{12... | collective-permute-start | bytes 1572872 | tf_op jit(solution)/shard_map/ppermute | solution.py:495
  653.0 34.6 %collective-permute-start.34 = (bf16[4,64,2816]{2,1,0:T(8,128)(2,1)S(1)}, bf16[4,64,2816]{2,1,0:T(8,128)(2,1)S(1)}, u32[]{:S(2)}, u32[]{:S(2)}) collective-permute-start(bf16[4,64,2816]{2,1,0:T(8,128)(2,1)S(1)} %get-tuple-element.79), channel_id=1, source_target_pairs={{0,24},{8,0},{16,8},{24,16},{1,25},{9,1},{17,9},{25,17},{2,26},{10... | collective-permute-start | bytes 4325384 | tf_op jit(solution)/shard_map/ppermute | solution.py:500
  655.4 122.5 %collective-permute-start.33 = (bf16[4,64,2816]{2,1,0:T(8,128)(2,1)S(1)}, bf16[4,64,2816]{2,1,0:T(8,128)(2,1)S(1)}, u32[]{:S(2)}, u32[]{:S(2)}) collective-permute-start(bf16[4,64,2816]{2,1,0:T(8,128)(2,1)S(1)} %get-tuple-element.80), channel_id=1, source_target_pairs={{0,16},{8,24},{16,0},{24,8},{1,17},{9,25},{17,1},{25,9},{2,18},{10... | collective-permute-start | bytes 4325384 | tf_op jit(solution)/shard_map/ppermute | solution.py:500
  668.6 109.3 %collective-permute-start.32 = (bf16[4,64,2816]{2,1,0:T(8,128)(2,1)S(1)}, bf16[4,64,2816]{2,1,0:T(8,128)(2,1)S(1)}, u32[]{:S(2)}, u32[]{:S(2)}) collective-permute-start(bf16[4,64,2816]{2,1,0:T(8,128)(2,1)S(1)} %get-tuple-element.78), channel_id=1, source_target_pairs={{0,8},{8,16},{16,24},{24,0},{1,9},{9,17},{17,25},{25,1},{2,10},{10... | collective-permute-start | bytes 4325384 | tf_op jit(solution)/shard_map/ppermute | solution.py:500
  671.6 131.2 %collective-permute-start.15 = (bf16[4,4,64,2432]{3,2,1,0:T(8,128)(2,1)}, bf16[4,4,64,2432]{3,2,1,0:T(8,128)(2,1)}, u32[]{:S(2)}, u32[]{:S(2)}) collective-permute-start(bf16[4,4,64,2432]{3,2,1,0:T(8,128)(2,1)} %fusion.8), channel_id=1, source_target_pairs={{0,1},{1,0},{2,3},{3,2},{4,5},{5,4},{6,7},{7,6},{8,9},{9,8},{10,11... | collective-permute-start | bytes 14942216 | tf_op jit(solution)/shard_map/ppermute | solution.py:504
  780.8 8.1 collective-permute-start.35
  782.4 20.3 %slice-start = ((s8[9437184]{0:T(1024)(128)(4,1)}), s8[4194304]{0:T(1024)(128)(4,1)S(1)}, s32[]{:S(2)}) async-start(s8[9437184]{0:T(1024)(128)(4,1)} %bitcast.241), calls=%async_computation | async-start | bytes 8388608
  782.4 20.3 %slice-start.1 = ((s8[9437184]{0:T(1024)(128)(4,1)}), s8[4194304]{0:T(1024)(128)(4,1)S(1)}, s32[]{:S(2)}) async-start(s8[9437184]{0:T(1024)(128)(4,1)} %bitcast.241), calls=%async_computation.1 | async-start | bytes 8388608
  790.8 11.2 %collective-permute-start.36 = (bf16[64,2816]{1,0:T(8,128)(2,1)S(1)}, bf16[64,2816]{1,0:T(8,128)(2,1)S(1)}, u32[]{:S(2)}, u32[]{:S(2)}) collective-permute-start(bf16[64,2816]{1,0:T(8,128)(2,1)S(1)} %get-tuple-element.103), channel_id=1, source_target_pairs={{0,4},{2,6},{4,0},{6,2},{1,5},{3,7},{5,1},{7,3},{8,12},{10,14},{12... | collective-permute-start | bytes 1081352 | tf_op jit(solution)/shard_map/ppermute | solution.py:495
  795.1 43.6 %collective-permute-start.26 = (bf16[2,4,64,1024]{3,2,1,0:T(8,128)(2,1)}, bf16[2,4,64,1024]{3,2,1,0:T(8,128)(2,1)}, u32[]{:S(2)}, u32[]{:S(2)}) collective-permute-start(bf16[2,4,64,1024]{3,2,1,0:T(8,128)(2,1)} %pad_maximum_fusion.11), channel_id=1, source_target_pairs={{0,4},{2,6},{4,0},{6,2},{1,5},{3,7},{5,1},{7,3},{8,12},{10,14},{12... | collective-permute-start | bytes 3145736 | tf_op jit(solution)/shard_map/ppermute | solution.py:495
  796.7 45.1 %collective-permute-start.24 = (bf16[2,4,64,1024]{3,2,1,0:T(8,128)(2,1)}, bf16[2,4,64,1024]{3,2,1,0:T(8,128)(2,1)}, u32[]{:S(2)}, u32[]{:S(2)}) collective-permute-start(bf16[2,4,64,1024]{3,2,1,0:T(8,128)(2,1)} %pad_maximum_fusion.13), channel_id=1, source_target_pairs={{0,2},{2,0},{4,6},{6,4},{1,3},{3,1},{5,7},{7,5},{8,10},{10,8},{12,... | collective-permute-start | bytes 3145736 | tf_op jit(solution)/shard_map/ppermute | solution.py:495
  798.3 33.5 %collective-permute-start.37 = (bf16[64,2816]{1,0:T(8,128)(2,1)S(1)}, bf16[64,2816]{1,0:T(8,128)(2,1)S(1)}, u32[]{:S(2)}, u32[]{:S(2)}) collective-permute-start(bf16[64,2816]{1,0:T(8,128)(2,1)S(1)} %get-tuple-element.102), channel_id=1, source_target_pairs={{0,6},{2,4},{4,2},{6,0},{1,7},{3,5},{5,3},{7,1},{8,14},{10,12},{12... | collective-permute-start | bytes 1081352 | tf_op jit(solution)/shard_map/ppermute | solution.py:495
  810.1 50.3 %collective-permute-start.18 = (bf16[2,4,64,1216]{3,2,1,0:T(8,128)(2,1)}, bf16[2,4,64,1216]{3,2,1,0:T(8,128)(2,1)}, u32[]{:S(2)}, u32[]{:S(2)}) collective-permute-start(bf16[2,4,64,1216]{3,2,1,0:T(8,128)(2,1)} %pad_maximum_fusion.9), channel_id=1, source_target_pairs={{0,4},{2,6},{4,0},{6,2},{1,5},{3,7},{5,1},{7,3},{8,12},{10,14},{12... | collective-permute-start | bytes 3735560 | tf_op jit(solution)/shard_map/ppermute | solution.py:495
  813.2 51.7 %collective-permute-start.16 = (bf16[2,4,64,1216]{3,2,1,0:T(8,128)(2,1)}, bf16[2,4,64,1216]{3,2,1,0:T(8,128)(2,1)}, u32[]{:S(2)}, u32[]{:S(2)}) collective-permute-start(bf16[2,4,64,1216]{3,2,1,0:T(8,128)(2,1)} %pad_maximum_fusion.10), channel_id=1, source_target_pairs={{0,2},{2,0},{4,6},{6,4},{1,3},{3,1},{5,7},{7,5},{8,10},{10,8},{12,... | collective-permute-start | bytes 3735560 | tf_op jit(solution)/shard_map/ppermute | solution.py:495
  841.4 20.6 %copy-start.17 = (bf16[1,4,64,2432]{3,2,1,0:T(8,128)(2,1)S(1)}, bf16[1,4,64,2432]{3,2,1,0:T(8,128)(2,1)}, u32[]{:S(2)}) copy-start(bf16[1,4,64,2432]{3,2,1,0:T(8,128)(2,1)} %copy-done.16) | copy-start | bytes 3735556
  841.4 37.1 %collective-permute-start.27 = (bf16[4,64,1024]{2,1,0:T(8,128)(2,1)}, bf16[4,64,1024]{2,1,0:T(8,128)(2,1)}, u32[]{:S(2)}, u32[]{:S(2)}) collective-permute-start(bf16[4,64,1024]{2,1,0:T(8,128)(2,1)} %fusion.57), channel_id=1, source_target_pairs={{0,2},{2,0},{4,6},{6,4},{1,3},{3,1},{5,7},{7,5},{8,10},{10,8},{12,... | collective-permute-start | bytes 1572872 | tf_op jit(solution)/shard_map/ppermute | solution.py:495
  843.3 19.8 %copy-start.10 = (f32[2,4,64,1024]{3,2,1,0:T(8,128)}, f32[2,4,64,1024]{3,2,1,0:T(8,128)S(1)}, u32[]{:S(2)}) copy-start(f32[2,4,64,1024]{3,2,1,0:T(8,128)S(1)} %convert_element_type.434) | copy-start | bytes 6291460
  844.4 34.1 %collective-permute-start.25 = (bf16[4,64,1024]{2,1,0:T(8,128)(2,1)}, bf16[4,64,1024]{2,1,0:T(8,128)(2,1)}, u32[]{:S(2)}, u32[]{:S(2)}) collective-permute-start(bf16[4,64,1024]{2,1,0:T(8,128)(2,1)} %fusion.56), channel_id=1, source_target_pairs={{0,4},{2,6},{4,0},{6,2},{1,5},{3,7},{5,1},{7,3},{8,12},{10,14},{12... | collective-permute-start | bytes 1572872 | tf_op jit(solution)/shard_map/ppermute | solution.py:495
  863.1 24.6 %collective-permute-start.19 = (bf16[4,64,1216]{2,1,0:T(8,128)(2,1)}, bf16[4,64,1216]{2,1,0:T(8,128)(2,1)S(1)}, u32[]{:S(2)}, u32[]{:S(2)}) collective-permute-start(bf16[4,64,1216]{2,1,0:T(8,128)(2,1)} %fusion.52), channel_id=1, source_target_pairs={{0,2},{2,0},{4,6},{6,4},{1,3},{3,1},{5,7},{7,5},{8,10},{10,8},{12,... | collective-permute-start | bytes 1867784 | tf_op jit(solution)/shard_map/ppermute | solution.py:495
  868.8 18.8 %collective-permute-start.17 = (bf16[4,64,1216]{2,1,0:T(8,128)(2,1)}, bf16[4,64,1216]{2,1,0:T(8,128)(2,1)}, u32[]{:S(2)}, u32[]{:S(2)}) collective-permute-start(bf16[4,64,1216]{2,1,0:T(8,128)(2,1)} %fusion.51), channel_id=1, source_target_pairs={{0,4},{2,6},{4,0},{6,2},{1,5},{3,7},{5,1},{7,3},{8,12},{10,14},{12... | collective-permute-start | bytes 1867784 | tf_op jit(solution)/shard_map/ppermute | solution.py:495
  881.4 13.6 %collective-permute-start.30 = (bf16[64,2048]{1,0:T(8,128)(2,1)S(1)}, bf16[64,2048]{1,0:T(8,128)(2,1)S(1)}, u32[]{:S(2)}, u32[]{:S(2)}) collective-permute-start(bf16[64,2048]{1,0:T(8,128)(2,1)S(1)} %get-tuple-element.112), channel_id=1, source_target_pairs={{0,24},{8,0},{16,8},{24,16},{1,25},{9,1},{17,9},{25,17},{2,26},{10... | collective-permute-start | bytes 786440 | tf_op jit(solution)/shard_map/ppermute | solution.py:500
  881.5 39.1 %collective-permute-start.29 = (bf16[64,2048]{1,0:T(8,128)(2,1)S(1)}, bf16[64,2048]{1,0:T(8,128)(2,1)S(1)}, u32[]{:S(2)}, u32[]{:S(2)}) collective-permute-start(bf16[64,2048]{1,0:T(8,128)(2,1)S(1)} %get-tuple-element.111), channel_id=1, source_target_pairs={{0,16},{8,24},{16,0},{24,8},{1,17},{9,25},{17,1},{25,9},{2,18},{10... | collective-permute-start | bytes 786440 | tf_op jit(solution)/shard_map/ppermute | solution.py:500
  885.7 34.9 %collective-permute-start.28 = (bf16[64,2048]{1,0:T(8,128)(2,1)S(1)}, bf16[64,2048]{1,0:T(8,128)(2,1)S(1)}, u32[]{:S(2)}, u32[]{:S(2)}) collective-permute-start(bf16[64,2048]{1,0:T(8,128)(2,1)S(1)} %get-tuple-element.110), channel_id=1, source_target_pairs={{0,8},{8,16},{16,24},{24,0},{1,9},{9,17},{17,25},{25,1},{2,10},{10... | collective-permute-start | bytes 786440 | tf_op jit(solution)/shard_map/ppermute | solution.py:500
  889.6 31.9 %collective-permute-start.22 = (bf16[64,2432]{1,0:T(8,128)(2,1)S(1)}, bf16[64,2432]{1,0:T(8,128)(2,1)S(1)}, u32[]{:S(2)}, u32[]{:S(2)}) collective-permute-start(bf16[64,2432]{1,0:T(8,128)(2,1)S(1)} %get-tuple-element.107), channel_id=1, source_target_pairs={{0,24},{8,0},{16,8},{24,16},{1,25},{9,1},{17,9},{25,17},{2,26},{10... | collective-permute-start | bytes 933896 | tf_op jit(solution)/shard_map/ppermute | solution.py:500
  891.5 38.2 %collective-permute-start.21 = (bf16[64,2432]{1,0:T(8,128)(2,1)S(1)}, bf16[64,2432]{1,0:T(8,128)(2,1)S(1)}, u32[]{:S(2)}, u32[]{:S(2)}) collective-permute-start(bf16[64,2432]{1,0:T(8,128)(2,1)S(1)} %get-tuple-element.106), channel_id=1, source_target_pairs={{0,16},{8,24},{16,0},{24,8},{1,17},{9,25},{17,1},{25,9},{2,18},{10... | collective-permute-start | bytes 933896 | tf_op jit(solution)/shard_map/ppermute | solution.py:500
  895.0 34.8 %collective-permute-start.20 = (bf16[64,2432]{1,0:T(8,128)(2,1)S(1)}, bf16[64,2432]{1,0:T(8,128)(2,1)S(1)}, u32[]{:S(2)}, u32[]{:S(2)}) collective-permute-start(bf16[64,2432]{1,0:T(8,128)(2,1)S(1)} %get-tuple-element.105), channel_id=1, source_target_pairs={{0,8},{8,16},{16,24},{24,0},{1,9},{9,17},{17,25},{25,1},{2,10},{10... | collective-permute-start | bytes 933896 | tf_op jit(solution)/shard_map/ppermute | solution.py:500
  (32 other events, 186.2 us)

commit v3 on v2

--- a/solution.py
+++ b/solution.py
@@ -390,114 +390,12 @@
     return vector * cosine + pltpu.roll(vector, vector.shape[-1] // 2, 1) * sine
 
 
-def stack_heads(ref, start, rows, heads, head_dim):
-    return jnp.concatenate(
-        [ref[pl.ds(start, rows), pl.ds(h * head_dim, head_dim)] for h in range(heads)], axis=0
-    )
-
-
-def masked_block(stacked, keys, query_place, query_segment, key_segment, heads, score_scale):
-    rows, extent = query_place.shape[0], keys.shape[0]
-    key_place = lax.broadcasted_iota(jnp.int32, (rows, extent), 1)
-    allowed = (query_place >= key_place) & (query_segment == key_segment)
-    bias = jnp.where(allowed, 0.0, MASKED).astype(F32)
-    scores = dot32(stacked, keys, ((1,), (1,))) * score_scale
-    scores = (scores.reshape(heads, rows, extent) + bias[None]).reshape(heads * rows, extent)
-    row_max = jnp.max(scores, axis=-1, keepdims=True)
-    weights = jnp.exp(scores - row_max)
-    total = jnp.sum(weights, axis=-1, keepdims=True)
-    return weights * (1.0 / total)
-
-
-def attend_back_kernel(
-    plan,
-    queries_ref,
-    grad_ref,
-    keys_ref,
-    values_ref,
-    place_ref,
-    segment_ref,
-    key_segment_ref,
-    cosine_ref,
-    sine_ref,
-    grad_lin_ref,
-    grad_keys_ref,
-    grad_values_ref,
-):
-    blocks, rows, pair, heads, head_dim, score_scale = plan
-
-    @pl.when(pl.program_id(0) == 0)
-    def _():
-        grad_keys_ref[...] = jnp.zeros_like(grad_keys_ref)
-        grad_values_ref[...] = jnp.zeros_like(grad_values_ref)
-
-    for block in range(blocks):
-        start = block * rows
-        extent = (block + 1) * pair * rows
-        stacked = stack_heads(queries_ref, start, rows, heads, head_dim)
-        grads = stack_heads(grad_ref, start, rows, heads, head_dim)
-        keys = keys_ref[pl.ds(0, extent), :]
-        values = values_ref[pl.ds(0, extent), :]
-        soft = masked_block(
-            stacked,
-            keys,
-            place_ref[pl.ds(start, rows), :],
-            segment_ref[pl.ds(start, rows), :],
-            key_segment_ref[:, pl.ds(0, extent)],
-            heads,
-            score_scale,
-        )
-        grad_soft = dot32(grads, values, ((1,), (1,)))
-        inner = jnp.sum(soft * grad_soft, axis=-1, keepdims=True)
-        grad_scores = (soft * (grad_soft - inner)).astype(BF16)
-        grad_values_ref[pl.ds(0, extent), :] += dot32(soft.astype(BF16), grads, ((0,), (0,)))
-        grad_keys_ref[pl.ds(0, extent), :] += (
-            dot32(grad_scores, stacked, ((0,), (0,))) * score_scale
-        )
-        grad_queries = dot32(grad_scores, keys, ((1,), (0,))) * score_scale
-        cosine, sine = cosine_ref[pl.ds(start, rows), :], sine_ref[pl.ds(start, rows), :]
-        for h in range(heads):
-            part = turn(grad_queries[h * rows : (h + 1) * rows], cosine, -sine)
-            grad_lin_ref[pl.ds(start, rows), pl.ds(h * head_dim, head_dim)] = part.astype(BF16)
-
-
-def whole(shape):
-    return pl.BlockSpec(shape, lambda g: (0,) * len(shape))
-
-
-def attention_call(kernel, plan, groups, wide, narrow, outs, name, flops):
-    rows = wide[0].shape[0]
-    group = wide[0].shape[1] // groups
-    column = pl.BlockSpec((rows, group), lambda g: (0, g))
-    return pl.pallas_call(
-        functools.partial(kernel, plan),
-        grid=(groups,),
-        in_specs=[column] * len(wide) + [whole(a.shape) for a in narrow],
-        out_specs=[column if a.shape[0] == rows else whole(a.shape) for a in outs],
-        out_shape=outs,
-        compiler_params=pltpu.CompilerParams(vmem_limit_bytes=48 * 1024 * 1024),
-        cost_estimate=pl.CostEstimate(
-            flops=flops, bytes_accessed=6 * rows * wide[0].shape[1], transcendentals=flops // 512
-        ),
-        name=name,
-    )(*wide, *narrow)
-
-
-def gather(value, axes, dim):
-    return lax.all_gather(value, axes, axis=dim, tiled=True)
-
-
 def scatter_sum(value, axes, dim):
     return lax.psum_scatter(value, axes, scatter_dimension=dim, tiled=True)
 
 
 def send_plane(value, step):
     return lax.ppermute(value, "seq", [(i, i ^ step) for i in range(4)])
-
-
-def send_line(value, step):
-    size = lax.axis_size("dp")
-    return lax.ppermute(value, "dp", [(i, (i + step) % size) for i in range(size)])
 
 
 def send_core(value):
@@ -520,41 +418,9 @@
     return out
 
 
-def scatter_plane(value):
-    half = value.shape[-1] // 2
-    left, right = value[..., :half], value[..., half:]
-    got = send_plane(jnp.stack([left[1], left[3]]), 1).astype(F32)
-    passed = send_plane((left[2].astype(F32) + got[1]).astype(BF16), 2).astype(F32)
-    left = left[0].astype(F32) + got[0] + passed
-    got = send_plane(right[2:], 2).astype(F32)
-    passed = send_plane((right[1].astype(F32) + got[1]).astype(BF16), 1).astype(F32)
-    right = right[0].astype(F32) + got[0] + passed
-    return jnp.concatenate([left, right], axis=-1)
-
-
-def scatter_line(value, plane):
-    size = lax.axis_size("dp")
-    total = block_of(value, plane).astype(F32)
-    for step in range(1, size):
-        total = total + send_line(block_of(value, (plane + step) % size), step).astype(F32)
-    return total
-
-
 def scatter_core(value, core, dim):
     other = send_core(block_of(value, 1 - core, dim))
     return (block_of(value, core, dim).astype(F32) + other.astype(F32)).astype(BF16)
-
-
-def scatter_every(value, plane, own, core):
-    planes, chips, pair, shard, columns = value.shape
-    value = scatter_core(value, core, 2)
-    blocks = jnp.stack([block_of(value, own ^ step, 1) for step in range(chips)])
-    value = scatter_plane(blocks).astype(BF16)
-    return scatter_line(value, plane)
-
-
-def by_step(blocks, own):
-    return jnp.stack([block_of(blocks, own ^ step) for step in range(4)])
 
 
 class Post:
@@ -879,6 +745,696 @@
         compiler_params=pltpu.CompilerParams(collective_id=1,has_side_effects=True,vmem_limit_bytes=60*1024*1024),name="front")(tok,cot,marks,wq_in,wo_in,gu_in,wd_in,freq)
 
 
+def back_kernel(
+    plan,
+    gh2,
+    grads_in,
+    middle,
+    x_in,
+    wq,
+    wo,
+    h1t_in,
+    q_in,
+    att_t_in,
+    kv_in,
+    cos_in,
+    sin_in,
+    marks_in,
+    gain_v,
+    home,
+    gq_out,
+    gkv_out,
+    go_out,
+    send_sem,
+    recv_sem,
+    local_sem,
+    mid_v,
+    gh1_v,
+    x_v,
+    proj_v,
+    h1t_v,
+    q_v,
+    att_t_v,
+    kv_v,
+    cos_v,
+    sin_v,
+    marks_v,
+    wo_b,
+    wq_b,
+    wk_v,
+    mix_v,
+    lin_v,
+    kvacc,
+    kvx,
+    gains_acc,
+    sq,
+    so,
+    rq,
+    ro,
+    tq,
+    to,
+    pq,
+    po,
+    uq,
+    uo,
+    zq,
+    zo,
+    skv,
+    rkv,
+    tkv,
+    pkv,
+    ukv,
+    zkv,
+    gl_v,
+):
+    tile, width, head_dim, group = plan
+    scale = head_dim**-0.5
+    chips, planes = 4, 4
+    rows = chips * tile
+    groups = width // group
+    heads = group // head_dim
+    shard = sq.shape[3]
+    p = Post(send_sem, recv_sem)
+    z, s, c = p.plane, p.own, p.core
+    others = ((p.to_x, p.by_x), (p.to_y, p.by_y), (p.to_far, p.far))
+    lines = [lax.rem(z + k, planes) for k in range(1, planes)]
+    bar = pltpu.get_barrier_semaphore()
+
+    def load(src, dst, index):
+        return pltpu.make_async_copy(src, dst, local_sem.at[index])
+
+    first = [
+        load(gh2, q_v, 0),
+        load(middle, mid_v, 1),
+        load(grads_in.at[s], x_v, 2),
+    ]
+    second = [
+        load(h1t_in, h1t_v, 3),
+        load(att_t_in, att_t_v, 5),
+        load(kv_in, kv_v, 6),
+        load(cos_in, cos_v, 7),
+        load(sin_in, sin_v, 8),
+        load(marks_in, marks_v, 9),
+        load(wq.at[:, :, :, :, pl.ds(width, 2 * head_dim)], wk_v, 10),
+    ]
+    tokens_again = load(x_in, x_v, 11)
+
+    def fetch(g):
+        at = pl.ds(pl.multiple_of(g * group, group), group)
+        slot = lax.rem(g, 2)
+        return (
+            load(wo.at[g], wo_b.at[slot], 12 + slot),
+            load(wq.at[:, :, :, :, at], wq_b.at[slot], 14 + slot),
+        )
+
+    for cp in first + second:
+        cp.start()
+    for cp in fetch(0):
+        cp.start()
+    for target in [t for t, _ in others] + [p.to_core] + [(a, s, c) for a in lines]:
+        pl.semaphore_signal(bar, inc=1, device_id=target, device_id_type=MESH)
+    pl.semaphore_wait(bar, 7)
+
+    def stage_a(g):
+        slot = lax.rem(g, 2)
+        return (
+            p.copy(sq.at[:, :, 1 - c], rq.at[slot], "aq", g, p.to_core),
+            p.copy(so.at[:, 1 - c], ro.at[slot], "ao", g, p.to_core),
+        )
+
+    def stage_b(g):
+        slot = lax.rem(g, 2)
+        copies = []
+        for i, (target, other) in enumerate(others):
+            copies.append(p.copy(tq.at[slot, :, other], pq.at[g, i], "bq%d" % i, g, target))
+            copies.append(p.copy(to.at[slot, other], po.at[g, i], "bo%d" % i, g, target))
+        return copies
+
+    def stage_c(g):
+        slot = lax.rem(g, 2)
+        return [
+            p.copy(uq.at[slot, a], zq.at[g, k], "cq%d" % k, g, (a, s, c))
+            for k, a in enumerate(lines)
+        ]
+
+    def stage_c_out(g, k):
+        return p.copy(uo.at[lax.rem(g, 2)], zo.at[k], "co", k, (g, s, c))
+
+    def wide(value):
+        return value.astype(F32)
+
+    def do_b(g):
+        slot = lax.rem(g, 2)
+        for cp in stage_a(g):
+            cp.wait_recv()
+
+        @pl.when(g >= 2)
+        def _():
+            for cp in stage_b(g - 2):
+                cp.wait_send()
+
+        def one(a, carry):
+            tq[slot, a] = (wide(sq[a, :, c]) + wide(rq[slot, a])).astype(BF16)
+            to[slot, a] = (wide(so[a, c]) + wide(ro[slot, a])).astype(BF16)
+            return carry
+
+        lax.fori_loop(0, planes, one, 0)
+        for cp in stage_b(g):
+            cp.start()
+
+    def do_c(g):
+        slot = lax.rem(g, 2)
+        for cp in stage_b(g):
+            cp.wait_recv()
+        total = wide(tq[slot, :, s])
+        mixed = wide(to[slot, s])
+        for i in range(3):
+            total = total + wide(pq[g, i])
+            mixed = mixed + wide(po[g, i])
+        uq[slot] = total.astype(BF16)
+        uo[slot] = mixed.astype(BF16)
+        for cp in stage_c(g):
+            cp.start()
+        for k in range(1, planes):
+
+            @pl.when(lax.rem(g + planes - z, planes) == k)
+            def _(k=k):
+                stage_c_out(g, k - 1).start()
+
+    def do_d(g):
+        slot = lax.rem(g, 2)
+        total = wide(uq[slot, z])
+        for k, cp in enumerate(stage_c(g)):
+            cp.wait_recv()
+            total = total + wide(zq[g, k])
+        gq_out[:, pl.ds(pl.multiple_of(g * group, group), group)] = total
+
+        @pl.when(z == g)
+        def _():
+            mixed = wide(uo[slot])
+            for k in range(planes - 1):
+                stage_c_out(g, k).wait_recv()
+                mixed = mixed + wide(zo[k])
+            go_out[...] = mixed
+
+        for k in range(1, planes):
+
+            @pl.when(lax.rem(g + planes - z, planes) == k)
+            def _(k=k):
+                stage_c_out(g, k - 1).wait_send()
+
+        for cp in stage_c(g):
+            cp.wait_send()
+
+    for cp in first:
+        cp.wait()
+    gains_acc[...] = jnp.zeros_like(gains_acc)
+
+    def norm_two(b, carry):
+        at = pl.ds(pl.multiple_of(b * tile, tile), tile)
+        m = mid_v[at, :]
+        inv = lax.rsqrt(jnp.mean(m * m, axis=-1, keepdims=True) + EPSILON)
+        normed = m * inv
+        grad = wide(q_v[at, :])
+        gains_acc[1:2, :] += jnp.sum(grad * normed, axis=0, keepdims=True)
+        grad = grad * gain_v[1:2, :]
+        grad = wide(x_v[b]) + inv * (grad - normed * jnp.mean(grad * normed, axis=-1, keepdims=True))
+        mid_v[at, :] = grad
+        proj_v[at, :] = grad.astype(BF16)
+        gh1_v[at, :] = jnp.zeros_like(grad)
+        return carry
+
+    lax.fori_loop(0, chips, norm_two, 0)
+    tokens_again.start()
+    queries = load(q_in, q_v, 4)
+    queries.start()
+    for cp in second + [queries]:
+        cp.wait()
+    kvacc[...] = jnp.zeros_like(kvacc)
+    seg_cols = [jnp.transpose(marks_v[c, b].astype(F32))[:, 0:1] for b in range(chips)]
+    key_seg = jnp.concatenate(
+        [marks_v[k % 2, k // 2, 0:1, :] for k in range(2 * chips)], axis=1
+    ).astype(F32)
+
+    def one_group(g, carry):
+        slot = lax.rem(g, 2)
+        column = pl.multiple_of(g * group, group)
+        for cp in fetch(g):
+            cp.wait()
+
+        @pl.when(g + 1 < groups)
+        def _():
+            for cp in fetch(g + 1):
+                cp.start()
+
+        w = wo_b[slot].reshape(group, width)
+        mix_v[...] = dot2(proj_v[...], w, 1, 1).astype(BF16)
+        for b in range(chips):
+            extent = (b + 1) * 2 * tile
+            at = pl.ds(b * tile, tile)
+            kvs = kv_v[pl.ds(0, b + 1)].reshape(extent, 2 * head_dim)
+            keys, values = kvs[:, :head_dim], kvs[:, head_dim:]
+            place = (2 * b + c) * tile + lax.broadcasted_iota(jnp.int32, (tile, extent), 0)
+            seen = lax.broadcasted_iota(jnp.int32, (tile, extent), 1)
+            allowed = (place >= seen) & (seg_cols[b] == key_seg[:, :extent])
+            bias = jnp.where(allowed, 0.0, MASKED).astype(F32)
+            cosine, sine = cos_v[at, :], sin_v[at, :]
+            for first_head in range(0, heads, 2):
+                span = range(first_head, first_head + 2)
+                q = jnp.concatenate(
+                    [q_v[at, pl.ds(pl.multiple_of(column + h * head_dim, head_dim), head_dim)] for h in span],
+                    axis=0,
+                )
+                grads = jnp.concatenate(
+                    [mix_v[at, pl.ds(h * head_dim, head_dim)] for h in span], axis=0
+                )
+                scores = dot2(q, keys, 1, 1) * scale
+                scores = (scores.reshape(2, tile, extent) + bias[None]).reshape(2 * tile, extent)
+                top = jnp.max(scores, axis=-1, keepdims=True)
+                soft = jnp.exp(scores - top)
+                soft = soft * (1.0 / jnp.sum(soft, axis=-1, keepdims=True))
+                grad_soft = dot2(grads, values, 1, 1)
+                inner = jnp.sum(soft * grad_soft, axis=-1, keepdims=True)
+                grad_scores = (soft * (grad_soft - inner)).astype(BF16)
+                both = jnp.concatenate(
+                    [dot2(grad_scores, q, 0, 0) * scale, dot2(soft.astype(BF16), grads, 0, 0)],
+                    axis=1,
+                )
+                kvacc[pl.ds(0, b + 1)] += both.reshape(b + 1, 2, tile, 2 * head_dim)
+                grad_q = dot2(grad_scores, keys, 1, 0) * scale
+                for i, h in enumerate(span):
+                    part = turn(grad_q[i * tile : (i + 1) * tile], cosine, -sine)
+                    lin_v[at, pl.ds(h * head_dim, head_dim)] = part.astype(BF16)
+
+        @pl.when(g >= 1)
+        def _():
+            do_b(g - 1)
+            for cp in stage_a(g - 1):
+                cp.wait_send()
+
+        left = att_t_v[pl.ds(column, group), :]
+
+        def weights(n, carry):
+            at = pl.ds(pl.multiple_of(n * group, group), group)
+            part = dot2(h1t_v[at, :], lin_v[...], 1, 0)
+            sq[n] = part.astype(BF16).reshape(chips, 2, shard, group)
+            part = dot2(left, proj_v[:, at], 1, 0)
+            so[:, :, :, at] = part.astype(BF16).reshape(chips, 2, shard, group)
+            return carry
+
+        lax.fori_loop(0, planes, weights, 0)
+        for cp in stage_a(g):
+            cp.start()
+
+        def inputs(n, carry):
+            at = pl.ds(pl.multiple_of(n * group, group), group)
+            gh1_v[:, at] += dot2(lin_v[...], wq_b[slot, n].reshape(group, group), 1, 1)
+            return carry
+
+        lax.fori_loop(0, planes, inputs, 0)
+
+        @pl.when(g >= 2)
+        def _():
+            do_c(g - 2)
+
+        @pl.when(g >= 3)
+        def _():
+            do_d(g - 3)
+
+        return carry
+
+    lax.fori_loop(0, groups, one_group, 0)
+
+    to_other = p.copy(kvacc.at[:, 1 - c], kvx, "kx", 0, p.to_core)
+    to_other.start()
+    do_b(groups - 1)
+    to_other.wait_recv()
+    for b in range(chips):
+        at = pl.ds(b * tile, tile)
+        part = kvacc[b, c] + kvx[b]
+        turned = turn(part[:, :head_dim], cos_v[at, :], -sin_v[at, :])
+        gl_v[at, :] = jnp.concatenate([turned, part[:, head_dim:]], axis=1).astype(BF16)
+
+    def last_inputs(n, carry):
+        at = pl.ds(pl.multiple_of(n * group, group), group)
+        gh1_v[:, at] += dot2(gl_v[...], wk_v[n].reshape(group, 2 * head_dim), 1, 1)
+        part = dot2(h1t_v[at, :], gl_v[...], 1, 0).astype(BF16)
+        skv[n, :, :, :, pl.ds(0, 2 * head_dim)] = part.reshape(chips, 2, shard, 2 * head_dim)
+        return carry
+
+    lax.fori_loop(0, planes, last_inputs, 0)
+    tokens_again.wait()
+
+    def norm_one(b, carry):
+        at = pl.ds(pl.multiple_of(b * tile, tile), tile)
+        x = wide(x_v[b])
+        inv = lax.rsqrt(jnp.mean(x * x, axis=-1, keepdims=True) + EPSILON)
+        normed = x * inv
+        grad = gh1_v[at, :]
+        gains_acc[0:1, :] += jnp.sum(grad * normed, axis=0, keepdims=True)
+        grad = grad * gain_v[0:1, :]
+        grad = mid_v[at, :] + inv * (
+            grad - normed * jnp.mean(grad * normed, axis=-1, keepdims=True)
+        )
+        proj_v[at, :] = grad.astype(BF16)
+        return carry
+
+    lax.fori_loop(0, chips, norm_one, 0)
+    for i in range(width // head_dim):
+        part = gains_acc[:, pl.ds(i * head_dim, head_dim)]
+        part = jnp.concatenate([part, jnp.zeros((head_dim - 8, head_dim), F32)], axis=0)
+        part = jnp.transpose(part).astype(BF16).reshape(2, shard, head_dim)
+        skv[i // 4, i % 4, :, :, pl.ds(2 * head_dim, head_dim)] = part
+    a_kv = p.copy(skv.at[:, :, 1 - c], rkv, "akv", 0, p.to_core)
+    a_kv.start()
+    homes = [
+        p.copy(proj_v.at[pl.ds(pl.multiple_of(o * tile, tile), tile)], home.at[s], "home", i, t)
+        for i, (t, o) in enumerate(others)
+    ]
+    do_c(groups - 2)
+    a_kv.wait_recv()
+
+    def last_b(a, carry):
+        tkv[a] = (wide(skv[a, :, c]) + wide(rkv[a])).astype(BF16)
+        return carry
+
+    lax.fori_loop(0, planes, last_b, 0)
+    b_kv = [
+        p.copy(tkv.at[:, o], pkv.at[i], "bkv", i, t) for i, (t, o) in enumerate(others)
+    ]
+    for cp in b_kv:
+        cp.start()
+    for cp in homes:
+        cp.start()
+    own_home = load(proj_v.at[pl.ds(pl.multiple_of(s * tile, tile), tile)], home.at[s], 0)
+    own_home.start()
+    do_d(groups - 3)
+    do_c(groups - 1)
+    do_d(groups - 2)
+    total = wide(tkv[:, s])
+    for i, cp in enumerate(b_kv):
+        cp.wait_recv()
+        total = total + wide(pkv[i])
+    ukv[...] = total.astype(BF16)
+    c_kv = [
+        p.copy(ukv.at[a], zkv.at[k], "ckv", k, (a, s, c)) for k, a in enumerate(lines)
+    ]
+    for cp in c_kv:
+        cp.start()
+    do_d(groups - 1)
+    total = wide(ukv[z])
+    for k, cp in enumerate(c_kv):
+        cp.wait_recv()
+        total = total + wide(zkv[k])
+    gkv_out[...] = total
+    for cp in homes:
+        cp.wait_recv()
+    own_home.wait()
+    for cp in [to_other, a_kv] + b_kv + c_kv + homes:
+        cp.wait_send()
+    for cp in list(stage_a(groups - 1)) + stage_b(groups - 2) + stage_b(groups - 1):
+        cp.wait_send()
+
+
+def back(tile, gh2, grads_in, middle, x_in, wq, wo, h1t, q, att_t, kv, cosine, sine, marks, gains):
+    planes, chips, pair, shard, width = wo.shape
+    rows = chips * tile
+    head_dim = kv.shape[-1] // 2
+    group = 512
+    groups = width // group
+    last = wq.shape[-1] - width
+    V = pltpu.VMEM
+    sd = jax.ShapeDtypeStruct
+    outs = [
+        sd((chips, tile, width), BF16),
+        sd((shard, width), F32),
+        sd((shard, last), F32),
+        sd((shard, width), F32),
+    ]
+    anyspec = pl.BlockSpec(memory_space=pl.ANY)
+    inner = pl.BlockSpec(memory_space=V)
+    scratch = [
+        pltpu.SemaphoreType.DMA((GROUPS, 4)),
+        pltpu.SemaphoreType.DMA((GROUPS, 4)),
+        pltpu.SemaphoreType.DMA((16,)),
+        V((rows, width), F32),
+        V((rows, width), F32),
+        V((chips, tile, width), BF16),
+        V((rows, width), BF16),
+        V((width, rows), BF16),
+        V((rows, width), BF16),
+        V((width, rows), BF16),
+        V((chips, pair, tile, 2 * head_dim), BF16),
+        V((rows, head_dim), F32),
+        V((rows, head_dim), F32),
+        V(marks.shape, jnp.int32),
+        V((2, chips, pair, shard, width), BF16),
+        V((2, planes, chips, pair, shard, group), BF16),
+        V((planes, chips, pair, shard, 2 * head_dim), BF16),
+        V((rows, group), BF16),
+        V((rows, group), BF16),
+        V((chips, pair, tile, 2 * head_dim), F32),
+        V((chips, tile, 2 * head_dim), F32),
+        V((8, width), F32),
+        V((planes, chips, pair, shard, group), BF16),
+        V((chips, pair, shard, width), BF16),
+        V((2, planes, chips, shard, group), BF16),
+        V((2, chips, shard, width), BF16),
+        V((2, planes, chips, shard, group), BF16),
+        V((2, chips, shard, width), BF16),
+        V((groups, 3, planes, shard, group), BF16),
+        V((groups, 3, shard, width), BF16),
+        V((2, planes, shard, group), BF16),
+        V((2, shard, width), BF16),
+        V((groups, 3, shard, group), BF16),
+        V((3, shard, width), BF16),
+        V((planes, chips, pair, shard, last), BF16),
+        V((planes, chips, shard, last), BF16),
+        V((planes, chips, shard, last), BF16),
+        V((3, planes, shard, last), BF16),
+        V((planes, shard, last), BF16),
+        V((3, shard, last), BF16),
+        V((rows, 2 * head_dim), BF16),
+    ]
+    return pl.pallas_call(
+        functools.partial(back_kernel, (tile, width, head_dim, group)),
+        out_shape=outs,
+        in_specs=[anyspec] * 13 + [inner],
+        out_specs=[anyspec] + [inner] * 3,
+        scratch_shapes=scratch,
+        compiler_params=pltpu.CompilerParams(
+            collective_id=2, has_side_effects=True, vmem_limit_bytes=63 * 1024 * 1024
+        ),
+        cost_estimate=pl.CostEstimate(
+            flops=60_000_000_000, bytes_accessed=60_000_000, transcendentals=10_000_000
+        ),
+        name="back",
+    )(gh2, grads_in, middle, x_in, wq, wo, h1t, q, att_t, kv, cosine, sine, marks, gains)
+
+
+def middle_kernel(
+    plan,
+    two,
+    grads,
+    gate_up,
+    down,
+    residual,
+    pre_out,
+    hidden_out,
+    partial_out,
+    sum_out,
+    send_sem,
+    recv_sem,
+    local_sem,
+    gu_v,
+    down_v,
+    res_v,
+    two_v,
+    e_v,
+    pre_v,
+    hidden_v,
+    far_v,
+    x_v,
+    y_v,
+    own_v,
+    xa_far,
+    xa_own,
+    yb_far,
+    yb_own,
+    ya_pass,
+    xb_pass,
+):
+    rows, width, hidden = plan
+    half = width // 2
+    wide_tile, out_tile = 256, 512
+    p = Post(send_sem, recv_sem)
+    low, high = pl.ds(0, half), pl.ds(half, half)
+    order = (p.far, p.by_x, p.by_y, p.own)
+    targets = (far_v, x_v, y_v, own_v)
+
+    def load(src, dst, index):
+        return pltpu.make_async_copy(src, dst, local_sem.at[index])
+
+    def fetch(i):
+        return (
+            load(two.at[order[i]], two_v.at[i % 2], 2 * (i % 2)),
+            load(grads.at[order[i]], e_v.at[i % 2], 2 * (i % 2) + 1),
+        )
+
+    def keep_pre(i):
+        at = pl.ds(pl.multiple_of(order[i] * rows, rows), rows)
+        return load(pre_v, pre_out.at[at], 4)
+
+    def keep_hidden(i):
+        at = pl.ds(pl.multiple_of(order[i] * rows, rows), rows)
+        return load(hidden_v.at[i], hidden_out.at[at], 5 + i)
+
+    def place(i):
+        return load(two_v.at[i % 2], partial_out.at[order[i]], i % 2)
+
+    weights = [load(gate_up, gu_v, 9), load(down, down_v, 10), load(residual, res_v, 11)]
+    for cp in list(fetch(0)) + weights:
+        cp.start()
+    bar = pltpu.get_barrier_semaphore()
+    for target in (p.to_x, p.to_y):
+        pl.semaphore_signal(bar, inc=1, device_id=target, device_id_type=MESH)
+    pl.semaphore_wait(bar, 2)
+    for cp in weights:
+        cp.wait()
+
+    def chunk(i, start, size):
+        at, above = pl.ds(start, size), pl.ds(start + hidden, size)
+        gate = dot2(two_v[i % 2], gu_v[:, at], 1, 0)
+        up = dot2(two_v[i % 2], gu_v[:, above], 1, 0)
+        grad = dot2(e_v[i % 2], down_v[at, :], 1, 1)
+        sig = jax.nn.sigmoid(gate)
+        silu = gate * sig
+        hidden_v[i, :, at] = (silu * up).astype(BF16)
+        pre_v[:, at] = (grad * up * sig * (1.0 + gate * (1.0 - sig))).astype(BF16)
+        pre_v[:, above] = (grad * silu).astype(BF16)
+
+    whole_tiles = hidden // wide_tile
+    sends = []
+    for i in range(4):
+        for cp in fetch(i):
+            cp.wait()
+        if i < 3:
+            for cp in fetch(i + 1):
+                cp.start()
+
+        def step(j, carry, i=i):
+            chunk(i, pl.multiple_of(j * wide_tile, wide_tile), wide_tile)
+            return carry
+
+        lax.fori_loop(0, whole_tiles, step, 0)
+        if hidden % wide_tile:
+            chunk(i, whole_tiles * wide_tile, hidden % wide_tile)
+        keep_pre(i).start()
+        keep_hidden(i).start()
+
+        def back_tile(n, carry, i=i):
+            at = pl.ds(pl.multiple_of(n * out_tile, out_tile), out_tile)
+            targets[i][:, at] = dot2(pre_v[...], gu_v[at, :], 1, 1).astype(BF16)
+            return carry
+
+        lax.fori_loop(0, width // out_tile, back_tile, 0)
+        keep_pre(i).wait()
+        if i == 0:
+            go = [
+                p.copy(far_v.at[:, low], xa_far, "xa_far", 0, p.to_x),
+                p.copy(far_v.at[:, high], yb_far, "yb_far", 0, p.to_y),
+            ]
+        elif i == 1:
+            go = [p.copy(x_v.at[:, low], xa_own, "xa_own", 0, p.to_x)]
+            sends[1].wait_recv()
+            x_v[:, high] = (x_v[:, high].astype(F32) + yb_far[...].astype(F32)).astype(BF16)
+            go.append(p.copy(x_v.at[:, high], xb_pass, "xb_pass", 0, p.to_x))
+        elif i == 2:
+            go = [p.copy(y_v.at[:, high], yb_own, "yb_own", 0, p.to_y)]
+            sends[0].wait_recv()
+            y_v[:, low] = (y_v[:, low].astype(F32) + xa_far[...].astype(F32)).astype(BF16)
+            go.append(p.copy(y_v.at[:, low], ya_pass, "ya_pass", 0, p.to_y))
+        else:
+            go = []
+        for cp in go:
+            cp.start()
+        sends += go
+
+    for i in range(4):
+        if i >= 2:
+            place(i - 2).wait()
+
+        def out_chunk(n, carry, i=i):
+            at = pl.ds(pl.multiple_of(n * out_tile, out_tile), out_tile)
+            part = dot2(hidden_v[i], down_v[:, at], 1, 0)
+            if i == 3:
+                part = part + res_v[:, at]
+            two_v[i % 2, :, at] = part.astype(BF16)
+            return carry
+
+        lax.fori_loop(0, width // out_tile, out_chunk, 0)
+        place(i).start()
+    for i in range(4):
+        keep_hidden(i).wait()
+    for cp in sends[2:]:
+        cp.wait_recv()
+    own_v[:, low] = (
+        own_v[:, low].astype(F32) + xa_own[...].astype(F32) + ya_pass[...].astype(F32)
+    ).astype(BF16)
+    own_v[:, high] = (
+        own_v[:, high].astype(F32) + yb_own[...].astype(F32) + xb_pass[...].astype(F32)
+    ).astype(BF16)
+    done = load(own_v, sum_out, 4)
+    done.start()
+    place(2).wait()
+    place(3).wait()
+    done.wait()
+    for cp in sends:
+        cp.wait_send()
+
+
+def middle_call(two, grads, gate_up, down, residual):
+    chips, rows, width = two.shape
+    hidden = down.shape[0]
+    V = pltpu.VMEM
+    sd = jax.ShapeDtypeStruct
+    anyspec = pl.BlockSpec(memory_space=pl.ANY)
+    block = (rows, width)
+    part = (rows, width // 2)
+    return pl.pallas_call(
+        functools.partial(middle_kernel, (rows, width, hidden)),
+        out_shape=[
+            sd((chips * rows, 2 * hidden), BF16),
+            sd((chips * rows, hidden), BF16),
+            sd((chips,) + block, BF16),
+            sd(block, BF16),
+        ],
+        in_specs=[anyspec] * 5,
+        out_specs=[anyspec] * 4,
+        scratch_shapes=[
+            pltpu.SemaphoreType.DMA((8, 4)),
+            pltpu.SemaphoreType.DMA((8, 4)),
+            pltpu.SemaphoreType.DMA((12,)),
+            V((width, 2 * hidden), BF16),
+            V((hidden, width), BF16),
+            V(block, F32),
+            V((2,) + block, BF16),
+            V((2,) + block, BF16),
+            V((rows, 2 * hidden), BF16),
+            V((chips, rows, hidden), BF16),
+        ]
+        + [V(block, BF16)] * 4
+        + [V(part, BF16)] * 6,
+        compiler_params=pltpu.CompilerParams(
+            collective_id=3, has_side_effects=True, vmem_limit_bytes=63 * 1024 * 1024
+        ),
+        cost_estimate=pl.CostEstimate(
+            flops=80_000_000_000, bytes_accessed=60_000_000, transcendentals=10_000_000
+        ),
+        name="feed_forward",
+    )(two, grads, gate_up, down, residual)
+
+
 def body_plane(
     tokens,
     cotangent,
@@ -935,116 +1491,66 @@
         cosine,
         sine,
     ) = front(tokens, cotangent, marks, w_in, w_out, gate_up, w_down)
-    x_rows = x_rows.reshape(rows, width).astype(F32)
-    w_qkv = w_qkv.reshape(width, qkv + head_dim)
-    gain_one, gain_two = w_qkv[:, qkv].astype(F32), w_qkv[:, qkv + 1].astype(F32)
-    out_mat = out_mat.reshape(width, width)
+    gains = jnp.pad(w_qkv[..., qkv : qkv + 2].reshape(width, 2).T, ((0, 6), (0, 0))).astype(F32)
     gate_up = gate_up.reshape(width, 2 * own_hidden)
     down_mat = down_mat.reshape(own_hidden, width)
-    grads_in = grads_in.reshape(chips * rows, width)
+    plane_grads = grads_in.reshape(chips * rows, width)
     plane_two = plane_two.reshape(chips * rows, width)
-    kv = kv.reshape(rows * pair, 2 * head_dim)
-    keys, values = kv[:, :head_dim], kv[:, head_dim:]
-    query_segment = block_of(marks, core)[:, 0].reshape(rows, 1)
-    key_segment = marks[:, :, 0].transpose(1, 0, 2).reshape(1, rows * pair)
-    query_place = (
-        (jnp.arange(chips, dtype=jnp.int32)[:, None] * pair + core) * tile
-        + jnp.arange(tile, dtype=jnp.int32)[None, :]
-    ).reshape(rows, 1)
-    groups = max(1, head_count // 4)
-    heads = head_count // groups
-    plan = (chips, tile, pair, heads, head_dim, score_scale)
-    pairs_seen = tile * tile * pair * chips * (chips + 1) // 2 * head_count * head_dim
-    narrow = (keys, values, query_place, query_segment, key_segment, cosine, sine)
-    inverse_one = lax.rsqrt(jnp.mean(x_rows * x_rows, axis=-1, keepdims=True) + EPSILON)
-    normed_one = x_rows * inverse_one
-    inverse_two = lax.rsqrt(jnp.mean(middle * middle, axis=-1, keepdims=True) + EPSILON)
-    normed_two = middle * inverse_two
-
-    gate_up_lin = jnp.dot(plane_two, gate_up, preferred_element_type=F32)
-    gate_proj, up_proj = gate_up_lin[:, :own_hidden], gate_up_lin[:, own_hidden:]
-    gate_sigmoid = jax.nn.sigmoid(gate_proj)
-    gate_silu = gate_proj * gate_sigmoid
-    hidden_mlp = (gate_silu * up_proj).astype(BF16)
-    partial_out = jnp.dot(hidden_mlp, down_mat, preferred_element_type=F32).astype(BF16)
-    result = middle + scatter_plane(by_step(partial_out.reshape(chips, rows, width), own))
-    layer_rows = swap_blocks(result.astype(BF16).reshape(chips, tile, width), own)
-
-    grad_hidden = dot32(grads_in, down_mat, ((1,), (1,)))
-    grad_gate_pre = (
-        grad_hidden * up_proj * gate_sigmoid * (1.0 + gate_proj * (1.0 - gate_sigmoid))
-    ).astype(BF16)
-    grad_up_pre = (grad_hidden * gate_silu).astype(BF16)
-    grad_pre = jnp.concatenate([grad_gate_pre, grad_up_pre], axis=1)
-    partial_two = dot32(grad_pre, gate_up, ((1,), (1,))).astype(BF16)
-    grad_hidden_two = scatter_plane(by_step(partial_two.reshape(chips, rows, width), own))
+
+    grad_pre, hidden_mlp, partial_out, grad_hidden_two = middle_call(
+        plane_two.reshape(chips, rows, width),
+        grads_in.reshape(chips, rows, width),
+        gate_up,
+        down_mat,
+        middle,
+    )
+    layer_rows = scatter_sum(partial_out.reshape(chips, chips, tile, width), "seq", 1)
+    layer_rows = layer_rows.reshape(micro, tile, width)
+    grad_down = dot32(hidden_mlp, plane_grads, ((0,), (0,))).astype(BF16)
     grad_gate_up = dot32(plane_two, grad_pre, ((0,), (0,))).astype(BF16)
-    grad_down = dot32(hidden_mlp, grads_in, ((0,), (0,))).astype(BF16)
-
     grad_down = scatter_core(grad_down.reshape(planes, pair, -1, width), core, 1)
-    grad_down = scatter_line(grad_down, plane)
     grad_gate_up = scatter_core(
         grad_gate_up.reshape(planes, chips, pair, shard, 2 * own_hidden), core, 2
     )
-    grad_gate_up = scatter_line(grad_gate_up, plane).astype(BF16)
+    layer_rows, grad_down, grad_gate_up = lax.optimization_barrier(
+        (layer_rows, grad_down, grad_gate_up)
+    )
+    grad_down = scatter_sum(grad_down, "dp", 0).reshape(-1, width).astype(F32)
+    grad_gate_up = scatter_sum(grad_gate_up, "dp", 0).reshape(chips, shard, 2 * own_hidden)
     grad_gate_up = swap_blocks(grad_gate_up, own).reshape(chips, shard, 2, planes, piece)
     grad_gate_up = grad_gate_up.transpose(2, 1, 3, 0, 4).reshape(2, shard, hidden).astype(F32)
 
-    grad_gain_two = jnp.sum(grad_hidden_two * normed_two, axis=0)
-    grad_rows = lax.dynamic_slice_in_dim(grads_in, own * rows, rows, axis=0).astype(F32)
-    grad_middle = grad_rows + norm_back(grad_hidden_two * gain_two, normed_two, inverse_two)
-    grad_proj = grad_middle.astype(BF16)
-    grad_mixed = dot32(grad_proj, out_mat, ((1,), (1,))).astype(BF16)
-    grad_query_lin, grad_keys, grad_values = attention_call(
-        attend_back_kernel,
-        plan,
-        groups,
-        (queries, grad_mixed),
-        narrow,
-        [
-            jax.ShapeDtypeStruct((rows, width), BF16),
-            jax.ShapeDtypeStruct((rows * pair, head_dim), F32),
-            jax.ShapeDtypeStruct((rows * pair, head_dim), F32),
-        ],
-        "attend_back",
-        10 * pairs_seen,
-    )
-    grad_kv = jnp.concatenate([grad_keys, grad_values], axis=1)
-    grad_kv = grad_kv.reshape(chips, pair, tile, 2 * head_dim)
-    grad_kv = block_of(grad_kv, core, 1) + send_core(block_of(grad_kv, 1 - core, 1))
-    grad_kv = grad_kv.reshape(rows, 2 * head_dim)
-    grad_keys = grad_kv[:, :head_dim]
-    grad_keys = grad_keys * cosine - jnp.roll(grad_keys, head_dim // 2, axis=1) * sine
-    grad_lin = jnp.concatenate(
-        [grad_query_lin, grad_keys.astype(BF16), grad_kv[:, head_dim:].astype(BF16)], axis=1
-    )
-    grad_out = dot32(attended, grad_proj, ((0,), (0,))).astype(BF16)
-    grad_hidden_one = dot32(grad_lin, w_qkv[:, :qkv], ((1,), (1,)))
-    grad_gain_one = jnp.sum(grad_hidden_one * normed_one, axis=0)
-    grad_input = grad_middle + norm_back(grad_hidden_one * gain_one, normed_one, inverse_one)
-    grad_input = swap_blocks(grad_input.astype(BF16).reshape(chips, tile, width), own)
-    grad_out = scatter_every(grad_out.reshape(planes, chips, pair, shard, width), plane, own, core)
-    grad_gains = jnp.pad(
-        jnp.stack([grad_gain_one, grad_gain_two], axis=1), ((0, 0), (0, head_dim - 2))
-    )
-    grad_qkv = dot32(hidden_one, grad_lin, ((0,), (0,)))
-    grad_qkv = jnp.concatenate([grad_qkv, grad_gains], axis=1).astype(BF16)
-    grad_qkv = grad_qkv.reshape(planes, chips, pair, shard, qkv + head_dim)
-    grad_qkv = scatter_every(grad_qkv, plane, own, core)
+    grad_input, grad_q, grad_kv, grad_out = back(
+        tile,
+        grad_hidden_two,
+        grads_in,
+        middle,
+        x_rows,
+        w_qkv,
+        out_mat,
+        hidden_one.T,
+        queries,
+        attended.T,
+        kv,
+        cosine,
+        sine,
+        marks,
+        gains,
+    )
     return (
         layer_rows,
         kv_home[..., :head_dim],
         kv_home[..., head_dim:],
         grad_input.astype(F32),
-        grad_qkv[:, :width],
-        grad_qkv[:, width : width + head_dim],
-        grad_qkv[:, width + head_dim : qkv],
+        grad_q,
+        grad_kv[:, :head_dim],
+        grad_kv[:, head_dim : 2 * head_dim],
         grad_out,
         grad_gate_up[0],
         grad_gate_up[1],
         grad_down,
-        grad_qkv[:, qkv],
-        grad_qkv[:, qkv + 1],
+        grad_kv[:, 2 * head_dim],
+        grad_kv[:, 2 * head_dim + 1],
     )
 
 

time: 939 us -> 774 us (0.82)
  Pallas kernels: 318 us -> 573 us
  waiting for transfers between devices: 206 us -> 49.9 us
  matrix products: 189 us -> 45 us
  other arithmetic: 96 us -> 23.1 us
  starting transfers between devices: 46.3 us -> 6.22 us
  local copies, waits for them, and re-layouts: 74.4 us -> 56.2 us
  between operations: 1.94 us -> 14.5 us
    pallas_call x1 -> x2, Pallas kernels: 24.5 us -> 280 us  [the longest x1 172 us: back(): pl.pallas_call(functools.partial(back_kernel, (tile, width, head_dim, gro...]
    ppermute x12 -> x0, waiting for transfers between devices: 134 us -> none  [send_line(): lax.ppermute(value, 'dp', [(i, (i + step) % size) for i in range(size)])]
    dot_general x8 -> x2, matrix products: 142 us -> 45 us  [dot32(): lax.dot_general(left, right, ((contract[0], contract[1]), ((), ())), pref...]
    ppermute x25 -> x3, waiting for transfers between devices: 72.6 us -> 13.4 us  [send_plane(): return lax.ppermute(value, 'seq', [(i, i ^ step) for i in range(4)])]
    dot_general x2 -> x0, matrix products: 47.3 us -> none  [the longest x1 32.1 us: body_plane(): gate_up_lin = jnp.dot(plane_two, gate_up, preferred_element_type=F32)]
    convert_element_type x18 -> x2, other arithmetic: 33.3 us -> 3 us  [the longest x1 2.37 us: body_plane(): grad_down = scatter_sum(grad_down, 'dp', 0).reshape(-1, width).astype(F32)]
    ppermute x25 -> x3, starting transfers between devices: 27.1 us -> 5.51 us  [send_plane(): return lax.ppermute(value, 'seq', [(i, i ^ step) for i in range(4)])]
    reduce_scatter x0 -> x2, waiting for transfers between devices: none -> 21.4 us  [scatter_sum(): return lax.psum_scatter(value, axes, scatter_dimension=dim, tiled=True)]
  transfers between devices with their start and end apart: 42 -> 8, of which waited for: 14 -> 4; matrix products, arithmetic and copies ran while one was open for 27% -> 11% of each run, Pallas kernels for 3% -> 22%
where the time goes in v3:
time: 774 us; the launch traced here: 768 us
  Pallas kernels  573 us (74%)
  local copies, waits for them, and re-layouts  56.2 us (7%)
  waiting for transfers between devices  49.9 us (6%)
  matrix products  45 us (6%)
  other arithmetic  23.1 us (3%)
  between operations  14.5 us (2%)
    pallas_call x1, Pallas kernels, front(): pl.pallas_call(functools.partial(front_kernel, (tile, width, head_dim, gr...  294 us
    pallas_call x1, Pallas kernels, back(): pl.pallas_call(functools.partial(back_kernel, (tile, width, head_dim, gro...  172 us
    pallas_call x1, Pallas kernels, middle_call(): pl.pallas_call(functools.partial(middle_kernel, (rows, width, hidden)), o...  108 us
    dot_general x2, matrix products, dot32(): lax.dot_general(left, right, ((contract[0], contract[1]), ((), ())), pref...  45 us
    reduce_scatter x2, waiting for transfers between devices, scatter_sum(): return lax.psum_scatter(value, axes, scatter_dimension=dim, tiled=True)  21.4 us
  transfers between devices with their start and end apart: 8, of which 4 were waited for; matrix products, arithmetic and copies ran while one was open for 11% of the time, Pallas kernels for 22%

profile of v3, /device:TPU:0, one launch (start us, length us, event | category | flops | bytes accessed | tf_op | source)
XLA Modules:
  0.0 768.2 jit_solution(3856491186373311262)
XLA Ops:
  7.2 2.7 stack.33
  10.3 2.7 stack.34
  13.0 0.3 copy.48
  13.4 1.1 maximum_bitcast_fusion
  14.5 2.2 reshape.89.gu_in
  16.9 0.6 maximum_bitcast_fusion.1.freq
  17.5 0.6 pad.12.marks
  18.1 0.7 fusion.3.wq_in
  18.8 293.5 %front.1 = (bf16[4,128,2048]{2,1,0:T(8,128)(2,1)}, s32[2,4,8,128]{3,2,1,0:T(8,128)}, bf16[4,4,2,64,2432]{4,3,2,1,0:T(8,128)(2,1)}, bf16[4,4,2,64,2048]{4,3,2,1,0...) custom-call(bf16[4,128,2048]{2,1,0:T(8,128)(2,1)} %tok.1, ...), custom_call_target="tpu_custom_call" | custom-call | tf_op jit(solution)/shard_map/front/pallas_call | solution.py:738
  312.4 107.7 %feed_forward.1 = (bf16[2048,2816]{1,0:T(8,128)(2,1)}, bf16[2048,1408]{1,0:T(8,128)(2,1)}, bf16[4,512,2048]{2,1,0:T(8,128)(2,1)}, bf16[512,2048]{1,0:T(8,128)(2,1)}) custom-call(bf16[4,512,2048]{2,1,0:T(8,128)(2,1)} %get-tuple-element.40.two, bf16[4,512,2048]{2,1,0:T(8,128)(2,1)} %bitcast.70, bf16[2048,2816]{1,0:T(8,128)(2,1)} %bitcast.69, ...), custom_call_target="tpu_custom_call" | custom-call | flops 80000000000 | bytes 60000000 | tf_op jit(solution)/shard_map/feed_forward/pallas_call | solution.py:1404
  420.1 8.4 %copy.49 = bf16[4,4,128,2048]{3,2,0,1:T(8,128)(2,1)} copy(bf16[4,4,128,2048]{3,2,1,0:T(8,128)(2,1)} %bitcast.60) | data formatting | bytes 16777216 | tf_op jit(solution)/shard_map/reshape | solution.py:1507
  428.5 30.2 %convolution_convert_fusion = bf16[2048,2816]{1,0:T(8,128)(2,1)S(1)} fusion(bf16[2048,2048]{1,0:T(8,128)(2,1)} %bitcast.72, bf16[2048,2816]{1,0:T(8,128)(2,1)} %get-tuple-element.47), kind=kOutput, calls=%fused_computation.2 | convolution fusion | flops 23628087296 | bytes 31457280 | tf_op jit(solution)/shard_map/dot_general | solution.py:386
  458.8 3.2 dynamic-slice_bitcast_fusion
  462.0 3.1 copy-done
  465.1 14.8 %convolution_convert_fusion.1 = bf16[1408,2048]{1,0:T(8,128)(2,1)S(1)} fusion(bf16[2048,1408]{1,0:T(8,128)(2,1)S(1)} %bitcast.78, bf16[2048,2048]{1,0:T(8,128)(2,1)} %bitcast.71), kind=kOutput, calls=%fused_computation.3 | convolution fusion | flops 11814043648 | bytes 19922944 | tf_op jit(solution)/shard_map/dot_general | solution.py:386
  479.9 2.5 copy-done.1
  482.4 1.8 dynamic-slice_bitcast_fusion.1
  484.2 0.6 collective-permute-start
  484.8 5.1 collective-permute-done
  489.9 4.7 fusion.1
  494.6 8.7 %fusion = bf16[4,4,64,2816]{3,2,1,0:T(8,128)(2,1)} fusion(bf16[4,4,64,2816]{3,2,1,0:T(8,128)(2,1)} %collective-permute-done.1, bf16[4,4,2,64,2816]{4,3,2,1,0:T(8,128)(2,1)} %bitcast.59, s32[]{:T(128)S(6)} %select_n.24), kind=kLoop, calls=%fused_computation.1 | loop fusion | flops 11534336 | bytes 17301508 | tf_op jit(solution)/shard_map/convert_element_type | solution.py:423
  503.3 10.0 %reduce-scatter.10.cloned.1.call-done = bf16[4,1,128,2048]{3,2,0,1:T(8,128)(2,1)} async-done(((bf16[4,4,128,2048]{3,2,0,1:T(8,128)(2,1)}), bf16[4,1,128,2048]{3,2,0,1:T(8,128)(2,1)}) %reduce-scatter.10.cloned.1.call-update) | async-done | bytes 2097168
  513.3 1.2 slice.31
  514.8 4.1 copy.51
  518.9 2.5 copy.52
  521.4 0.6 pad_convert_fusion.gain_v
  522.0 172.2 %back.1 = (bf16[4,128,2048]{2,1,0:T(8,128)(2,1)}, f32[64,2048]{1,0:T(8,128)}, f32[64,384]{1,0:T(8,128)}, f32[64,2048]{1,0:T(8,128)}) custom-call(bf16[512,2048]{1,0:T(8,128)(2,1)} %get-tuple-element.50.gh2, bf16[4,4,128,2048]{3,2,1,0:T(8,128)(2,1)} %get-tuple-element.41.grads_in, f32[512,2048]{1,0:T(8,128)} %get-tuple-element.44.residual.middle, ...), custom_call_target="tpu_custom_call" | custom-call | flops 60000002048 | bytes 60000000 | tf_op jit(solution)/shard_map/back/pallas_call | solution.py:1219
  694.2 4.2 convert_element_type.67
  698.4 0.7 slice_reduce_fusion
  699.1 0.6 fusion.6
  699.8 0.7 fusion.5
  700.5 1.3 dynamic-slice_bitcast_fusion.2
  701.8 0.5 collective-permute-start.2
  702.3 21.4 %reduce-scatter.8.cloned.1.call-done = bf16[1,176,2048]{2,1,0:T(8,128)(2,1)} async-done(((bf16[4,176,2048]{2,1,0:T(8,128)(2,1)}), bf16[1,176,2048]{2,1,0:T(8,128)(2,1)}) %reduce-scatter.8.cloned.1.call-update) | async-done | bytes 720912 | tf_op jit(solution)/shard_map/reduce_scatter | solution.py:394
  723.7 2.4 bitcast_convert_fusion
  726.1 3.4 collective-permute-start.3
  729.5 1.6 collective-permute-start.4
  731.0 0.8 bitcast_dynamic-update-slice_fusion.2
  731.8 13.4 %collective-permute-done.3 = bf16[64,2816]{1,0:T(8,128)(2,1)S(1)} collective-permute-done((bf16[64,2816]{1,0:T(8,128)(2,1)S(1)}, bf16[64,2816]{1,0:T(8,128)(2,1)S(1)}, u32[]{:S(2)}, u32[]{:S(2)}) %collective-permute-start.3) | collective-permute-done | bytes 360480 | tf_op jit(solution)/shard_map/ppermute | solution.py:398
  745.2 0.8 bitcast_dynamic-update-slice_fusion.1
  746.0 0.8 bitcast_dynamic-update-slice_fusion
  746.8 3.8 reshape.104
  750.6 2.0 copy.58
  752.6 0.5 fusion.4
  753.2 2.7 squeeze.37
  755.9 2.7 squeeze.38
  758.6 1.9 copy.64
  760.5 0.8 copy.65
  (46 shorter events, 0.9 us)
Async XLA Ops:
  7.2 506.1 %reduce-scatter.10.cloned.1.call-start = ((), (), s32[]{:S(2)}) async-start(), calls=%async_computation.5 | async-start | bytes 10485760
  13.0 3.8 copy-start.11
  13.0 3.8 copy-start.12
  13.0 4.5 copy-start.9
  13.0 4.5 copy-start.10
  13.0 5.1 copy-start.4
  13.0 5.1 copy-start.7
  13.0 5.0 copy-start.8
  428.4 36.6 %slice-start = ((s8[5767168]{0:T(1024)(128)(4,1)}), s8[1572864]{0:T(1024)(128)(4,1)S(1)}, s32[]{:S(2)}) async-start(s8[5767168]{0:T(1024)(128)(4,1)} %bitcast.77), calls=%async_computation.6 | async-start | bytes 3145728
  428.5 272.1 %reduce-scatter.6.cloned.1.call-start = ((), (), s32[]{:S(2)}) async-start(), calls=%async_computation.3 | async-start | bytes 7208960 | tf_op jit(solution)/shard_map/reduce_scatter | solution.py:394
  428.5 36.5 %slice-start.1 = ((s8[5767168]{0:T(1024)(128)(4,1)}), s8[4194304]{0:T(1024)(128)(4,1)S(1)}, s32[]{:S(2)}) async-start(s8[5767168]{0:T(1024)(128)(4,1)} %bitcast.77), calls=%async_computation.7 | async-start | bytes 8388608
  458.8 6.3 copy-start
  465.1 29.5 %collective-permute-start.1 = (bf16[4,4,64,2816]{3,2,1,0:T(8,128)(2,1)}, bf16[4,4,64,2816]{3,2,1,0:T(8,128)(2,1)}, u32[]{:S(2)}, u32[]{:S(2)}) collective-permute-start(bf16[4,4,64,2816]{3,2,1,0:T(8,128)(2,1)} %dynamic-slice_bitcast_fusion), channel_id=1, source_target_pairs={{0,1},{1,0},{2,3},{3,2},{4,5},{5,4},{6,7},{7,6},{8,9},{9,8},{10,11... | collective-permute-start | bytes 17301512 | tf_op jit(solution)/shard_map/ppermute | solution.py:402
  479.9 2.5 copy-start.1
  484.2 5.7 collective-permute-start
  513.3 5.6 copy-start.2
  513.3 210.4 %reduce-scatter.8.cloned.1.call-start = ((), (), s32[]{:S(2)}) async-start(), calls=%async_computation.4 | async-start | bytes 3604480 | tf_op jit(solution)/shard_map/reduce_scatter | solution.py:394
  694.2 4.2 copy-start.6
  694.2 5.6 copy-start.5
  701.8 29.2 %collective-permute-start.2 = (bf16[64,2816]{1,0:T(8,128)(2,1)S(1)}, bf16[64,2816]{1,0:T(8,128)(2,1)S(1)}, u32[]{:S(2)}, u32[]{:S(2)}) collective-permute-start(bf16[64,2816]{1,0:T(8,128)(2,1)S(1)} %get-tuple-element.73), channel_id=1, source_target_pairs={{0,2},{2,0},{4,6},{6,4},{1,3},{3,1},{5,7},{7,5},{8,10},{10,8},{12,... | collective-permute-start | bytes 1081352 | tf_op jit(solution)/shard_map/ppermute | solution.py:398
  726.1 19.1 %collective-permute-start.3 = (bf16[64,2816]{1,0:T(8,128)(2,1)S(1)}, bf16[64,2816]{1,0:T(8,128)(2,1)S(1)}, u32[]{:S(2)}, u32[]{:S(2)}) collective-permute-start(bf16[64,2816]{1,0:T(8,128)(2,1)S(1)} %get-tuple-element.72), channel_id=1, source_target_pairs={{0,4},{2,6},{4,0},{6,2},{1,5},{3,7},{5,1},{7,3},{8,12},{10,14},{12... | collective-permute-start | bytes 1081352 | tf_op jit(solution)/shard_map/ppermute | solution.py:398
  729.5 16.5 %collective-permute-start.4 = (bf16[64,2816]{1,0:T(8,128)(2,1)S(1)}, bf16[64,2816]{1,0:T(8,128)(2,1)S(1)}, u32[]{:S(2)}, u32[]{:S(2)}) collective-permute-start(bf16[64,2816]{1,0:T(8,128)(2,1)S(1)} %get-tuple-element.71), channel_id=1, source_target_pairs={{0,6},{2,4},{4,2},{6,0},{1,7},{3,5},{5,3},{7,1},{8,14},{10,12},{12... | collective-permute-start | bytes 1081352 | tf_op jit(solution)/shard_map/ppermute | solution.py:398
  755.9 4.6 copy-start.3
Sparse Core Ops, SparseCore 0:
  428.6 84.5 reduce-scatter.9
  515.6 130.3 reduce-scatter.5
  648.4 75.2 reduce-scatter.7

commit v4 on v3

--- a/solution.py
+++ b/solution.py
@@ -10,6 +10,11 @@
 
 EPSILON = 1e-05
 MASKED = -1e30
+LINE, PLANE, CORE = "dp", "seq", "fsdp"
+EVERY = (LINE, PLANE, CORE)
+SCORES, KEYS = "qhd,kd->hqk", "hqk,qhd->kd"
+ROWS, COLUMNS = "nf,df->nd", "nd,nf->df"
+OUTER, INNER = "nd,ne->de", "ne,de->nd"
 
 
 def rope_tables(places, half_dim):
@@ -51,7 +56,7 @@
     def one_block(block_item):
         block_query, block_place, block_segment = block_item
         scores = (
-            jnp.einsum("qhd,kd->hqk", block_query, keys_seq, preferred_element_type=jnp.float32)
+            jnp.einsum(SCORES, block_query, keys_seq, preferred_element_type=jnp.float32)
             * score_scale
         )
         scores = mask_scores(scores, block_place, block_segment, key_segment)
@@ -82,13 +87,13 @@
         grad_keys, grad_values = running
         block_query, block_grad, block_total, block_place, block_segment = block_item
         scores = (
-            jnp.einsum("qhd,kd->hqk", block_query, keys_seq, preferred_element_type=jnp.float32)
+            jnp.einsum(SCORES, block_query, keys_seq, preferred_element_type=jnp.float32)
             * score_scale
         )
         scores = mask_scores(scores, block_place, block_segment, key_segment)
         soft_weights = jnp.exp(scores - block_total)
         grad_soft = jnp.einsum(
-            "qhd,kd->hqk", block_grad, values_seq, preferred_element_type=jnp.float32
+            SCORES, block_grad, values_seq, preferred_element_type=jnp.float32
         )
         inner_sum = jnp.sum(soft_weights * grad_soft, axis=-1, keepdims=True)
         grad_scores = (soft_weights * (grad_soft - inner_sum)).astype(jnp.bfloat16)
@@ -99,12 +104,12 @@
         grad_keys = (
             grad_keys
             + jnp.einsum(
-                "hqk,qhd->kd", grad_scores, block_query, preferred_element_type=jnp.float32
+                KEYS, grad_scores, block_query, preferred_element_type=jnp.float32
             )
             * score_scale
         )
         grad_values = grad_values + jnp.einsum(
-            "hqk,qhd->kd",
+            KEYS,
             soft_weights.astype(jnp.bfloat16),
             block_grad,
             preferred_element_type=jnp.float32,
@@ -144,23 +149,23 @@
     micro_count, tok_rows, model_width = tokens.shape
     head_dim = w_key.shape[1]
     head_count = model_width // head_dim
-    seq_size = lax.axis_size("seq")
-    pair_size = lax.axis_size("fsdp")
+    seq_size = lax.axis_size(PLANE)
+    pair_size = lax.axis_size(CORE)
     local_heads = head_count // seq_size
     row_count = micro_count * tok_rows
     query_rows = seq_size * tok_rows
     block_rows = min(512, query_rows)
     score_scale = 1.0 / math.sqrt(head_dim)
     gathered = (
-        lax.all_gather(w_query, ("dp", "seq", "fsdp"), axis=0, tiled=True),
-        lax.all_gather(w_key, ("dp", "seq", "fsdp"), axis=0, tiled=True),
-        lax.all_gather(w_value, ("dp", "seq", "fsdp"), axis=0, tiled=True),
-        lax.all_gather(w_out, ("dp", "seq", "fsdp"), axis=0, tiled=True),
-        lax.all_gather(w_gate, ("dp", "seq", "fsdp"), axis=0, tiled=True),
-        lax.all_gather(w_up, ("dp", "seq", "fsdp"), axis=0, tiled=True),
-        lax.all_gather(w_down, ("dp", "seq", "fsdp"), axis=0, tiled=True),
-        lax.all_gather(gain_attn, ("dp", "seq", "fsdp"), axis=0, tiled=True),
-        lax.all_gather(gain_mlp, ("dp", "seq", "fsdp"), axis=0, tiled=True),
+        lax.all_gather(w_query, EVERY, axis=0, tiled=True),
+        lax.all_gather(w_key, EVERY, axis=0, tiled=True),
+        lax.all_gather(w_value, EVERY, axis=0, tiled=True),
+        lax.all_gather(w_out, EVERY, axis=0, tiled=True),
+        lax.all_gather(w_gate, EVERY, axis=0, tiled=True),
+        lax.all_gather(w_up, EVERY, axis=0, tiled=True),
+        lax.all_gather(w_down, EVERY, axis=0, tiled=True),
+        lax.all_gather(gain_attn, EVERY, axis=0, tiled=True),
+        lax.all_gather(gain_mlp, EVERY, axis=0, tiled=True),
     )
     query_mat, key_mat, value_mat, out_mat, gate_mat, up_mat, down_mat, gain_one, gain_two = (
         gathered
@@ -183,12 +188,12 @@
     keys_local = keys_local.reshape(micro_count, tok_rows, head_dim)
     values_local = values_local.reshape(micro_count, tok_rows, head_dim)
     keys_seq, values_seq, segment_seq = (
-        lax.all_gather(keys_local, ("seq", "fsdp"), axis=1, tiled=True),
-        lax.all_gather(values_local, ("seq", "fsdp"), axis=1, tiled=True),
-        lax.all_gather(segments.astype(jnp.bfloat16), ("seq", "fsdp"), axis=1, tiled=True),
+        lax.all_gather(keys_local, (PLANE, CORE), axis=1, tiled=True),
+        lax.all_gather(values_local, (PLANE, CORE), axis=1, tiled=True),
+        lax.all_gather(segments.astype(jnp.bfloat16), (PLANE, CORE), axis=1, tiled=True),
     )
     key_segment = segment_seq.astype(jnp.int32)
-    pair_index = lax.axis_index("fsdp")
+    pair_index = lax.axis_index(CORE)
     query_place = (
         (jnp.arange(seq_size, dtype=jnp.int32)[:, None] * pair_size + pair_index) * tok_rows
         + jnp.arange(tok_rows, dtype=jnp.int32)[None, :]
@@ -201,7 +206,7 @@
     ).reshape(micro_count, query_rows)
     head_queries = lax.all_to_all(
         queries.reshape(micro_count, tok_rows, model_width),
-        "seq",
+        PLANE,
         split_axis=2,
         concat_axis=1,
         tiled=True,
@@ -216,7 +221,7 @@
     )
     mixed_rows = lax.all_to_all(
         attended.reshape(micro_count, query_rows, local_heads * head_dim),
-        "seq",
+        PLANE,
         split_axis=1,
         concat_axis=2,
         tiled=True,
@@ -233,15 +238,15 @@
     hidden_mlp = (gate_silu * up_proj).astype(jnp.bfloat16)
     result = middle + jnp.dot(hidden_mlp, down_mat, preferred_element_type=jnp.float32)
     back_weights = (
-        lax.all_gather(w_query, ("dp", "seq", "fsdp"), axis=0, tiled=True),
-        lax.all_gather(w_key, ("dp", "seq", "fsdp"), axis=0, tiled=True),
-        lax.all_gather(w_value, ("dp", "seq", "fsdp"), axis=0, tiled=True),
-        lax.all_gather(w_out, ("dp", "seq", "fsdp"), axis=0, tiled=True),
-        lax.all_gather(w_gate, ("dp", "seq", "fsdp"), axis=0, tiled=True),
-        lax.all_gather(w_up, ("dp", "seq", "fsdp"), axis=0, tiled=True),
-        lax.all_gather(w_down, ("dp", "seq", "fsdp"), axis=0, tiled=True),
-        lax.all_gather(gain_attn, ("dp", "seq", "fsdp"), axis=0, tiled=True),
-        lax.all_gather(gain_mlp, ("dp", "seq", "fsdp"), axis=0, tiled=True),
+        lax.all_gather(w_query, EVERY, axis=0, tiled=True),
+        lax.all_gather(w_key, EVERY, axis=0, tiled=True),
+        lax.all_gather(w_value, EVERY, axis=0, tiled=True),
+        lax.all_gather(w_out, EVERY, axis=0, tiled=True),
+        lax.all_gather(w_gate, EVERY, axis=0, tiled=True),
+        lax.all_gather(w_up, EVERY, axis=0, tiled=True),
+        lax.all_gather(w_down, EVERY, axis=0, tiled=True),
+        lax.all_gather(gain_attn, EVERY, axis=0, tiled=True),
+        lax.all_gather(gain_mlp, EVERY, axis=0, tiled=True),
     )
     query_mat, key_mat, value_mat, out_mat, gate_mat, up_mat, down_mat, gain_one, gain_two = (
         back_weights
@@ -257,24 +262,24 @@
     ).astype(jnp.bfloat16)
     grad_up_pre = (grad_hidden * gate_silu).astype(jnp.bfloat16)
     grad_gate_w = jnp.einsum(
-        "nd,nf->df", hidden_two, grad_gate_pre, preferred_element_type=jnp.float32
-    )
-    grad_up_w = jnp.einsum("nd,nf->df", hidden_two, grad_up_pre, preferred_element_type=jnp.float32)
+        COLUMNS, hidden_two, grad_gate_pre, preferred_element_type=jnp.float32
+    )
+    grad_up_w = jnp.einsum(COLUMNS, hidden_two, grad_up_pre, preferred_element_type=jnp.float32)
     grad_hidden_two = jnp.einsum(
-        "nf,df->nd", grad_gate_pre, gate_mat, preferred_element_type=jnp.float32
-    ) + jnp.einsum("nf,df->nd", grad_up_pre, up_mat, preferred_element_type=jnp.float32)
+        ROWS, grad_gate_pre, gate_mat, preferred_element_type=jnp.float32
+    ) + jnp.einsum(ROWS, grad_up_pre, up_mat, preferred_element_type=jnp.float32)
     grad_gain_two = jnp.sum(grad_hidden_two * normed_two, axis=0)
     grad_middle = grad_rows + norm_back(
         grad_hidden_two * gain_two.astype(jnp.float32), normed_two, inverse_two
     )
     grad_proj = grad_middle.astype(jnp.bfloat16)
-    grad_out_w = jnp.einsum("nd,ne->de", mixed_rows, grad_proj, preferred_element_type=jnp.float32)
+    grad_out_w = jnp.einsum(OUTER, mixed_rows, grad_proj, preferred_element_type=jnp.float32)
     grad_mixed = jnp.einsum(
-        "ne,de->nd", grad_proj, out_mat, preferred_element_type=jnp.float32
+        INNER, grad_proj, out_mat, preferred_element_type=jnp.float32
     ).astype(jnp.bfloat16)
     grad_heads = lax.all_to_all(
         grad_mixed.reshape(micro_count, tok_rows, model_width),
-        "seq",
+        PLANE,
         split_axis=2,
         concat_axis=1,
         tiled=True,
@@ -292,17 +297,17 @@
         grad_head_queries.reshape(micro_count, query_rows, local_heads * head_dim).astype(
             jnp.bfloat16
         ),
-        "seq",
+        PLANE,
         split_axis=1,
         concat_axis=2,
         tiled=True,
     ).astype(jnp.float32)
     grad_keys_own, grad_values_own = (
         lax.psum_scatter(
-            grad_keys_seq.astype(jnp.bfloat16), ("seq", "fsdp"), scatter_dimension=1, tiled=True
+            grad_keys_seq.astype(jnp.bfloat16), (PLANE, CORE), scatter_dimension=1, tiled=True
         ).astype(jnp.float32),
         lax.psum_scatter(
-            grad_values_seq.astype(jnp.bfloat16), ("seq", "fsdp"), scatter_dimension=1, tiled=True
+            grad_values_seq.astype(jnp.bfloat16), (PLANE, CORE), scatter_dimension=1, tiled=True
         ).astype(jnp.float32),
     )
     grad_query_lin = (
@@ -319,22 +324,22 @@
     )
     grad_value_lin = grad_values_own.reshape(row_count, head_dim).astype(jnp.bfloat16)
     grad_query_w = jnp.einsum(
-        "nd,ne->de", hidden_one, grad_query_lin, preferred_element_type=jnp.float32
+        OUTER, hidden_one, grad_query_lin, preferred_element_type=jnp.float32
     )
     grad_key_w = jnp.einsum(
-        "nd,ne->de", hidden_one, grad_key_lin, preferred_element_type=jnp.float32
+        OUTER, hidden_one, grad_key_lin, preferred_element_type=jnp.float32
     )
     grad_value_w = jnp.einsum(
-        "nd,ne->de", hidden_one, grad_value_lin, preferred_element_type=jnp.float32
+        OUTER, hidden_one, grad_value_lin, preferred_element_type=jnp.float32
     )
     grad_hidden_one = jnp.einsum(
-        "ne,de->nd", grad_query_lin, query_mat, preferred_element_type=jnp.float32
+        INNER, grad_query_lin, query_mat, preferred_element_type=jnp.float32
     )
     grad_hidden_one = grad_hidden_one + jnp.einsum(
-        "ne,de->nd", grad_key_lin, key_mat, preferred_element_type=jnp.float32
+        INNER, grad_key_lin, key_mat, preferred_element_type=jnp.float32
     )
     grad_hidden_one = grad_hidden_one + jnp.einsum(
-        "ne,de->nd", grad_value_lin, value_mat, preferred_element_type=jnp.float32
+        INNER, grad_value_lin, value_mat, preferred_element_type=jnp.float32
     )
     grad_gain_one = jnp.sum(grad_hidden_one * normed_one, axis=0)
     grad_input = grad_middle + norm_back(
@@ -351,12 +356,12 @@
     )
     shards = tuple(
         lax.psum_scatter(
-            grad.astype(jnp.bfloat16), ("dp", "seq", "fsdp"), scatter_dimension=0, tiled=True
+            grad.astype(jnp.bfloat16), EVERY, scatter_dimension=0, tiled=True
         ).astype(jnp.float32)
         for grad in matrix_grads
     ) + (
-        lax.psum_scatter(grad_gain_one, ("dp", "seq", "fsdp"), scatter_dimension=0, tiled=True),
-        lax.psum_scatter(grad_gain_two, ("dp", "seq", "fsdp"), scatter_dimension=0, tiled=True),
+        lax.psum_scatter(grad_gain_one, EVERY, scatter_dimension=0, tiled=True),
+        lax.psum_scatter(grad_gain_two, EVERY, scatter_dimension=0, tiled=True),
     )
     layer_rows = result.reshape(micro_count, tok_rows, model_width).astype(jnp.bfloat16)
     return (
@@ -395,11 +400,11 @@
 
 
 def send_plane(value, step):
-    return lax.ppermute(value, "seq", [(i, i ^ step) for i in range(4)])
+    return lax.ppermute(value, PLANE, [(i, i ^ step) for i in range(4)])
 
 
 def send_core(value):
-    return lax.ppermute(value, "fsdp", [(0, 1), (1, 0)])
+    return lax.ppermute(value, CORE, [(0, 1), (1, 0)])
 
 
 def block_of(value, index, dim=0):
@@ -425,8 +430,8 @@
 
 class Post:
     def __init__(self, send_sem, recv_sem):
-        self.plane=lax.axis_index("dp"); self.own=lax.axis_index("seq"); self.core=lax.axis_index("fsdp")
-        self.planes=lax.axis_size("dp")
+        self.plane=lax.axis_index(LINE); self.own=lax.axis_index(PLANE); self.core=lax.axis_index(CORE)
+        self.planes=lax.axis_size(LINE)
         x=lax.rem(self.own,2); y=lax.div(self.own,2)
         self.by_x=self.own+1-2*x; self.by_y=self.own+2-4*y; self.far=3-self.own
         z,s,c=self.plane,self.own,self.core
@@ -523,10 +528,10 @@
     return dot32(l, r, ((ca,), (cb,)))
 
 
-def front_kernel(plan,tok,cot,marks,wq_in,wo_in,gu_in,wd_in,freq,
-    x_out,marks_out,wq_out,wo_out,gu,wd,E,two,middle_out,h1_out,q_out,att_out,kv_out,home,cos_out,sin_out,
-    send_sem,recv_sem,local_sem,b_cot,b_gu,b_wd,
-    x_v,marks_v,wq_v,wo_v,h1_v,lin_v,q_v,att_v,kv_v,mid_v,two_v,cos_v,sin_v,gain_v):
+def front_kernel(plan,tok,cot,marks,wq_in,wo_in,gu_in,freq,
+    x_out,marks_out,wq_out,wo_out,gu,E,two,middle_out,h1_out,q_out,att_out,kv_out,home,cos_out,sin_out,
+    send_sem,recv_sem,local_sem,b_cot,b_gu,
+    x_v,marks_v,wq_v,wo_v,h1_v,lin_v,q_v,att_v,kv_v,mid_v,two_v,cos_v,sin_v,gain_v,h1t_v,att_t_v):
     tile,width,head_dim,group=plan
     scale=head_dim**-0.5
     p=Post(send_sem,recv_sem)
@@ -543,7 +548,7 @@
     def out(src,dst):
         outs_.append(local(src,dst))
     loads=[local(tok.at[s],x_v.at[s]),local(marks.at[s],marks_v.at[c,s]),local(wq_in,wq_v.at[z,s,c]),local(wo_in,wo_v.at[z,s,c])]
-    late=[local(cot,b_cot),local(gu_in.at[s],b_gu),local(wd_in,b_wd)]
+    late=[local(cot,b_cot),local(gu_in.at[s],b_gu)]
     p.barrier()
     def attention_weight(name, arr, src):
         n=arr.shape[3]//2
@@ -564,24 +569,28 @@
     def swapped(dst_of,name):
         for i,(t,o) in enumerate(others):
             p.wait(dst_of(o),name,i)
+    swap(gu_in,lambda b: gu.at[z,b,c],"gu")
     q_line.start()
+    q_spread.start(z,wq_in)
     swap(tok,lambda b: x_v.at[b],"tok")
-    q_spread.start(z,wq_in)
     for i,(t,o) in enumerate(others):
         p.send(marks.at[o],marks_v.at[c,s],"mk",i,t)
         p.send(marks.at[o],marks_v.at[c,s],"mk2",i,(z,o,1-c))
     p.send(marks.at[s],marks_v.at[c,s],"mk2",3,p.to_core)
     fwd=lambda a,here: q_spread.start(a,wq_v.at[a,s,c],(here,))
-    wd_line=Line(p,"wd_z",lambda a: wd.at[a,c],wd_in)
+    gufwd=lambda a,here: to_sibling("gu",gu,a,(here,))
+    ofwd=lambda a,here: o_spread.start(a,wo_v.at[a,s,c],(here,))
     gu_line=Line(p,"gu_z",lambda a: gu.at[a,:,c],gu.at[z,:,c])
+    for cp in loads+late: cp.wait()
+    out(b_cot,E.at[:,s]); out(b_gu,gu.at[z,s,c]); own_gu=outs_[-1]
     q_line.hop(1,fwd)
-    wd_line.start()
     q_line.hop(2,fwd)
     q_line.hop(3,fwd)
-    swap(gu_in,lambda b: gu.at[z,b,c],"gu")
-    for cp in loads+late: cp.wait()
-    out(b_cot,E.at[:,s]); out(b_gu,gu.at[z,s,c]); own_gu=outs_[-1]; out(b_wd,wd.at[z,c]); own_wd=outs_[-1]
+    swapped(lambda b: gu.at[z,b,c],"gu")
+    own_gu.wait(); outs_[:]=[o for o in outs_ if o is not own_gu]
+    gu_line.start(); to_sibling("gu",gu,z,())
     for k in range(4): each(k,lambda a,w: q_spread.relay(a,w))
+    gu_line.hop(1,gufwd)
     o_line.start(); o_spread.start(z,wo_in)
     def each_q(a,w):
         q_spread.arrive(a,w); to_sibling("wq",wq_v,a,w)
@@ -590,13 +599,8 @@
     for i,(t,o) in enumerate(others):
         p.wait(marks_v.at[c,o],"mk",i); p.wait(marks_v.at[1-c,o],"mk2",i)
     p.wait(marks_v.at[1-c,s],"mk2",3)
-    swapped(lambda b: gu.at[z,b,c],"gu")
-    own_gu.wait(); outs_[:]=[o for o in outs_ if o is not own_gu]
-    gu_line.start(); to_sibling("gu",gu,z,())
     for a in range(4): p.wait(wq_v.at[a,:,1-c],"wq_c",a)
     out(x_v,x_out); out(marks_v,marks_out); out(wq_v,wq_out)
-    ofwd=lambda a,here: o_spread.start(a,wo_v.at[a,s,c],(here,))
-    gufwd=lambda a,here: to_sibling("gu",gu,a,(here,))
     e_parts=[]
     for i in range(2):
         def sub(lo,n,i=i): return lambda _,b: E.at[pl.ds(2*i+lo,n),b]
@@ -608,6 +612,7 @@
         a,b=divmod(i,4)
         block=wq_v[a,b,:,:,pl.ds(qkv,head_dim)].reshape(head_dim,head_dim).astype(F32)
         gain_v[:,pl.ds(i*head_dim,head_dim)]=jnp.transpose(block)[0:8]
+    e_start(0); e_start(1)
     def norm_block(b,carry):
         x=x_v[b].astype(F32)
         inv=lax.rsqrt(jnp.mean(x*x,axis=-1,keepdims=True)+EPSILON)
@@ -630,12 +635,12 @@
     kv_v[:,pl.ds(c,1)]=kv.reshape(chips,1,tile,2*head_dim)
     p.send(kv_v.at[:,c],kv_v.at[:,c],"kv",0,p.to_core)
     swap(kv_v.at[:,c],lambda b: home.at[b],"home")
-    out(kv_v.at[s,c],home.at[s]); out(h1_v,h1_out); out(cos_v,cos_out); out(sin_v,sin_out)
+    out(kv_v.at[s,c],home.at[s]); out(cos_v,cos_out); out(sin_v,sin_out)
     steps={0:[lambda: o_line.hop(2,ofwd)],
            1:[lambda: p.wait(kv_v.at[:,1-c],"kv",0), lambda: o_line.hop(3,ofwd)],
-           2:[lambda: wd_line.hop(1), lambda: each(0,lambda a,w: o_spread.relay(a,w)), lambda: each(1,lambda a,w: o_spread.relay(a,w))],
-           3:[lambda: each(2,lambda a,w: o_spread.relay(a,w)), lambda: each(3,lambda a,w: o_spread.relay(a,w)),lambda: gu_line.hop(1,gufwd)],
-           4:[lambda: wd_line.hop(2), lambda: e_start(0)]}
+           2:[lambda: each(0,lambda a,w: o_spread.relay(a,w)), lambda: each(1,lambda a,w: o_spread.relay(a,w))],
+           3:[lambda: each(2,lambda a,w: o_spread.relay(a,w)), lambda: each(3,lambda a,w: o_spread.relay(a,w))],
+           4:[]}
     def lin_group(g,carry):
         w=wq_v[:,:,:,:,pl.ds(pl.multiple_of(g*group,group),group)].reshape(width,group)
         lin_v[...]=dot2(h1_v[...],w,1,0)
@@ -648,6 +653,7 @@
     for f in steps[0]: f()
     lax.fori_loop(0,groups,lin_group,0)
     for f in steps[1]: f()
+    gu_line.hop(2,gufwd)
     out(kv_v,kv_out); out(q_v,q_out)
     def attend_group(g,carry):
         for b in range(chips):
@@ -673,7 +679,6 @@
                 for f in steps[i]: f()
         return carry
     lax.fori_loop(0,groups,attend_group,0)
-    out(att_v,att_out)
     def each_o(a,w):
         o_spread.arrive(a,w); to_sibling("wo",wo_v,a,w)
     for k in range(4): each(k,each_o)
@@ -687,6 +692,8 @@
         for b in range(chips):
             mid_v[pl.ds(b*tile,tile),at]=x_v[b,:,at].astype(F32)+lin_v[pl.ds(b*tile,tile),:]
         return carry
+    e_parts[0].relay(0)
+    e_parts[1].relay(0)
     lax.fori_loop(0,groups,project,0)
     out(mid_v,middle_out)
     def norm_two(b,carry):
@@ -696,31 +703,23 @@
         two_v[at,:]=(m*inv*gain_v[1:2,:]).astype(BF16)
         return carry
     lax.fori_loop(0,chips,norm_two,0)
-    half=rows//2
-    two_spread=Spread(p,"two",lambda _,b: two.at[b],lambda _,b: two.at[b,pl.ds(0,half)],lambda _,b: two.at[b,pl.ds(half,half)])
-    two_spread.start(0,two_v)
-    out(two_v,two.at[s])
-    e_start(1)
-    wd_line.hop(3)
-    gu_line.hop(2,gufwd)
-    e_parts[0].relay(0)
-    own_wd.wait(); outs_[:]=[o for o in outs_ if o is not own_wd]
-    p.send(wd.at[:,c],wd.at[:,c],"wd_c",0,p.to_core)
+    out(two_v,two)
+    for i in range(width//head_dim):
+        at=slice(i*head_dim,(i+1)*head_dim)
+        h1t_v[at,:]=jnp.transpose(h1_v[:,at])
+        att_t_v[at,:]=jnp.transpose(att_v[:,at])
+    out(h1t_v,h1_out); out(att_t_v,att_out)
     gu_line.hop(3,gufwd)
-    two_spread.relay(0)
     e_parts[0].arrive(0)
-    e_parts[1].relay(0)
-    two_spread.arrive(0)
     e_parts[1].arrive(0)
-    p.wait(wd.at[:,1-c],"wd_c",0)
     for a in range(4): p.wait(gu.at[a,:,1-c],"gu_c",a)
     swapped(lambda b: home.at[b],"home")
     for cp in outs_: cp.wait()
     p.finish()
     assert len(p.groups)<=GROUPS, len(p.groups)
 
-def front(tok,cot,marks,wq_in,wo_in,gu_in,wd_in):
-    Z,S,C=lax.axis_size("dp"),lax.axis_size("seq"),lax.axis_size("fsdp")
+def front(tok,cot,marks,wq_in,wo_in,gu_in):
+    Z,S,C=lax.axis_size(LINE),lax.axis_size(PLANE),lax.axis_size(CORE)
     sd=jax.ShapeDtypeStruct
     micro,tile,width=tok.shape
     rows=micro*tile
@@ -730,19 +729,19 @@
     freq=jnp.exp(-jnp.log(jnp.float32(10000.0))*jnp.arange(half,dtype=F32)/half)
     freq=jnp.concatenate([freq,freq])[None]
     outs=[sd((S,tile,width),BF16),sd((C,)+marks.shape,jnp.int32),sd((Z,S,C)+wq_in.shape,BF16),sd((Z,S,C)+wo_in.shape,BF16),
-          sd((Z,S,C)+gu_in.shape[1:],BF16),sd((Z,C)+wd_in.shape,BF16),sd((S,)+cot.shape,BF16),
-          sd((S,rows,width),BF16),sd((rows,width),F32),sd((rows,width),BF16),sd((rows,width),BF16),sd((rows,width),BF16),
+          sd((Z,S,C)+gu_in.shape[1:],BF16),sd((S,)+cot.shape,BF16),
+          sd((rows,width),BF16),sd((rows,width),F32),sd((width,rows),BF16),sd((rows,width),BF16),sd((width,rows),BF16),
           sd((S,C,tile,2*head_dim),BF16),sd((S,tile,2*head_dim),BF16),sd((rows,head_dim),F32),sd((rows,head_dim),F32)]
     anyspec=pl.BlockSpec(memory_space=pl.ANY)
     V=pltpu.VMEM
     return pl.pallas_call(functools.partial(front_kernel,(tile,width,head_dim,group)),out_shape=outs,
-        in_specs=[anyspec]*7+[pl.BlockSpec(memory_space=V)],out_specs=[anyspec]*len(outs),
+        in_specs=[anyspec]*6+[pl.BlockSpec(memory_space=V)],out_specs=[anyspec]*len(outs),
         scratch_shapes=[pltpu.SemaphoreType.DMA((GROUPS,4)),pltpu.SemaphoreType.DMA((GROUPS,4)),pltpu.SemaphoreType.DMA((32,)),
-          V(cot.shape,BF16),V(gu_in.shape[1:],BF16),V(wd_in.shape,BF16),
+          V(cot.shape,BF16),V(gu_in.shape[1:],BF16),
           V((S,tile,width),BF16),V((C,)+marks.shape,jnp.int32),V((Z,S,C)+wq_in.shape,BF16),V((Z,S,C)+wo_in.shape,BF16),
           V((rows,width),BF16),V((rows,group),F32),V((rows,width),BF16),V((rows,width),BF16),V((S,C,tile,2*head_dim),BF16),
-          V((rows,width),F32),V((rows,width),BF16),V((rows,head_dim),F32),V((rows,head_dim),F32),V((8,width),F32)],
-        compiler_params=pltpu.CompilerParams(collective_id=1,has_side_effects=True,vmem_limit_bytes=60*1024*1024),name="front")(tok,cot,marks,wq_in,wo_in,gu_in,wd_in,freq)
+          V((rows,width),F32),V((rows,width),BF16),V((rows,head_dim),F32),V((rows,head_dim),F32),V((8,width),F32),V((width,rows),BF16),V((width,rows),BF16)],
+        compiler_params=pltpu.CompilerParams(collective_id=1,has_side_effects=True,vmem_limit_bytes=60*1024*1024),cost_estimate=pl.CostEstimate(flops=20_000_000_000,bytes_accessed=100_000_000,transcendentals=10_000_000),name="front")(tok,cot,marks,wq_in,wo_in,gu_in,freq)
 
 
 def back_kernel(
@@ -1226,7 +1225,7 @@
             collective_id=2, has_side_effects=True, vmem_limit_bytes=63 * 1024 * 1024
         ),
         cost_estimate=pl.CostEstimate(
-            flops=60_000_000_000, bytes_accessed=60_000_000, transcendentals=10_000_000
+            flops=1_000_000_000, bytes_accessed=1_000_000, transcendentals=0
         ),
         name="back",
     )(gh2, grads_in, middle, x_in, wq, wo, h1t, q, att_t, kv, cosine, sine, marks, gains)
@@ -1234,11 +1233,12 @@
 
 def middle_kernel(
     plan,
-    two,
+    two_in,
     grads,
     gate_up,
     down,
     residual,
+    two_out,
     pre_out,
     hidden_out,
     partial_out,
@@ -1248,7 +1248,8 @@
     local_sem,
     gu_v,
     down_v,
-    res_v,
+    res_b,
+    out_b,
     two_v,
     e_v,
     pre_v,
@@ -1267,46 +1268,67 @@
     rows, width, hidden = plan
     half = width // 2
     wide_tile, out_tile = 256, 512
+    tiles = width // out_tile
     p = Post(send_sem, recv_sem)
     low, high = pl.ds(0, half), pl.ds(half, half)
-    order = (p.far, p.by_x, p.by_y, p.own)
-    targets = (far_v, x_v, y_v, own_v)
+    top, bottom = pl.ds(0, rows // 2), pl.ds(rows // 2, rows // 2)
+    order = (p.own, p.by_x, p.by_y, p.far)
+    targets = (own_v, x_v, y_v, far_v)
 
     def load(src, dst, index):
         return pltpu.make_async_copy(src, dst, local_sem.at[index])
 
     def fetch(i):
-        return (
-            load(two.at[order[i]], two_v.at[i % 2], 2 * (i % 2)),
-            load(grads.at[order[i]], e_v.at[i % 2], 2 * (i % 2) + 1),
-        )
+        return load(grads.at[order[i]], e_v, 0)
 
     def keep_pre(i):
         at = pl.ds(pl.multiple_of(order[i] * rows, rows), rows)
-        return load(pre_v, pre_out.at[at], 4)
+        return load(pre_v, pre_out.at[at], 1)
 
     def keep_hidden(i):
         at = pl.ds(pl.multiple_of(order[i] * rows, rows), rows)
-        return load(hidden_v.at[i], hidden_out.at[at], 5 + i)
-
-    def place(i):
-        return load(two_v.at[i % 2], partial_out.at[order[i]], i % 2)
-
-    weights = [load(gate_up, gu_v, 9), load(down, down_v, 10), load(residual, res_v, 11)]
-    for cp in list(fetch(0)) + weights:
+        return load(hidden_v.at[i], hidden_out.at[at], 2 + i)
+
+    def keep_two(i):
+        return load(two_v.at[order[i]], two_out.at[order[i]], 6 + i)
+
+    def columns(n):
+        return pl.ds(pl.multiple_of(n * out_tile, out_tile), out_tile)
+
+    def residual_tile(n):
+        return load(residual.at[:, columns(n)], res_b.at[lax.rem(n, 2)], 10 + lax.rem(n, 2))
+
+    def place(i, n):
+        slot = lax.rem(n, 2)
+        return load(out_b.at[slot], partial_out.at[order[i], :, columns(n)], 12 + slot)
+
+    weights = [load(gate_up, gu_v, 14), load(down, down_v, 15)]
+    mine = load(two_in, two_v.at[p.own], 16)
+    for cp in [mine, fetch(0)] + weights:
         cp.start()
+    residual_tile(0).start()
     bar = pltpu.get_barrier_semaphore()
     for target in (p.to_x, p.to_y):
         pl.semaphore_signal(bar, inc=1, device_id=target, device_id_type=MESH)
     pl.semaphore_wait(bar, 2)
-    for cp in weights:
+    sends = [
+        p.copy(two_in, two_v.at[p.own], "two_x", 0, p.to_x),
+        p.copy(two_in, two_v.at[p.own], "two_y", 0, p.to_y),
+    ]
+    relays = [
+        p.copy(two_v.at[p.by_x, top], two_v.at[p.by_x, top], "two_l", 0, p.to_y),
+        p.copy(two_v.at[p.by_y, bottom], two_v.at[p.by_y, bottom], "two_h", 0, p.to_x),
+    ]
+    for cp in sends:
+        cp.start()
+    for cp in weights + [mine]:
         cp.wait()
 
     def chunk(i, start, size):
         at, above = pl.ds(start, size), pl.ds(start + hidden, size)
-        gate = dot2(two_v[i % 2], gu_v[:, at], 1, 0)
-        up = dot2(two_v[i % 2], gu_v[:, above], 1, 0)
-        grad = dot2(e_v[i % 2], down_v[at, :], 1, 1)
+        gate = dot2(two_v[order[i]], gu_v[:, at], 1, 0)
+        up = dot2(two_v[order[i]], gu_v[:, above], 1, 0)
+        grad = dot2(e_v[...], down_v[at, :], 1, 1)
         sig = jax.nn.sigmoid(gate)
         silu = gate * sig
         hidden_v[i, :, at] = (silu * up).astype(BF16)
@@ -1314,13 +1336,22 @@
         pre_v[:, above] = (grad * silu).astype(BF16)
 
     whole_tiles = hidden // wide_tile
-    sends = []
+    x_low = p.copy(x_v.at[:, low], xa_own, "xa_own", 0, p.to_x)
+    y_high = p.copy(y_v.at[:, high], yb_own, "yb_own", 0, p.to_y)
+    far_low = p.copy(far_v.at[:, low], xa_far, "xa_far", 0, p.to_x)
+    far_high = p.copy(far_v.at[:, high], yb_far, "yb_far", 0, p.to_y)
+    x_high = p.copy(x_v.at[:, high], xb_pass, "xb_pass", 0, p.to_x)
+    y_low = p.copy(y_v.at[:, low], ya_pass, "ya_pass", 0, p.to_y)
     for i in range(4):
-        for cp in fetch(i):
-            cp.wait()
-        if i < 3:
-            for cp in fetch(i + 1):
-                cp.start()
+        if i == 1:
+            for cp, relay in zip(sends, relays):
+                cp.wait_recv()
+                relay.start()
+        if i == 3:
+            for relay in relays:
+                relay.wait_recv()
+        fetch(i).wait()
+        keep_two(i).start()
 
         def step(j, carry, i=i):
             chunk(i, pl.multiple_of(j * wide_tile, wide_tile), wide_tile)
@@ -1329,54 +1360,56 @@
         lax.fori_loop(0, whole_tiles, step, 0)
         if hidden % wide_tile:
             chunk(i, whole_tiles * wide_tile, hidden % wide_tile)
+        if i < 3:
+            fetch(i + 1).start()
         keep_pre(i).start()
         keep_hidden(i).start()
 
         def back_tile(n, carry, i=i):
-            at = pl.ds(pl.multiple_of(n * out_tile, out_tile), out_tile)
-            targets[i][:, at] = dot2(pre_v[...], gu_v[at, :], 1, 1).astype(BF16)
+            targets[i][:, columns(n)] = dot2(pre_v[...], gu_v[columns(n), :], 1, 1).astype(BF16)
             return carry
 
-        lax.fori_loop(0, width // out_tile, back_tile, 0)
+        lax.fori_loop(0, tiles, back_tile, 0)
         keep_pre(i).wait()
-        if i == 0:
-            go = [
-                p.copy(far_v.at[:, low], xa_far, "xa_far", 0, p.to_x),
-                p.copy(far_v.at[:, high], yb_far, "yb_far", 0, p.to_y),
-            ]
-        elif i == 1:
-            go = [p.copy(x_v.at[:, low], xa_own, "xa_own", 0, p.to_x)]
-            sends[1].wait_recv()
-            x_v[:, high] = (x_v[:, high].astype(F32) + yb_far[...].astype(F32)).astype(BF16)
-            go.append(p.copy(x_v.at[:, high], xb_pass, "xb_pass", 0, p.to_x))
-        elif i == 2:
-            go = [p.copy(y_v.at[:, high], yb_own, "yb_own", 0, p.to_y)]
-            sends[0].wait_recv()
-            y_v[:, low] = (y_v[:, low].astype(F32) + xa_far[...].astype(F32)).astype(BF16)
-            go.append(p.copy(y_v.at[:, low], ya_pass, "ya_pass", 0, p.to_y))
-        else:
-            go = []
-        for cp in go:
+        for cp in ((), (x_low,), (y_high,), (far_low, far_high))[i]:
             cp.start()
-        sends += go
-
-    for i in range(4):
-        if i >= 2:
-            place(i - 2).wait()
-
-        def out_chunk(n, carry, i=i):
-            at = pl.ds(pl.multiple_of(n * out_tile, out_tile), out_tile)
-            part = dot2(hidden_v[i], down_v[:, at], 1, 0)
-            if i == 3:
-                part = part + res_v[:, at]
-            two_v[i % 2, :, at] = part.astype(BF16)
+
+    def output(i):
+        def out_chunk(n, carry):
+            @pl.when(n >= 2)
+            def _():
+                place(i, n - 2).wait()
+
+            part = dot2(hidden_v[i], down_v[:, columns(n)], 1, 0)
+            if i == 0:
+
+                @pl.when(n + 1 < tiles)
+                def _():
+                    residual_tile(n + 1).start()
+
+                residual_tile(n).wait()
+                part = part + res_b[lax.rem(n, 2)]
+            out_b[lax.rem(n, 2)] = part.astype(BF16)
+            place(i, n).start()
             return carry
 
-        lax.fori_loop(0, width // out_tile, out_chunk, 0)
-        place(i).start()
+        lax.fori_loop(0, tiles, out_chunk, 0)
+        place(i, tiles - 2).wait()
+        place(i, tiles - 1).wait()
+
+    for i in (0, 1, 2):
+        output(i)
+    far_high.wait_recv()
+    x_v[:, high] = (x_v[:, high].astype(F32) + yb_far[...].astype(F32)).astype(BF16)
+    x_high.start()
+    far_low.wait_recv()
+    y_v[:, low] = (y_v[:, low].astype(F32) + xa_far[...].astype(F32)).astype(BF16)
+    y_low.start()
+    output(3)
     for i in range(4):
         keep_hidden(i).wait()
-    for cp in sends[2:]:
+        keep_two(i).wait()
+    for cp in (x_low, y_low, y_high, x_high):
         cp.wait_recv()
     own_v[:, low] = (
         own_v[:, low].astype(F32) + xa_own[...].astype(F32) + ya_pass[...].astype(F32)
@@ -1384,17 +1417,16 @@
     own_v[:, high] = (
         own_v[:, high].astype(F32) + yb_own[...].astype(F32) + xb_pass[...].astype(F32)
     ).astype(BF16)
-    done = load(own_v, sum_out, 4)
+    done = load(own_v, sum_out, 0)
     done.start()
-    place(2).wait()
-    place(3).wait()
     done.wait()
-    for cp in sends:
+    for cp in sends + relays + [x_low, x_high, y_low, y_high, far_low, far_high]:
         cp.wait_send()
 
 
 def middle_call(two, grads, gate_up, down, residual):
-    chips, rows, width = two.shape
+    chips = grads.shape[0]
+    rows, width = two.shape
     hidden = down.shape[0]
     V = pltpu.VMEM
     sd = jax.ShapeDtypeStruct
@@ -1404,22 +1436,24 @@
     return pl.pallas_call(
         functools.partial(middle_kernel, (rows, width, hidden)),
         out_shape=[
+            sd((chips,) + block, BF16),
             sd((chips * rows, 2 * hidden), BF16),
             sd((chips * rows, hidden), BF16),
             sd((chips,) + block, BF16),
             sd(block, BF16),
         ],
         in_specs=[anyspec] * 5,
-        out_specs=[anyspec] * 4,
+        out_specs=[anyspec] * 5,
         scratch_shapes=[
-            pltpu.SemaphoreType.DMA((8, 4)),
-            pltpu.SemaphoreType.DMA((8, 4)),
-            pltpu.SemaphoreType.DMA((12,)),
+            pltpu.SemaphoreType.DMA((10, 4)),
+            pltpu.SemaphoreType.DMA((10, 4)),
+            pltpu.SemaphoreType.DMA((17,)),
             V((width, 2 * hidden), BF16),
             V((hidden, width), BF16),
-            V(block, F32),
-            V((2,) + block, BF16),
-            V((2,) + block, BF16),
+            V((2, rows, 512), F32),
+            V((2, rows, 512), BF16),
+            V((chips,) + block, BF16),
+            V(block, BF16),
             V((rows, 2 * hidden), BF16),
             V((chips, rows, hidden), BF16),
         ]
@@ -1433,6 +1467,228 @@
         ),
         name="feed_forward",
     )(two, grads, gate_up, down, residual)
+
+
+def trade_kernel(blocks, gate_out, up_out, got, send_sem, recv_sem, local_sem):
+    chips, shard, columns = got.shape
+    piece = columns // 8
+    p = Post(send_sem, recv_sem)
+    others = ((p.to_x, p.by_x), (p.to_y, p.by_y), (p.to_far, p.far))
+    mine = pltpu.make_async_copy(blocks.at[p.own], got.at[p.own], local_sem.at[0])
+    mine.start()
+    bar = pltpu.get_barrier_semaphore()
+    for target, _ in others:
+        pl.semaphore_signal(bar, inc=1, device_id=target, device_id_type=MESH)
+    pl.semaphore_wait(bar, 3)
+    copies = [
+        p.copy(blocks.at[o], got.at[p.own], "trade", i, t) for i, (t, o) in enumerate(others)
+    ]
+    for cp in copies:
+        cp.start()
+    mine.wait()
+    for cp in copies:
+        cp.wait_recv()
+    for half, out in enumerate((gate_out, up_out)):
+        parts = [
+            got[chip, :, (half * 4 + plane) * piece : (half * 4 + plane + 1) * piece].astype(F32)
+            for plane in range(4)
+            for chip in range(chips)
+        ]
+        out[...] = jnp.concatenate(parts, axis=1)
+    for cp in copies:
+        cp.wait_send()
+
+
+def trade(blocks, hidden):
+    chips, shard, columns = blocks.shape
+    V = pltpu.VMEM
+    return pl.pallas_call(
+        trade_kernel,
+        out_shape=[jax.ShapeDtypeStruct((shard, hidden), F32)] * 2,
+        in_specs=[pl.BlockSpec(memory_space=pl.ANY)],
+        out_specs=[pl.BlockSpec(memory_space=V)] * 2,
+        scratch_shapes=[
+            V(blocks.shape, BF16),
+            pltpu.SemaphoreType.DMA((1, 4)),
+            pltpu.SemaphoreType.DMA((1, 4)),
+            pltpu.SemaphoreType.DMA((1,)),
+        ],
+        compiler_params=pltpu.CompilerParams(
+            collective_id=4, has_side_effects=True, vmem_limit_bytes=32 * 1024 * 1024
+        ),
+        name="trade",
+    )(blocks)
+
+
+class PlaneSum:
+    def __init__(self, post, partial, column, buffers, local_sem):
+        p = self.p = post
+        self.x_v, self.y_v, self.own_v = buffers[:3]
+        self.xa_far, self.xa_own, self.yb_far, self.yb_own, self.ya_pass, self.xb_pass = buffers[3:]
+        half = self.xa_far.shape[-1]
+        self.low, self.high = pl.ds(0, half), pl.ds(half, half)
+        low, high, both = (
+            pl.ds(column, half),
+            pl.ds(column + half, half),
+            pl.ds(column, 2 * half),
+        )
+        self.loads = [
+            pltpu.make_async_copy(partial.at[:, chip, :, both], ref, local_sem.at[i])
+            for i, (chip, ref) in enumerate(
+                ((p.by_x, self.x_v), (p.by_y, self.y_v), (p.own, self.own_v))
+            )
+        ]
+        self.far_low = p.copy(partial.at[:, p.far, :, low], self.xa_far, "xa_far", 0, p.to_x)
+        self.far_high = p.copy(partial.at[:, p.far, :, high], self.yb_far, "yb_far", 0, p.to_y)
+        self.x_low = p.copy(partial.at[:, p.by_x, :, low], self.xa_own, "xa_own", 0, p.to_x)
+        self.y_high = p.copy(partial.at[:, p.by_y, :, high], self.yb_own, "yb_own", 0, p.to_y)
+        self.x_high = p.copy(self.x_v.at[:, :, self.high], self.xb_pass, "xb_pass", 0, p.to_x)
+        self.y_low = p.copy(self.y_v.at[:, :, self.low], self.ya_pass, "ya_pass", 0, p.to_y)
+
+    def start(self):
+        for cp in [self.far_low, self.far_high, self.x_low, self.y_high] + self.loads:
+            cp.start()
+
+    def turn(self):
+        for cp in self.loads:
+            cp.wait()
+        self.far_high.wait_recv()
+        total = self.x_v[:, :, self.high].astype(F32) + self.yb_far[...].astype(F32)
+        self.x_v[:, :, self.high] = total.astype(BF16)
+        self.x_high.start()
+        self.far_low.wait_recv()
+        total = self.y_v[:, :, self.low].astype(F32) + self.xa_far[...].astype(F32)
+        self.y_v[:, :, self.low] = total.astype(BF16)
+        self.y_low.start()
+
+    def finish(self, out, sem):
+        for cp in (self.x_low, self.y_low, self.y_high, self.x_high):
+            cp.wait_recv()
+        for at, direct, passed in (
+            (self.low, self.xa_own, self.ya_pass),
+            (self.high, self.yb_own, self.xb_pass),
+        ):
+            total = self.own_v[:, :, at].astype(F32) + direct[...].astype(F32)
+            self.own_v[:, :, at] = (total + passed[...].astype(F32)).astype(BF16)
+        done = pltpu.make_async_copy(self.own_v, out, sem)
+        done.start()
+        done.wait()
+        for cp in (self.far_low, self.far_high, self.x_low, self.y_high, self.x_high, self.y_low):
+            cp.wait_send()
+
+
+def weight_grad_kernel(
+    plan, left, right, partial, sum_out, rows_out, send_sem, recv_sem, local_sem, *scratch
+):
+    turned, width, tile, column = plan
+    left_v, right_v, left_t, stage, got, total_v = scratch[:6]
+    planes = got.shape[0]
+    p = Post(send_sem, recv_sem)
+    c = p.core
+    plane_sum = PlaneSum(p, partial, column, scratch[6:], local_sem)
+    load_left = pltpu.make_async_copy(left, left_v, local_sem.at[3])
+    load_right = pltpu.make_async_copy(right, right_v, local_sem.at[4])
+    load_left.start()
+    load_right.start()
+    bar = pltpu.get_barrier_semaphore()
+    for target in (p.to_x, p.to_y, p.to_core):
+        pl.semaphore_signal(bar, inc=1, device_id=target, device_id_type=MESH)
+    pl.semaphore_wait(bar, 3)
+    plane_sum.start()
+    height = 1
+    for size in stage.shape[1:-1]:
+        height *= size
+    rank = len(stage.shape) - 1
+    own = (slice(None),) * (rank - 3) + (c,)
+    other = (slice(None),) * (rank - 3) + (1 - c,)
+
+    def to_core(z):
+        return p.copy(stage.at[(z % 2,) + other], got.at[z], "core", z, p.to_core)
+
+    def keep(z):
+        return pltpu.make_async_copy(total_v.at[z % 2], sum_out.at[z], local_sem.at[5 + z % 2])
+
+    def add(z):
+        to_core(z).wait_recv()
+        if z >= 2:
+            keep(z - 2).wait()
+        mine = stage[(z % 2,) + own].astype(F32)
+        total_v[z % 2] = (mine + got[z].astype(F32)).astype(BF16)
+        keep(z).start()
+
+    load_left.wait()
+    for z in range(planes):
+        if z >= 2:
+            to_core(z - 2).wait_send()
+        start = z * height
+        first = start // turned * turned
+        last = -(-(start + height) // turned) * turned
+        for at in range(first, last, turned):
+            if at >= start or z == 0:
+                left_t[pl.ds(at, turned), :] = jnp.transpose(left_v[:, at : at + turned])
+        if z == 0:
+            load_right.wait()
+
+        def columns(n, carry, z=z, start=start):
+            at = pl.ds(pl.multiple_of(n * tile, tile), tile)
+            part = dot2(left_t[pl.ds(start, height), :], right_v[:, at], 1, 0).astype(BF16)
+            stage[z % 2, ..., at] = part.reshape(stage.shape[1:-1] + (tile,))
+            return carry
+
+        lax.fori_loop(0, width // tile, columns, 0)
+        to_core(z).start()
+        if z >= 1:
+            add(z - 1)
+        if z == 2:
+            plane_sum.turn()
+    add(planes - 1)
+    plane_sum.finish(rows_out, local_sem.at[7])
+    for z in (planes - 2, planes - 1):
+        keep(z).wait()
+        to_core(z).wait_send()
+
+
+def weight_grad(left, right, partial, block, tile, column, name, identity):
+    planes = block[0]
+    rows, height = left.shape
+    width = right.shape[1]
+    chips, tokens = partial.shape[0], partial.shape[2]
+    half = partial.shape[3] // 4
+    V = pltpu.VMEM
+    anyspec = pl.BlockSpec(memory_space=pl.ANY)
+    inner = block[1:]
+    kept = inner[:-2] + inner[-1:]
+    part = (chips, tokens, half)
+    both = (chips, tokens, 2 * half)
+    return pl.pallas_call(
+        functools.partial(weight_grad_kernel, (128, width, tile, column)),
+        out_shape=[
+            jax.ShapeDtypeStruct((planes,) + kept + (width,), BF16),
+            jax.ShapeDtypeStruct(both, BF16),
+        ],
+        in_specs=[anyspec] * 3,
+        out_specs=[anyspec] * 2,
+        scratch_shapes=[
+            pltpu.SemaphoreType.DMA((7, 4)),
+            pltpu.SemaphoreType.DMA((7, 4)),
+            pltpu.SemaphoreType.DMA((8,)),
+            V(left.shape, BF16),
+            V(right.shape, BF16),
+            V((height, rows), BF16),
+            V((2,) + inner + (width,), BF16),
+            V((planes,) + kept + (width,), BF16),
+            V((2,) + kept + (width,), BF16),
+        ]
+        + [V(both, BF16)] * 3
+        + [V(part, BF16)] * 6,
+        compiler_params=pltpu.CompilerParams(
+            collective_id=identity, has_side_effects=True, vmem_limit_bytes=62 * 1024 * 1024
+        ),
+        cost_estimate=pl.CostEstimate(
+            flops=2 * rows * height * width, bytes_accessed=40_000_000, transcendentals=0
+        ),
+        name=name,
+    )(left, right, partial)
 
 
 def body_plane(
@@ -1453,12 +1709,12 @@
     micro, tile, width = tokens.shape
     head_dim = w_key.shape[1]
     head_count = width // head_dim
-    planes = lax.axis_size("dp")
-    chips = lax.axis_size("seq")
-    pair = lax.axis_size("fsdp")
-    plane = lax.axis_index("dp")
-    own = lax.axis_index("seq")
-    core = lax.axis_index("fsdp")
+    planes = lax.axis_size(LINE)
+    chips = lax.axis_size(PLANE)
+    pair = lax.axis_size(CORE)
+    plane = lax.axis_index(LINE)
+    own = lax.axis_index(PLANE)
+    core = lax.axis_index(CORE)
     rows = micro * tile
     hidden = w_gate.shape[1]
     shard = w_query.shape[0]
@@ -1479,9 +1735,8 @@
         w_qkv,
         out_mat,
         gate_up,
-        down_mat,
         grads_in,
-        plane_two,
+        hidden_two,
         middle,
         hidden_one,
         queries,
@@ -1490,35 +1745,45 @@
         kv_home,
         cosine,
         sine,
-    ) = front(tokens, cotangent, marks, w_in, w_out, gate_up, w_down)
+    ) = front(tokens, cotangent, marks, w_in, w_out, gate_up)
     gains = jnp.pad(w_qkv[..., qkv : qkv + 2].reshape(width, 2).T, ((0, 6), (0, 0))).astype(F32)
     gate_up = gate_up.reshape(width, 2 * own_hidden)
-    down_mat = down_mat.reshape(own_hidden, width)
+    down_mat = lax.all_gather(w_down, (LINE, CORE), axis=0, tiled=True)
     plane_grads = grads_in.reshape(chips * rows, width)
-    plane_two = plane_two.reshape(chips * rows, width)
-
-    grad_pre, hidden_mlp, partial_out, grad_hidden_two = middle_call(
-        plane_two.reshape(chips, rows, width),
+
+    plane_two, grad_pre, hidden_mlp, partial_out, grad_hidden_two = middle_call(
+        hidden_two,
         grads_in.reshape(chips, rows, width),
         gate_up,
         down_mat,
         middle,
     )
-    layer_rows = scatter_sum(partial_out.reshape(chips, chips, tile, width), "seq", 1)
-    layer_rows = layer_rows.reshape(micro, tile, width)
-    grad_down = dot32(hidden_mlp, plane_grads, ((0,), (0,))).astype(BF16)
-    grad_gate_up = dot32(plane_two, grad_pre, ((0,), (0,))).astype(BF16)
-    grad_down = scatter_core(grad_down.reshape(planes, pair, -1, width), core, 1)
-    grad_gate_up = scatter_core(
-        grad_gate_up.reshape(planes, chips, pair, shard, 2 * own_hidden), core, 2
-    )
-    layer_rows, grad_down, grad_gate_up = lax.optimization_barrier(
-        (layer_rows, grad_down, grad_gate_up)
-    )
-    grad_down = scatter_sum(grad_down, "dp", 0).reshape(-1, width).astype(F32)
-    grad_gate_up = scatter_sum(grad_gate_up, "dp", 0).reshape(chips, shard, 2 * own_hidden)
-    grad_gate_up = swap_blocks(grad_gate_up, own).reshape(chips, shard, 2, planes, piece)
-    grad_gate_up = grad_gate_up.transpose(2, 1, 3, 0, 4).reshape(2, shard, hidden).astype(F32)
+    plane_two = plane_two.reshape(chips * rows, width)
+    partial_out = partial_out.reshape(chips, chips, tile, width)
+    grad_down, rows_low = weight_grad(
+        hidden_mlp,
+        plane_grads,
+        partial_out,
+        (planes, pair, piece // pair),
+        512,
+        0,
+        "down_grad",
+        6,
+    )
+    grad_down, grad_pre = lax.optimization_barrier((grad_down, grad_pre))
+    grad_gate_up, rows_high = weight_grad(
+        plane_two,
+        grad_pre,
+        partial_out,
+        (planes, chips, pair, shard),
+        256,
+        width // 2,
+        "gate_up_grad",
+        5,
+    )
+    layer_rows = jnp.concatenate([rows_low, rows_high], axis=-1)
+    grad_down = scatter_sum(grad_down, LINE, 0).reshape(-1, width).astype(F32)
+    grad_gate_up = scatter_sum(grad_gate_up, LINE, 0).reshape(chips, shard, 2 * own_hidden)
 
     grad_input, grad_q, grad_kv, grad_out = back(
         tile,
@@ -1528,15 +1793,16 @@
         x_rows,
         w_qkv,
         out_mat,
-        hidden_one.T,
+        hidden_one,
         queries,
-        attended.T,
+        attended,
         kv,
         cosine,
         sine,
         marks,
         gains,
     )
+    grad_gate, grad_up = trade(grad_gate_up, hidden)
     return (
         layer_rows,
         kv_home[..., :head_dim],
@@ -1546,8 +1812,8 @@
         grad_kv[:, :head_dim],
         grad_kv[:, head_dim : 2 * head_dim],
         grad_out,
-        grad_gate_up[0],
-        grad_gate_up[1],
+        grad_gate,
+        grad_up,
         grad_down,
         grad_kv[:, 2 * head_dim],
         grad_kv[:, 2 * head_dim + 1],
@@ -1555,40 +1821,40 @@
 
 
 def body(tokens, *rest):
-    if tokens.shape[0] == lax.axis_size("seq") == 4 and lax.axis_size("fsdp") == 2:
+    if tokens.shape[0] == lax.axis_size(PLANE) == 4 and lax.axis_size(CORE) == 2:
         return body_plane(tokens, *rest)
     return body_general(tokens, *rest)
 
 
 def solution(mesh):
     in_specs = (
-        P(None, ("dp", "seq", "fsdp"), None),
-        P(None, ("dp", "seq", "fsdp"), None),
-        P(None, ("dp", "seq", "fsdp")),
-        P(None, ("dp", "seq", "fsdp")),
-        P(("dp", "seq", "fsdp"), None),
-        P(("dp", "seq", "fsdp"), None),
-        P(("dp", "seq", "fsdp"), None),
-        P(("dp", "seq", "fsdp"), None),
-        P(("dp", "seq", "fsdp"), None),
-        P(("dp", "seq", "fsdp"), None),
-        P(("dp", "seq", "fsdp"), None),
-        P(("dp", "seq", "fsdp")),
-        P(("dp", "seq", "fsdp")),
+        P(None, EVERY, None),
+        P(None, EVERY, None),
+        P(None, EVERY),
+        P(None, EVERY),
+        P(EVERY, None),
+        P(EVERY, None),
+        P(EVERY, None),
+        P(EVERY, None),
+        P(EVERY, None),
+        P(EVERY, None),
+        P(EVERY, None),
+        P(EVERY),
+        P(EVERY),
     )
     out_specs = (
-        P(None, ("dp", "seq", "fsdp"), None),
-        P(None, ("dp", "seq", "fsdp"), None),
-        P(None, ("dp", "seq", "fsdp"), None),
-        P(None, ("dp", "seq", "fsdp"), None),
-        P(("dp", "seq", "fsdp"), None),
-        P(("dp", "seq", "fsdp"), None),
-        P(("dp", "seq", "fsdp"), None),
-        P(("dp", "seq", "fsdp"), None),
-        P(("dp", "seq", "fsdp"), None),
-        P(("dp", "seq", "fsdp"), None),
-        P(("dp", "seq", "fsdp"), None),
-        P(("dp", "seq", "fsdp")),
-        P(("dp", "seq", "fsdp")),
+        P(None, EVERY, None),
+        P(None, EVERY, None),
+        P(None, EVERY, None),
+        P(None, EVERY, None),
+        P(EVERY, None),
+        P(EVERY, None),
+        P(EVERY, None),
+        P(EVERY, None),
+        P(EVERY, None),
+        P(EVERY, None),
+        P(EVERY, None),
+        P(EVERY),
+        P(EVERY),
     )
     return jax.shard_map(body, mesh=mesh, in_specs=in_specs, out_specs=out_specs, check_vma=False)

time: 774 us -> 703 us (0.908)
  Pallas kernels: 573 us -> 655 us
  waiting for transfers between devices: 49.9 us -> 0.74 us
  matrix products: 45 us -> 0 us
  local copies, waits for them, and re-layouts: 56.2 us -> 16.1 us
  other arithmetic: 23.1 us -> 11.4 us
    pallas_call x0 -> x3, Pallas kernels: none -> 105 us  [the longest x2 85.4 us: weight_grad(): pl.pallas_call(functools.partial(weight_grad_kernel, (128, width, tile, c...]
    pallas_call x1, Pallas kernels: 294 us -> 223 us  [front(): pl.pallas_call(functools.partial(front_kernel, (tile, width, head_dim, gr...]
    pallas_call x1, Pallas kernels: 108 us -> 154 us  [middle_call(): pl.pallas_call(functools.partial(middle_kernel, (rows, width, hidden)), o...]
    dot_general x2 -> x0, matrix products: 45 us -> none  [dot32(): lax.dot_general(left, right, ((contract[0], contract[1]), ((), ())), pref...]
    reduce_scatter x2, waiting for transfers between devices: 21.4 us -> 0.01 us  [scatter_sum(): return lax.psum_scatter(value, axes, scatter_dimension=dim, tiled=True)]
    ppermute x5 -> x0, waiting for transfers between devices: 18.5 us -> none  [the longest x3 13.4 us: send_plane(): return lax.ppermute(value, 'seq', [(i, i ^ step) for i in range(4)])]
    convert_element_type x3 -> x1, other arithmetic: 15.8 us -> 2.46 us  [body_plane(): grad_down = scatter_sum(grad_down, LINE, 0).reshape(-1, width).astype(F32)]
    squeeze x5 -> x0, local copies, waits for them, and re-layouts: 11.7 us -> none  [the longest x3 6.25 us: block_of(): return lax.dynamic_index_in_dim(value, index, axis=dim, keepdims=False)]
  transfers between devices with their start and end apart: 8 -> 3, of which waited for: 4 -> 0; matrix products, arithmetic and copies ran while one was open for 11% -> 3% of each run, Pallas kernels for 22% -> 64%
where the time goes in v4:
time: 703 us; the launch traced here: 698 us
  Pallas kernels  655 us (93%)
  local copies, waits for them, and re-layouts  16.1 us (2%)
  between operations  14.5 us (2%)
  other arithmetic  11.4 us (2%)
    pallas_call x1, Pallas kernels, front(): pl.pallas_call(functools.partial(front_kernel, (tile, width, head_dim, gr...  223 us
    pallas_call x1, Pallas kernels, back(): pl.pallas_call(functools.partial(back_kernel, (tile, width, head_dim, gro...  174 us
    pallas_call x1, Pallas kernels, middle_call(): pl.pallas_call(functools.partial(middle_kernel, (rows, width, hidden)), o...  154 us
    pallas_call x2, Pallas kernels, weight_grad(): pl.pallas_call(functools.partial(weight_grad_kernel, (128, width, tile, c...  85.4 us
    pallas_call x1, Pallas kernels, trade(): pl.pallas_call(trade_kernel, out_shape=[jax.ShapeDtypeStruct((shard, hidd...  19.2 us
  transfers between devices with their start and end apart: 3, of which 0 were waited for; matrix products, arithmetic and copies ran while one was open for 3% of the time, Pallas kernels for 64%

profile of v4, /device:TPU:0, one launch (start us, length us, event | category | flops | bytes accessed | tf_op | source)
XLA Modules:
  0.0 698.3 jit_solution(8570240182935323235)
XLA Ops:
  7.2 0.0 all-gather.2.cloned.1.call-start
  7.2 0.7 all-gather.2.cloned.1.call-update
  7.9 0.0 reduce-scatter.5.cloned.1.call-start
  8.0 2.7 stack.33
  10.7 0.3 copy.37
  11.0 1.2 stack.34
  12.2 0.3 copy.38
  12.5 1.1 maximum_bitcast_fusion
  13.7 0.0 copy-start.13
  13.7 0.0 copy-start.14
  13.7 0.0 copy-start.11
  13.7 0.0 copy-start.12
  13.7 0.0 copy-start.6
  13.7 0.0 copy-start.9
  13.7 0.0 copy-start.10
  13.8 2.2 reshape.58.gu_in
  16.0 0.1 copy.36
  16.2 0.6 pad.12.marks
  16.8 0.6 maximum_bitcast_fusion.1.freq
  17.4 0.7 fusion.1.wq_in
  18.1 223.0 %front.1 = (bf16[4,128,2048]{2,1,0:T(8,128)(2,1)}, s32[2,4,8,128]{3,2,1,0:T(8,128)}, bf16[4,4,2,64,2432]{4,3,2,1,0:T(8,128)(2,1)}, bf16[4,4,2,64,2048]{4,3,2,1,0...) custom-call(bf16[4,128,2048]{2,1,0:T(8,128)(2,1)} %tok.1, ...), custom_call_target="tpu_custom_call" | custom-call | flops 20000000000 | bytes 100000000 | tf_op jit(solution)/shard_map/front/pallas_call | solution.py:737
  241.1 0.0 all-gather.2.cloned.1.call-done.down
  241.2 153.9 %feed_forward.1 = (bf16[4,512,2048]{2,1,0:T(8,128)(2,1)}, bf16[2048,2816]{1,0:T(8,128)(2,1)}, bf16[2048,1408]{1,0:T(8,128)(2,1)}, bf16[4,512,2048]{2,1,0:T(8,128)(2,1)}, bf16[512,2048]{1,0:T(8,128)(2,1)}) custom-call(bf16[512,2048]{1,0:T(8,128)(2,1)} %get-tuple-element.45.two_in, bf16[4,512,2048]{2,1,0:T(8,128)(2,1)} %bitcast.20, ...), custom_call_target="tpu_custom_call" | custom-call | flops 80000000000 | bytes 60000000 | tf_op jit(solution)/shard_map/feed_forward/pallas_call | solution.py:1436
  395.0 38.1 %down_grad.1 = (bf16[4,176,2048]{2,1,0:T(8,128)(2,1)}, bf16[4,128,1024]{2,1,0:T(8,128)(2,1)}) custom-call(bf16[2048,1408]{1,0:T(8,128)(2,1)} %get-tuple-element.49.left, bf16[2048,2048]{1,0:T(8,128)(2,1)} %bitcast.21, bf16[4,4,128,2048]{3,2,1,0:T(8,128)(2,1)} %bitcast.30), custom_call_target="tpu_custom_call" | custom-call | flops 11811160064 | bytes 40000000 | tf_op jit(solution)/shard_map/down_grad/pallas_call | solution.py:1663
  433.1 0.0 reduce-scatter.5.cloned.1.call-update
  433.1 0.0 reduce-scatter.3.cloned.1.call-start
  433.2 47.3 %gate_up_grad.1 = (bf16[4,4,64,2816]{3,2,1,0:T(8,128)(2,1)}, bf16[4,128,1024]{2,1,0:T(8,128)(2,1)}) custom-call(bf16[2048,2048]{1,0:T(8,128)(2,1)} %bitcast.29, bf16[2048,2816]{1,0:T(8,128)(2,1)} %get-tuple-element.55.right, bf16[4,4,128,2048]{3,2,1,0:T(8,128)(2,1)} %bitcast.31), custom_call_target="tpu_custom_call" | custom-call | flops 23622320128 | bytes 40000000 | tf_op jit(solution)/shard_map/gate_up_grad/pallas_call | solution.py:1663
  480.5 0.0 reduce-scatter.3.cloned.1.call-update
  480.5 1.1 slice.23
  481.6 0.2 copy.40
  481.9 0.6 pad_convert_fusion.gain_v
  482.5 0.0 copy-done.7
  482.5 0.7 fusion.2
  483.3 174.0 %back.1 = (bf16[4,128,2048]{2,1,0:T(8,128)(2,1)}, f32[64,2048]{1,0:T(8,128)}, f32[64,384]{1,0:T(8,128)}, f32[64,2048]{1,0:T(8,128)}) custom-call(bf16[512,2048]{1,0:T(8,128)(2,1)} %get-tuple-element.58.gh2, bf16[4,4,128,2048]{3,2,1,0:T(8,128)(2,1)} %get-tuple-element.46.grads_in, f32[512,2048]{1,0:T(8,128)} %get-tuple-element.48.residual.middle, ...), custom_call_target="tpu_custom_call" | custom-call | flops 1000000000 | bytes 1000000 | tf_op jit(solution)/shard_map/back/pallas_call | solution.py:1218
  657.2 0.0 copy-start.8
  657.2 0.0 copy-start.1
  657.3 0.0 copy-start.2
  657.3 4.3 convert_element_type.17
  661.5 0.7 slice_reduce_fusion
  662.2 0.6 fusion.3
  662.9 1.5 pad_maximum_fusion
  664.4 2.5 bitcast_convert_fusion
  666.9 1.4 copy-done
  668.2 19.2 %trade.1 = (f32[64,5632]{1,0:T(8,128)S(1)}, f32[64,5632]{1,0:T(8,128)S(1)}) custom-call(bf16[4,64,2816]{2,1,0:T(8,128)(2,1)S(1)} %bitcast.19), custom_call_target="tpu_custom_call" | custom-call | tf_op jit(solution)/shard_map/trade/pallas_call | solution.py:1505
  687.5 0.8 copy.45
  688.3 0.8 copy.46
  689.0 1.1 copy.47
  690.1 1.1 copy.48
  (23 shorter events, 0.1 us)
Async XLA Ops:
  7.2 3.8 copy-start.3
  7.2 234.0 %all-gather.2.cloned.1.call-start = ((), (), s32[]{:S(2)}) async-start(), calls=%async_computation.2 | async-start | bytes 6488064 | tf_op jit(solution)/shard_map/all_gather | solution.py:1751
  7.9 656.5 %reduce-scatter.5.cloned.1.call-start = ((), (), s32[]{:S(2)}) async-start(), calls=%async_computation.4 | async-start | bytes 3604480 | tf_op jit(solution)/shard_map/reduce_scatter | solution.py:399
  13.7 2.3 copy-start.13
  13.7 2.3 copy-start.14
  13.7 2.4 copy-start.11
  13.7 2.4 copy-start.12
  13.7 3.7 copy-start.6
  13.7 3.6 copy-start.9
  13.7 3.6 copy-start.10
  433.1 233.7 %reduce-scatter.3.cloned.1.call-start = ((), (), s32[]{:S(2)}) async-start(), calls=%async_computation.3 | async-start | bytes 7208960 | tf_op jit(solution)/shard_map/reduce_scatter | solution.py:399
  480.5 2.0 copy-start.7
  657.2 4.3 copy-start.8
  657.2 5.6 copy-start.1
  657.3 5.6 copy-start.2
  664.4 23.1 %copy-start.5 = (f32[64,2048]{1,0:T(8,128)S(1)}, f32[64,2048]{1,0:T(8,128)}, u32[]{:S(2)}) copy-start(f32[64,2048]{1,0:T(8,128)} %get-tuple-element.100) | copy-start | bytes 1572868
  664.4 23.9 %copy-start.4 = (f32[64,2048]{1,0:T(8,128)S(1)}, f32[64,2048]{1,0:T(8,128)}, u32[]{:S(2)}) copy-start(f32[64,2048]{1,0:T(8,128)} %get-tuple-element.103) | copy-start | bytes 1572868
  666.9 1.4 copy-start
Sparse Core Ops, SparseCore 0:
  9.7 85.5 all-gather.1
  433.2 59.0 reduce-scatter.4
  494.6 137.4 reduce-scatter.2

commit v5 on v4

--- a/solution.py
+++ b/solution.py
@@ -1025,6 +1025,10 @@
                     part = turn(grad_q[i * tile : (i + 1) * tile], cosine, -sine)
                     lin_v[at, pl.ds(h * head_dim, head_dim)] = part.astype(BF16)
 
+        @pl.when(g >= 3)
+        def _():
+            do_c(g - 3)
+
         @pl.when(g >= 1)
         def _():
             do_b(g - 1)
@@ -1052,20 +1056,13 @@
 
         lax.fori_loop(0, planes, inputs, 0)
 
-        @pl.when(g >= 2)
-        def _():
-            do_c(g - 2)
-
-        @pl.when(g >= 3)
-        def _():
-            do_d(g - 3)
-
         return carry
 
     lax.fori_loop(0, groups, one_group, 0)
 
     to_other = p.copy(kvacc.at[:, 1 - c], kvx, "kx", 0, p.to_core)
     to_other.start()
+    do_c(groups - 3)
     do_b(groups - 1)
     to_other.wait_recv()
     for b in range(chips):
@@ -1110,6 +1107,7 @@
         p.copy(proj_v.at[pl.ds(pl.multiple_of(o * tile, tile), tile)], home.at[s], "home", i, t)
         for i, (t, o) in enumerate(others)
     ]
+    do_d(groups - 4)
     do_c(groups - 2)
     a_kv.wait_recv()
 

time: 703 us -> 696 us (0.990)
    pallas_call x1, Pallas kernels: 174 us -> 166 us  [back(): pl.pallas_call(functools.partial(back_kernel, (tile, width, head_dim, gro...]
  transfers between devices with their start and end apart: 3 -> 3, of which waited for: 0 -> 0; matrix products, arithmetic and copies ran while one was open for 3% -> 3% of each run, Pallas kernels for 64% -> 63%
where the time goes in v5:
time: 696 us; the launch traced here: 691 us
  Pallas kernels  648 us (93%)
  local copies, waits for them, and re-layouts  16.1 us (2%)
  between operations  14.5 us (2%)
  other arithmetic  11.4 us (2%)
    pallas_call x1, Pallas kernels, front(): pl.pallas_call(functools.partial(front_kernel, (tile, width, head_dim, gr...  223 us
    pallas_call x1, Pallas kernels, back(): pl.pallas_call(functools.partial(back_kernel, (tile, width, head_dim, gro...  166 us
    pallas_call x1, Pallas kernels, middle_call(): pl.pallas_call(functools.partial(middle_kernel, (rows, width, hidden)), o...  154 us
    pallas_call x2, Pallas kernels, weight_grad(): pl.pallas_call(functools.partial(weight_grad_kernel, (128, width, tile, c...  85.4 us
    pallas_call x1, Pallas kernels, trade(): pl.pallas_call(trade_kernel, out_shape=[jax.ShapeDtypeStruct((shard, hidd...  19.7 us
  transfers between devices with their start and end apart: 3, of which 0 were waited for; matrix products, arithmetic and copies ran while one was open for 3% of the time, Pallas kernels for 63%

profile of v5, /device:TPU:0, one launch (start us, length us, event | category | flops | bytes accessed | tf_op | source)
XLA Modules:
  0.0 691.2 jit_solution(10076318276234702656)
XLA Ops:
  7.2 0.0 copy-start.3
  7.2 0.0 all-gather.2.cloned.1.call-start
  7.2 0.7 all-gather.2.cloned.1.call-update
  7.9 0.0 reduce-scatter.5.cloned.1.call-start
  8.0 2.7 stack.33
  10.7 0.3 copy.37
  11.0 0.0 copy-done.3
  11.0 1.2 stack.34
  12.2 0.3 copy.38
  12.5 1.1 maximum_bitcast_fusion
  13.7 0.0 copy-start.13
  13.7 0.0 copy-start.14
  13.7 0.0 copy-start.11
  13.7 0.0 copy-start.12
  13.7 0.0 copy-start.6
  13.7 0.0 copy-start.9
  13.7 0.0 copy-start.10
  13.8 2.2 reshape.58.gu_in
  16.0 0.0 copy-done.13
  16.0 0.1 copy.36
  16.1 0.0 copy-done.11
  16.2 0.6 pad.12.marks
  16.8 0.6 maximum_bitcast_fusion.1.freq
  17.4 0.7 fusion.1.wq_in
  18.1 223.0 %front.1 = (bf16[4,128,2048]{2,1,0:T(8,128)(2,1)}, s32[2,4,8,128]{3,2,1,0:T(8,128)}, bf16[4,4,2,64,2432]{4,3,2,1,0:T(8,128)(2,1)}, bf16[4,4,2,64,2048]{4,3,2,1,0...) custom-call(bf16[4,128,2048]{2,1,0:T(8,128)(2,1)} %tok.1, ...), custom_call_target="tpu_custom_call" | custom-call | flops 20000000000 | bytes 100000000 | tf_op jit(solution)/shard_map/front/pallas_call | solution.py:737
  241.1 0.0 all-gather.2.cloned.1.call-done.down
  241.2 153.9 %feed_forward.1 = (bf16[4,512,2048]{2,1,0:T(8,128)(2,1)}, bf16[2048,2816]{1,0:T(8,128)(2,1)}, bf16[2048,1408]{1,0:T(8,128)(2,1)}, bf16[4,512,2048]{2,1,0:T(8,128)(2,1)}, bf16[512,2048]{1,0:T(8,128)(2,1)}) custom-call(bf16[512,2048]{1,0:T(8,128)(2,1)} %get-tuple-element.45.two_in, bf16[4,512,2048]{2,1,0:T(8,128)(2,1)} %bitcast.20, ...), custom_call_target="tpu_custom_call" | custom-call | flops 80000000000 | bytes 60000000 | tf_op jit(solution)/shard_map/feed_forward/pallas_call | solution.py:1434
  395.0 38.1 %down_grad.1 = (bf16[4,176,2048]{2,1,0:T(8,128)(2,1)}, bf16[4,128,1024]{2,1,0:T(8,128)(2,1)}) custom-call(bf16[2048,1408]{1,0:T(8,128)(2,1)} %get-tuple-element.49.left, bf16[2048,2048]{1,0:T(8,128)(2,1)} %bitcast.21, bf16[4,4,128,2048]{3,2,1,0:T(8,128)(2,1)} %bitcast.30), custom_call_target="tpu_custom_call" | custom-call | flops 11811160064 | bytes 40000000 | tf_op jit(solution)/shard_map/down_grad/pallas_call | solution.py:1661
  433.1 0.0 reduce-scatter.5.cloned.1.call-update
  433.1 0.0 reduce-scatter.3.cloned.1.call-start
  433.2 47.3 %gate_up_grad.1 = (bf16[4,4,64,2816]{3,2,1,0:T(8,128)(2,1)}, bf16[4,128,1024]{2,1,0:T(8,128)(2,1)}) custom-call(bf16[2048,2048]{1,0:T(8,128)(2,1)} %bitcast.29, bf16[2048,2816]{1,0:T(8,128)(2,1)} %get-tuple-element.55.right, bf16[4,4,128,2048]{3,2,1,0:T(8,128)(2,1)} %bitcast.31), custom_call_target="tpu_custom_call" | custom-call | flops 23622320128 | bytes 40000000 | tf_op jit(solution)/shard_map/gate_up_grad/pallas_call | solution.py:1661
  480.5 0.0 reduce-scatter.3.cloned.1.call-update
  480.5 1.1 slice.23
  481.6 0.2 copy.40
  481.9 0.6 pad_convert_fusion.gain_v
  482.5 0.7 fusion.2
  483.3 166.3 %back.1 = (bf16[4,128,2048]{2,1,0:T(8,128)(2,1)}, f32[64,2048]{1,0:T(8,128)}, f32[64,384]{1,0:T(8,128)}, f32[64,2048]{1,0:T(8,128)}) custom-call(bf16[512,2048]{1,0:T(8,128)(2,1)} %get-tuple-element.58.gh2, bf16[4,4,128,2048]{3,2,1,0:T(8,128)(2,1)} %get-tuple-element.46.grads_in, f32[512,2048]{1,0:T(8,128)} %get-tuple-element.48.residual.middle, ...), custom_call_target="tpu_custom_call" | custom-call | flops 1000000000 | bytes 1000000 | tf_op jit(solution)/shard_map/back/pallas_call | solution.py:1216
  649.6 4.3 convert_element_type.17
  653.9 0.7 slice_reduce_fusion
  654.6 0.6 fusion.3
  655.3 1.5 pad_maximum_fusion
  656.8 2.5 bitcast_convert_fusion
  659.2 1.4 copy-done
  660.6 19.7 %trade.1 = (f32[64,5632]{1,0:T(8,128)S(1)}, f32[64,5632]{1,0:T(8,128)S(1)}) custom-call(bf16[4,64,2816]{2,1,0:T(8,128)(2,1)S(1)} %bitcast.19), custom_call_target="tpu_custom_call" | custom-call | tf_op jit(solution)/shard_map/trade/pallas_call | solution.py:1503
  680.3 0.8 copy.45
  681.1 0.8 copy.46
  681.9 1.1 copy.47
  683.0 1.1 copy.48
  (23 shorter events, 0.1 us)
Async XLA Ops:
  7.2 3.8 copy-start.3
  7.2 234.0 %all-gather.2.cloned.1.call-start = ((), (), s32[]{:S(2)}) async-start(), calls=%async_computation.2 | async-start | bytes 6488064 | tf_op jit(solution)/shard_map/all_gather | solution.py:1749
  7.9 648.9 %reduce-scatter.5.cloned.1.call-start = ((), (), s32[]{:S(2)}) async-start(), calls=%async_computation.4 | async-start | bytes 3604480 | tf_op jit(solution)/shard_map/reduce_scatter | solution.py:399
  13.7 2.3 copy-start.13
  13.7 2.3 copy-start.14
  13.7 2.4 copy-start.11
  13.7 2.4 copy-start.12
  13.7 3.7 copy-start.6
  13.7 3.6 copy-start.9
  13.7 3.6 copy-start.10
  433.1 226.1 %reduce-scatter.3.cloned.1.call-start = ((), (), s32[]{:S(2)}) async-start(), calls=%async_computation.3 | async-start | bytes 7208960 | tf_op jit(solution)/shard_map/reduce_scatter | solution.py:399
  480.5 2.0 copy-start.7
  649.6 4.3 copy-start.8
  649.6 5.6 copy-start.1
  649.6 5.6 copy-start.2
  656.8 23.6 %copy-start.5 = (f32[64,2048]{1,0:T(8,128)S(1)}, f32[64,2048]{1,0:T(8,128)}, u32[]{:S(2)}) copy-start(f32[64,2048]{1,0:T(8,128)} %get-tuple-element.100) | copy-start | bytes 1572868
  656.8 24.4 %copy-start.4 = (f32[64,2048]{1,0:T(8,128)S(1)}, f32[64,2048]{1,0:T(8,128)}, u32[]{:S(2)}) copy-start(f32[64,2048]{1,0:T(8,128)} %get-tuple-element.103) | copy-start | bytes 1572868
  659.2 1.4 copy-start
Sparse Core Ops, SparseCore 0:
  9.7 85.5 all-gather.1
  433.2 59.0 reduce-scatter.4
  494.6 137.4 reduce-scatter.2
